TPU v7x, 128 devices: a whole 4x4x4 slice. The times are simulated.
128 devices in a mesh: ctx: 16 (over y, z_hi, core), ch: 2 (over z_lo), dp: 4 (over x).
Axes of the slice: x: 4, y: 4, z: 4 (z_hi: 2, z_lo: 2; z = z_hi * 2 + z_lo), core: 2. Of those that a mesh axis runs over, the one named last changes fastest.
Arguments:
- features: bfloat16 [32768, 3, 4096], P(('dp', 'ctx'), None, 'ch'), parts along dimension 0, may hold values from -6 to 6
- short_filter: float32 [3, 3, 4096], P(None, None, 'ch'), may hold values from -3.5 to 3.5
- mode_residue: float32 [16, 4096], P(None, 'ch'), may hold values from -0.18 to 0.18
- decay_mix: float32 [16, 4096], P(None, 'ch'), may hold values from 0 to 1
- skip_gain: float32 [4096], P('ch'), may hold values from 0.5 to 1.5
- counter: int32 [8], P('dp'), parts along dimension 0, may hold values from 0 to 1048575
- out_weight: bfloat16 [4096, 4096], P('ch'), may hold values from -0.09375 to 0.09375
Outputs:
- projected: bfloat16 [32768, 4096], P(('dp', 'ctx', 'ch')), parts along dimension 0
There are 4 independent parts, one for each index of `dp`. A program takes and returns all parts, laid end to end along the dimension named above; an argument that names none is the same for every part. Nothing has to cross between parts.
All inputs are finite; a program needn't handle non-finite values.
Results may differ from a plain program's by a relative error of at most 0.012.
Values may be sent and summed in bfloat16 or wider, within the bound.
No kernel may reach another device: no remote copies, remote signals or barrier semaphores. Data moves between devices by JAX's collectives and lax.ppermute only.
A program may use at most 256 MiB of HBM per device.

v0:
```python
import math

import jax
import jax.numpy as jnp
from jax import lax
from jax.sharding import PartitionSpec as P

SHORT = 3


keep_scale = 8.0 / 7.0
precise = lax.Precision.HIGHEST


def passed_along(value, axis, steps):
    count = lax.axis_size(axis)
    leading, last = (max(0, -steps), min(count, count - steps))
    return lax.ppermute(value, axis, [(source, source + steps) for source in range(leading, last)])


def keep_mask(hash_base, positions, channels):
    bits = (
        hash_base
        + positions[:, None] * jnp.int32(-1640531535)
        + channels[None, :] * jnp.int32(-2048144777)
    )
    bits = bits ^ lax.shift_right_logical(bits, jnp.full_like(bits, 16))
    bits = bits * jnp.int32(2146121005)
    bits = bits ^ lax.shift_right_logical(bits, jnp.full_like(bits, 15))
    bits = bits * jnp.int32(-2073254261)
    bits = bits ^ lax.shift_right_logical(bits, jnp.full_like(bits, 16))
    return lax.shift_right_logical(bits, jnp.full_like(bits, 29)) != 0


def rates_of(mix, length):
    return jnp.exp(-((1.0 - mix) * math.log(length) + mix * math.log(30.0)))


def contract(form, left, right):
    return jnp.einsum(form, left, right, precision=precise)


def trig_table(rows, cols, period):
    product = (
        jnp.arange(rows, dtype=jnp.int32)[:, None]
        * jnp.arange(cols, dtype=jnp.int32)[None, :]
        % period
    )
    angle = product.astype(jnp.float32) * (2.0 * math.pi / period)
    return (jnp.cos(angle), jnp.sin(angle))


def split_table(table):
    upper = table.astype(jnp.bfloat16)
    lower = (table - upper.astype(jnp.float32)).astype(jnp.bfloat16)
    return (upper, lower)


def narrow_section(table, grid):
    upper, lower = split_table(table)
    first = jnp.einsum("ka,abc->kbc", upper, grid, preferred_element_type=jnp.float32)
    return first + jnp.einsum("ka,abc->kbc", lower, grid, preferred_element_type=jnp.float32)


def forward_dft(grid, tables):
    cos_outer, sin_outer, twist_cos, twist_sin, cos_inner, sin_inner = tables
    first_real = narrow_section(cos_outer, grid)
    first_imag = -narrow_section(sin_outer, grid)
    turned_real = first_real * twist_cos[:, :, None] + first_imag * twist_sin[:, :, None]
    turned_imag = first_imag * twist_cos[:, :, None] - first_real * twist_sin[:, :, None]
    out_real = contract("kbc,bm->kmc", turned_real, cos_inner) + contract(
        "kbc,bm->kmc", turned_imag, sin_inner
    )
    out_imag = contract("kbc,bm->kmc", turned_imag, cos_inner) - contract(
        "kbc,bm->kmc", turned_real, sin_inner
    )
    return (out_real, out_imag)


def inverse_dft(spec_real, spec_imag, tables):
    cos_outer, sin_outer, twist_cos, twist_sin, cos_inner, sin_inner = tables
    back_real = contract("kmc,bm->kbc", spec_real, cos_inner) - contract(
        "kmc,bm->kbc", spec_imag, sin_inner
    )
    back_imag = contract("kmc,bm->kbc", spec_imag, cos_inner) + contract(
        "kmc,bm->kbc", spec_real, sin_inner
    )
    turned_real = back_real * twist_cos[:, :, None] - back_imag * twist_sin[:, :, None]
    turned_imag = back_imag * twist_cos[:, :, None] + back_real * twist_sin[:, :, None]
    return contract("ka,kbc->abc", cos_outer, turned_real) - contract(
        "ka,kbc->abc", sin_outer, turned_imag
    )


def filter_spectrum(residue, mix, length, outer_len, inner_len):
    total_len = 2 * length
    rates = rates_of(mix, length)
    freq = (
        jnp.arange(outer_len, dtype=jnp.int32)[:, None]
        + outer_len * jnp.arange(inner_len, dtype=jnp.int32)[None, :]
    )
    angle = freq.astype(jnp.float32) * (2.0 * math.pi / total_len)
    sine_full = jnp.sin(angle)[:, :, None]
    sine_half = jnp.sin(0.5 * angle)[:, :, None]
    parity = (1 - 2 * (freq % 2)).astype(jnp.float32)[:, :, None]
    width = residue.shape[1]

    def add_mode(order_index, totals):
        rate = rates[order_index][None, None, :]
        factor = jnp.exp(-rate)
        numer = 1.0 - parity * jnp.exp(-rate * length)
        denom_real = -jnp.expm1(-rate) + factor * 2.0 * sine_half * sine_half
        denom_imag = factor * sine_full
        scale = (
            residue[order_index][None, None, :]
            * numer
            / (denom_real * denom_real + denom_imag * denom_imag)
        )
        return (totals[0] + scale * denom_real, totals[1] - scale * denom_imag)

    empty = jnp.zeros((outer_len, inner_len, width), jnp.float32)
    return lax.fori_loop(0, residue.shape[0], add_mode, (empty, empty))


def causal_fft(signal, residue, mix):
    length, width = signal.shape
    total_len = 2 * length
    inner_len = 128
    outer_len = total_len // inner_len
    half_outer = outer_len // 2
    cos_outer, sin_outer = trig_table(outer_len, half_outer, outer_len)
    twist_cos, twist_sin = trig_table(outer_len, inner_len, total_len)
    cos_inner, sin_inner = trig_table(inner_len, inner_len, inner_len)
    tables = (cos_outer, sin_outer, twist_cos, twist_sin, cos_inner, sin_inner)
    sig_real, sig_imag = forward_dft(signal.reshape(half_outer, inner_len, width), tables)
    tap_real, tap_imag = filter_spectrum(residue, mix, length, outer_len, inner_len)
    prod_real = sig_real * tap_real - sig_imag * tap_imag
    prod_imag = sig_real * tap_imag + sig_imag * tap_real
    return inverse_dft(prod_real, prod_imag, tables).reshape(length, width) / total_len


def body(features, short_filter, mode_residue, decay_mix, skip_gain, counter, out_weight):
    tok_rows = features.shape[0]
    local_width = features.shape[2]
    ctx_count = lax.axis_size("ctx")
    ctx_index = lax.axis_index("ctx")
    ch_index = lax.axis_index("ch")
    edge = passed_along(features[tok_rows - (SHORT - 1) :], "ctx", 1)
    joined = jnp.concatenate([edge, features], axis=0).astype(jnp.float32)
    filtered = jnp.zeros((tok_rows, 3, local_width), jnp.float32)
    for lag in range(SHORT):
        filtered = (
            filtered
            + short_filter[:, lag, :][None] * joined[SHORT - 1 - lag : SHORT - 1 - lag + tok_rows]
        )
    query = filtered[:, 0]
    keyed = filtered[:, 1]
    valued = filtered[:, 2]
    positions = counter[1] + ctx_index * tok_rows + jnp.arange(tok_rows, dtype=jnp.int32)
    channels = ch_index * local_width + jnp.arange(local_width, dtype=jnp.int32)
    gated = jnp.where(
        keep_mask(counter[0], positions, channels), keyed * valued * keep_scale, 0.0
    ).astype(jnp.bfloat16)
    gated_wide = gated.astype(jnp.float32)
    col_width = local_width // ctx_count
    columns = lax.all_to_all(gated, "ctx", split_axis=1, concat_axis=0, tiled=True)
    residue_part = lax.dynamic_slice_in_dim(mode_residue, ctx_index * col_width, col_width, 1)
    mix_part = lax.dynamic_slice_in_dim(decay_mix, ctx_index * col_width, col_width, 1)
    convolved = causal_fft(columns, residue_part, mix_part)
    conv_out = lax.all_to_all(convolved, "ctx", split_axis=0, concat_axis=1, tiled=True)
    long_out = conv_out + skip_gain[None, :] * gated_wide
    mixed = (query * long_out).astype(jnp.bfloat16)
    return lax.psum_scatter(
        jnp.dot(mixed, out_weight, preferred_element_type=jnp.float32).astype(jnp.bfloat16),
        "ch",
        scatter_dimension=0,
        tiled=True,
    )


def solution(mesh):
    placed = (
        P(("dp", "ctx"), None, "ch"),
        P(None, None, "ch"),
        P(None, "ch"),
        P(None, "ch"),
        P("ch"),
        P("dp"),
        P("ch", None),
    )
    return jax.shard_map(
        body, mesh=mesh, in_specs=placed, out_specs=P(("dp", "ctx", "ch"), None), check_vma=False
    )
```

profile of v0, /device:TPU:0, one launch (start us, length us, event | category | flops | bytes accessed | tf_op | source)
XLA Modules:
  0.0 654.8 jit_solution(195904797394615386)
XLA Ops:
  22.9 11.6 %maximum_convert_fusion = f32[514,3,2048]{0,2,1:T(8,128)} fusion(bf16[512,3,2048]{0,2,1:T(8,128)(2,1)} %copy.65, bf16[2,3,2048]{0,2,1:T(8,128)(2,1)S(1)} %copy.64), kind=kLoop, calls=%fused_computation.62 | loop fusion | flops 12632064 | bytes 18948096 | tf_op jit(solution)/shard_map/convert_element_type | solution.py:149
  34.5 17.3 %fusion.17 = f32[512,3,2048]{0,2,1:T(8,128)S(1)} fusion(f32[514,3,2048]{0,2,1:T(8,128)} %maximum_convert_fusion, f32[3,2048]{1,0:T(4,128)S(1)} %get-tuple-element.271, f32[3,2048]{1,0:T(4,128)S(1)} %get-tuple-element.272, f32[3,2048]{1,0:T(4,128)S(1)} %bitcast.149), kind=kLoop, calls=%fused_computation.31 | loop fusion | flops 15728640 | bytes 50405376 | tf_op jit(solution)/shard_map/add | solution.py:153
  69.5 199.9 %while.19 = (s32[]{:T(128)}, f32[128,128,128]{2,1,0:T(8,128)}, f32[128,128,128]{2,1,0:T(8,128)}, f32[16,128]{1,0:T(8,128)S(1)}, f32[16,128]{1,0:T(8,128)S(1)}, /*index=5*/s32[128]{0:T(128)S(1)}, s32[]{:T(128)}, s32[]{:T(128)}) while((s32[]{:T(128)}, f32[128,128,128]{2,1,0:T(8,128)}, ...), condition=%wide.region_1.2_spmd.clone.clone.clone.clone, body=%wide.region_0.1_spmd.clone.clone.clone.clone.sunk | while | flops 35963392 | bytes 33956460 | solution.py:122
  70.1 9.4 %fusion.188 = (f32[128,128,128]{2,1,0:T(8,128)}, f32[128,128,128]{2,1,0:T(8,128)}) fusion(f32[128,128,128]{2,1,0:T(8,128)} %get-tuple-element.340, f32[128,128]{1,0:T(8,128)S(1)} %get-tuple-element.321, f32[128]{0:T(128)S(1)} %get-tuple-element.323, f32[128,128]{1,0:T(8,128)S(1)} %get-tuple-element.324, f32[128]{0:T(128)S(1)} %broadcast_multiply_fusion.2, ...), kind=kLoop, calls=%fused_computation.7.clone.1 | loop fusion | flops 35651584 | bytes 33753600 | tf_op jit(solution)/shard_map/while/body/eval_jaxpr/sub | solution.py:119
  80.1 12.1 %fusion.188 = (f32[128,128,128]{2,1,0:T(8,128)}, f32[128,128,128]{2,1,0:T(8,128)}) fusion(f32[128,128,128]{2,1,0:T(8,128)} %get-tuple-element.340, f32[128,128]{1,0:T(8,128)S(1)} %get-tuple-element.321, f32[128]{0:T(128)S(1)} %get-tuple-element.323, f32[128,128]{1,0:T(8,128)S(1)} %get-tuple-element.324, f32[128]{0:T(128)S(1)} %broadcast_multiply_fusion.2, ...), kind=kLoop, calls=%fused_computation.7.clone.1 | loop fusion | flops 35651584 | bytes 33753600 | tf_op jit(solution)/shard_map/while/body/eval_jaxpr/sub | solution.py:119
  92.7 12.1 %fusion.188 = (f32[128,128,128]{2,1,0:T(8,128)}, f32[128,128,128]{2,1,0:T(8,128)}) fusion(f32[128,128,128]{2,1,0:T(8,128)} %get-tuple-element.340, f32[128,128]{1,0:T(8,128)S(1)} %get-tuple-element.321, f32[128]{0:T(128)S(1)} %get-tuple-element.323, f32[128,128]{1,0:T(8,128)S(1)} %get-tuple-element.324, f32[128]{0:T(128)S(1)} %broadcast_multiply_fusion.2, ...), kind=kLoop, calls=%fused_computation.7.clone.1 | loop fusion | flops 35651584 | bytes 33753600 | tf_op jit(solution)/shard_map/while/body/eval_jaxpr/sub | solution.py:119
  105.4 12.1 %fusion.188 = (f32[128,128,128]{2,1,0:T(8,128)}, f32[128,128,128]{2,1,0:T(8,128)}) fusion(f32[128,128,128]{2,1,0:T(8,128)} %get-tuple-element.340, f32[128,128]{1,0:T(8,128)S(1)} %get-tuple-element.321, f32[128]{0:T(128)S(1)} %get-tuple-element.323, f32[128,128]{1,0:T(8,128)S(1)} %get-tuple-element.324, f32[128]{0:T(128)S(1)} %broadcast_multiply_fusion.2, ...), kind=kLoop, calls=%fused_computation.7.clone.1 | loop fusion | flops 35651584 | bytes 33753600 | tf_op jit(solution)/shard_map/while/body/eval_jaxpr/sub | solution.py:119
  118.0 12.1 %fusion.188 = (f32[128,128,128]{2,1,0:T(8,128)}, f32[128,128,128]{2,1,0:T(8,128)}) fusion(f32[128,128,128]{2,1,0:T(8,128)} %get-tuple-element.340, f32[128,128]{1,0:T(8,128)S(1)} %get-tuple-element.321, f32[128]{0:T(128)S(1)} %get-tuple-element.323, f32[128,128]{1,0:T(8,128)S(1)} %get-tuple-element.324, f32[128]{0:T(128)S(1)} %broadcast_multiply_fusion.2, ...), kind=kLoop, calls=%fused_computation.7.clone.1 | loop fusion | flops 35651584 | bytes 33753600 | tf_op jit(solution)/shard_map/while/body/eval_jaxpr/sub | solution.py:119
  130.7 12.1 %fusion.188 = (f32[128,128,128]{2,1,0:T(8,128)}, f32[128,128,128]{2,1,0:T(8,128)}) fusion(f32[128,128,128]{2,1,0:T(8,128)} %get-tuple-element.340, f32[128,128]{1,0:T(8,128)S(1)} %get-tuple-element.321, f32[128]{0:T(128)S(1)} %get-tuple-element.323, f32[128,128]{1,0:T(8,128)S(1)} %get-tuple-element.324, f32[128]{0:T(128)S(1)} %broadcast_multiply_fusion.2, ...), kind=kLoop, calls=%fused_computation.7.clone.1 | loop fusion | flops 35651584 | bytes 33753600 | tf_op jit(solution)/shard_map/while/body/eval_jaxpr/sub | solution.py:119
  143.4 12.1 %fusion.188 = (f32[128,128,128]{2,1,0:T(8,128)}, f32[128,128,128]{2,1,0:T(8,128)}) fusion(f32[128,128,128]{2,1,0:T(8,128)} %get-tuple-element.340, f32[128,128]{1,0:T(8,128)S(1)} %get-tuple-element.321, f32[128]{0:T(128)S(1)} %get-tuple-element.323, f32[128,128]{1,0:T(8,128)S(1)} %get-tuple-element.324, f32[128]{0:T(128)S(1)} %broadcast_multiply_fusion.2, ...), kind=kLoop, calls=%fused_computation.7.clone.1 | loop fusion | flops 35651584 | bytes 33753600 | tf_op jit(solution)/shard_map/while/body/eval_jaxpr/sub | solution.py:119
  156.0 12.1 %fusion.188 = (f32[128,128,128]{2,1,0:T(8,128)}, f32[128,128,128]{2,1,0:T(8,128)}) fusion(f32[128,128,128]{2,1,0:T(8,128)} %get-tuple-element.340, f32[128,128]{1,0:T(8,128)S(1)} %get-tuple-element.321, f32[128]{0:T(128)S(1)} %get-tuple-element.323, f32[128,128]{1,0:T(8,128)S(1)} %get-tuple-element.324, f32[128]{0:T(128)S(1)} %broadcast_multiply_fusion.2, ...), kind=kLoop, calls=%fused_computation.7.clone.1 | loop fusion | flops 35651584 | bytes 33753600 | tf_op jit(solution)/shard_map/while/body/eval_jaxpr/sub | solution.py:119
  168.7 12.1 %fusion.188 = (f32[128,128,128]{2,1,0:T(8,128)}, f32[128,128,128]{2,1,0:T(8,128)}) fusion(f32[128,128,128]{2,1,0:T(8,128)} %get-tuple-element.340, f32[128,128]{1,0:T(8,128)S(1)} %get-tuple-element.321, f32[128]{0:T(128)S(1)} %get-tuple-element.323, f32[128,128]{1,0:T(8,128)S(1)} %get-tuple-element.324, f32[128]{0:T(128)S(1)} %broadcast_multiply_fusion.2, ...), kind=kLoop, calls=%fused_computation.7.clone.1 | loop fusion | flops 35651584 | bytes 33753600 | tf_op jit(solution)/shard_map/while/body/eval_jaxpr/sub | solution.py:119
  181.4 12.1 %fusion.188 = (f32[128,128,128]{2,1,0:T(8,128)}, f32[128,128,128]{2,1,0:T(8,128)}) fusion(f32[128,128,128]{2,1,0:T(8,128)} %get-tuple-element.340, f32[128,128]{1,0:T(8,128)S(1)} %get-tuple-element.321, f32[128]{0:T(128)S(1)} %get-tuple-element.323, f32[128,128]{1,0:T(8,128)S(1)} %get-tuple-element.324, f32[128]{0:T(128)S(1)} %broadcast_multiply_fusion.2, ...), kind=kLoop, calls=%fused_computation.7.clone.1 | loop fusion | flops 35651584 | bytes 33753600 | tf_op jit(solution)/shard_map/while/body/eval_jaxpr/sub | solution.py:119
  194.0 12.1 %fusion.188 = (f32[128,128,128]{2,1,0:T(8,128)}, f32[128,128,128]{2,1,0:T(8,128)}) fusion(f32[128,128,128]{2,1,0:T(8,128)} %get-tuple-element.340, f32[128,128]{1,0:T(8,128)S(1)} %get-tuple-element.321, f32[128]{0:T(128)S(1)} %get-tuple-element.323, f32[128,128]{1,0:T(8,128)S(1)} %get-tuple-element.324, f32[128]{0:T(128)S(1)} %broadcast_multiply_fusion.2, ...), kind=kLoop, calls=%fused_computation.7.clone.1 | loop fusion | flops 35651584 | bytes 33753600 | tf_op jit(solution)/shard_map/while/body/eval_jaxpr/sub | solution.py:119
  206.7 12.1 %fusion.188 = (f32[128,128,128]{2,1,0:T(8,128)}, f32[128,128,128]{2,1,0:T(8,128)}) fusion(f32[128,128,128]{2,1,0:T(8,128)} %get-tuple-element.340, f32[128,128]{1,0:T(8,128)S(1)} %get-tuple-element.321, f32[128]{0:T(128)S(1)} %get-tuple-element.323, f32[128,128]{1,0:T(8,128)S(1)} %get-tuple-element.324, f32[128]{0:T(128)S(1)} %broadcast_multiply_fusion.2, ...), kind=kLoop, calls=%fused_computation.7.clone.1 | loop fusion | flops 35651584 | bytes 33753600 | tf_op jit(solution)/shard_map/while/body/eval_jaxpr/sub | solution.py:119
  219.4 12.1 %fusion.188 = (f32[128,128,128]{2,1,0:T(8,128)}, f32[128,128,128]{2,1,0:T(8,128)}) fusion(f32[128,128,128]{2,1,0:T(8,128)} %get-tuple-element.340, f32[128,128]{1,0:T(8,128)S(1)} %get-tuple-element.321, f32[128]{0:T(128)S(1)} %get-tuple-element.323, f32[128,128]{1,0:T(8,128)S(1)} %get-tuple-element.324, f32[128]{0:T(128)S(1)} %broadcast_multiply_fusion.2, ...), kind=kLoop, calls=%fused_computation.7.clone.1 | loop fusion | flops 35651584 | bytes 33753600 | tf_op jit(solution)/shard_map/while/body/eval_jaxpr/sub | solution.py:119
  232.0 12.1 %fusion.188 = (f32[128,128,128]{2,1,0:T(8,128)}, f32[128,128,128]{2,1,0:T(8,128)}) fusion(f32[128,128,128]{2,1,0:T(8,128)} %get-tuple-element.340, f32[128,128]{1,0:T(8,128)S(1)} %get-tuple-element.321, f32[128]{0:T(128)S(1)} %get-tuple-element.323, f32[128,128]{1,0:T(8,128)S(1)} %get-tuple-element.324, f32[128]{0:T(128)S(1)} %broadcast_multiply_fusion.2, ...), kind=kLoop, calls=%fused_computation.7.clone.1 | loop fusion | flops 35651584 | bytes 33753600 | tf_op jit(solution)/shard_map/while/body/eval_jaxpr/sub | solution.py:119
  244.7 12.1 %fusion.188 = (f32[128,128,128]{2,1,0:T(8,128)}, f32[128,128,128]{2,1,0:T(8,128)}) fusion(f32[128,128,128]{2,1,0:T(8,128)} %get-tuple-element.340, f32[128,128]{1,0:T(8,128)S(1)} %get-tuple-element.321, f32[128]{0:T(128)S(1)} %get-tuple-element.323, f32[128,128]{1,0:T(8,128)S(1)} %get-tuple-element.324, f32[128]{0:T(128)S(1)} %broadcast_multiply_fusion.2, ...), kind=kLoop, calls=%fused_computation.7.clone.1 | loop fusion | flops 35651584 | bytes 33753600 | tf_op jit(solution)/shard_map/while/body/eval_jaxpr/sub | solution.py:119
  257.3 12.1 %fusion.188 = (f32[128,128,128]{2,1,0:T(8,128)}, f32[128,128,128]{2,1,0:T(8,128)}) fusion(f32[128,128,128]{2,1,0:T(8,128)} %get-tuple-element.340, f32[128,128]{1,0:T(8,128)S(1)} %get-tuple-element.321, f32[128]{0:T(128)S(1)} %get-tuple-element.323, f32[128,128]{1,0:T(8,128)S(1)} %get-tuple-element.324, f32[128]{0:T(128)S(1)} %broadcast_multiply_fusion.2, ...), kind=kLoop, calls=%fused_computation.7.clone.1 | loop fusion | flops 35651584 | bytes 33753600 | tf_op jit(solution)/shard_map/while/body/eval_jaxpr/sub | solution.py:119
  286.5 11.7 %multiply_add_fusion.1 = (f32[128,128,128]{2,0,1:T(8,128)S(1)}, f32[128,128,128]{2,0,1:T(8,128)S(1)}) fusion(f32[128,128]{0,1:T(8,128)S(1)} %copy.72, f32[128,128]{0,1:T(8,128)S(1)} %copy.69, f32[128,128,128]{2,0,1:T(8,128)S(1)} %fusion.58, f32[128,128,128]{2,0,1:T(8,128)} %fusion.56, f32[128,128,128]{2,0,1:T(8,128)} %fusion.54, ...), kind=kOutput, calls=%fused_computation.52 | convolution fusion | flops 287457280 | bytes 44171264 | tf_op jit(solution)/shard_map/ka,abc->kbc/dot_general | solution.py:62
  298.2 17.5 %fusion.31 = f32[128,128,128]{2,0,1:T(8,128)} fusion(f32[128,128,128]{2,0,1:T(8,128)S(1)} %get-tuple-element.264), kind=kOutput, calls=%fused_computation.58 | convolution fusion | flops 3221454848 | bytes 16777216 | tf_op jit(solution)/shard_map/kbc,bm->kmc/dot_general | solution.py:40
  315.7 17.6 %fusion.33 = f32[128,128,128]{2,0,1:T(8,128)} fusion(f32[128,128,128]{2,0,1:T(8,128)S(1)} %get-tuple-element.264), kind=kOutput, calls=%fused_computation.60 | convolution fusion | flops 3221454848 | bytes 16777216 | tf_op jit(solution)/shard_map/kbc,bm->kmc/dot_general | solution.py:40
  333.3 17.7 %fusion.29 = f32[128,128,128]{2,0,1:T(8,128)} fusion(f32[128,128,128]{2,0,1:T(8,128)S(1)} %get-tuple-element.265), kind=kOutput, calls=%fused_computation.56 | convolution fusion | flops 3221454848 | bytes 16777216 | tf_op jit(solution)/shard_map/kbc,bm->kmc/dot_general | solution.py:40
  351.1 27.7 %fusion.25 = (f32[128,128,128]{2,1,0:T(8,128)}, f32[128,128,128]{2,1,0:T(8,128)}) fusion(f32[128,128,128]{2,1,0:T(8,128)} %get-tuple-element.149, f32[128,128,128]{2,1,0:T(8,128)} %get-tuple-element.148, f32[128,128,128]{2,0,1:T(8,128)} %fusion.31, f32[128,128,128]{2,0,1:T(8,128)} %fusion.33, f32[128,128,128]{2,0,1:T(8,128)} %fusion.29, ...), kind=kOutput, calls=%fused_computation.45 | convolution fusion | flops 3238232064 | bytes 67108864 | tf_op jit(solution)/shard_map/kbc,bm->kmc/dot_general | solution.py:40
  378.8 11.7 %fusion.74 = f32[128,128,128]{2,0,1:T(8,128)S(1)} fusion(f32[128,128,128]{2,1,0:T(8,128)} %get-tuple-element.262), kind=kOutput, calls=%fused_computation.118 | convolution fusion | flops 3221454848 | bytes 16777216 | tf_op jit(solution)/shard_map/kmc,bm->kbc/dot_general | solution.py:40
  399.1 10.9 %fusion.66 = f32[128,128,128]{2,0,1:T(8,128)S(1)} fusion(f32[128,128,128]{2,1,0:T(8,128)} %get-tuple-element.263), kind=kOutput, calls=%fused_computation.110 | convolution fusion | flops 3221454848 | bytes 16777216 | tf_op jit(solution)/shard_map/kmc,bm->kbc/dot_general | solution.py:40
  410.0 12.1 %fusion.72 = f32[128,128,128]{2,0,1:T(8,128)} fusion(f32[128,128,128]{2,1,0:T(8,128)} %get-tuple-element.263), kind=kOutput, calls=%fused_computation.116 | convolution fusion | flops 3221454848 | bytes 16777216 | tf_op jit(solution)/shard_map/kmc,bm->kbc/dot_general | solution.py:40
  422.1 33.1 %fusion.20 = f32[64,128,128]{2,0,1:T(8,128)} fusion(f32[128,128]{0,1:T(8,128)S(1)} %copy.72, f32[128,128]{0,1:T(8,128)S(1)} %copy.69, f32[128,128,128]{2,0,1:T(8,128)S(1)} %fusion.66, f32[128,128,128]{2,0,1:T(8,128)S(1)} %fusion.74, f32[128,128,128]{2,0,1:T(8,128)S(1)} %fusion.64, f32[128,128,128]{2,0,1:T(8,128)} %fusion.72), kind=kOutput, calls=%fused_computation.38 | convolution fusion | flops 1621213184 | bytes 37879808 | tf_op jit(solution)/shard_map/ka,kbc->abc/dot_general | solution.py:40
  455.2 33.1 %subtract_multiply_fusion = f32[64,128,128]{2,0,1:T(8,128)} fusion(f32[64,128,128]{2,0,1:T(8,128)} %fusion.20, f32[128,128]{0,1:T(8,128)S(1)} %copy.72, f32[128,128]{0,1:T(8,128)S(1)} %copy.69, f32[128,128,128]{2,0,1:T(8,128)S(1)} %fusion.66, f32[128,128,128]{2,0,1:T(8,128)S(1)} %fusion.74, f32[128,128,128]{2,0,1:T(8,128)S(1)} %fusion.64, ...), kind=kOutput, calls=%fused_computation.86 | convolution fusion | flops 1623310336 | bytes 42074112 | tf_op jit(solution)/shard_map/ka,kbc->abc/dot_general | solution.py:40
  502.4 53.5 %all-to-all-done.1 = f32[16,512,128]{2,1,0:T(8,128)} async-done(((f32[16,512,128]{2,1,0:T(8,128)}), f32[16,512,128]{2,1,0:T(8,128)}, u32[]{:S(2)}, u32[]{:S(2)}) %all-to-all-start.1) | async-done | bytes 4194336 | tf_op jit(solution)/shard_map/all_to_all | solution.py:170
  568.6 13.9 %convolution_convert_fusion = bf16[512,4096]{1,0:T(8,128)(2,1)} fusion(bf16[512,2048]{0,1:T(8,128)(2,1)S(1)} %fusion.45, bf16[2048,4096]{1,0:T(8,128)(2,1)} %param.15), kind=kOutput, calls=%fused_computation.69 | convolution fusion | flops 8592031744 | bytes 23068672 | tf_op jit(solution)/shard_map/dot_general | solution.py:174
  582.5 65.2 %reduce-scatter.2.cloned.1.call-done = bf16[256,4096]{1,0:T(8,128)(2,1)} async-done(((bf16[512,4096]{1,0:T(8,128)(2,1)}), bf16[256,4096]{1,0:T(8,128)(2,1)}) %reduce-scatter.2.cloned.1.call-update) | async-done | bytes 2097168 | tf_op jit(solution)/shard_map/reduce_scatter | solution.py:173
  (129 shorter events, 94.1 us)
Async XLA Ops:
  7.5 14.5 %collective-permute-start = (bf16[2,3,2048]{2,0,1:T(2,128)(2,1)S(1)}, bf16[2,3,2048]{2,0,1:T(2,128)(2,1)S(1)}, u32[]{:S(2)}, u32[]{:S(2)}) collective-permute-start(bf16[2,3,2048]{2,0,1:T(2,128)(2,1)S(1)} %slice.37), channel_id=1, source_target_pairs={{0,8},{8,16},{16,24},{24,32},{32,40},{40,48},{48,56},{56,64},{64,7... | collective-permute-start | bytes 73736 | tf_op jit(solution)/shard_map/ppermute | solution.py:18
  12.6 44.9 %copy-start.4 = (s32[512]{0:T(512)}, s32[512]{0:T(512)S(1)}, u32[]{:S(2)}) copy-start(s32[512]{0:T(512)S(1)} %multiply_add_fusion.2) | copy-start | bytes 6148
  51.8 4.5 copy-start
  60.4 209.7 %all-to-all-start = ((bf16[512,16,128]{0,2,1:T(8,128)(2,1)}), bf16[512,16,128]{0,2,1:T(8,128)(2,1)S(1)}, u32[]{:S(2)}, u32[]{:S(2)}) async-start(bf16[512,16,128]{0,2,1:T(8,128)(2,1)} %select_convert_fusion), calls=%async_computation | async-start | bytes 4194304 | tf_op jit(solution)/shard_map/all_to_all | solution.py:166
  270.2 1.3 copy-start.3
  298.2 35.1 %copy-start.2 = (f32[128,128,128]{2,0,1:T(8,128)}, f32[128,128,128]{2,0,1:T(8,128)S(1)}, u32[]{:S(2)}) copy-start(f32[128,128,128]{2,0,1:T(8,128)S(1)} %get-tuple-element.265) | copy-start | bytes 25165828
  378.8 11.7 %copy-start.1 = (f32[128,128,128]{2,1,0:T(8,128)S(1)}, f32[128,128,128]{2,1,0:T(8,128)}, u32[]{:S(2)}) copy-start(f32[128,128,128]{2,1,0:T(8,128)} %get-tuple-element.262) | copy-start | bytes 25165828
  494.9 66.6 %copy-start.5 = (s32[512]{0:T(512)S(1)}, s32[512]{0:T(512)}, u32[]{:S(2)}) copy-start(s32[512]{0:T(512)} %copy-done.4) | copy-start | bytes 6148
  494.9 66.6 %copy-start.6 = (f32[2048]{0:T(1024)S(1)}, f32[2048]{0:T(1024)}, u32[]{:S(2)}) copy-start(f32[2048]{0:T(1024)} %param.13) | copy-start | bytes 24580
  494.9 61.1 %all-to-all-start.1 = ((f32[16,512,128]{2,1,0:T(8,128)}), f32[16,512,128]{2,1,0:T(8,128)}, u32[]{:S(2)}, u32[]{:S(2)}) async-start(f32[16,512,128]{2,1,0:T(8,128)} %bitcast.146), calls=%async_computation.1 | async-start | bytes 8388608 | tf_op jit(solution)/shard_map/all_to_all | solution.py:170
  502.4 145.3 %reduce-scatter.2.cloned.1.call-start = ((), (), s32[]{:S(2)}) async-start(), calls=%async_computation.3 | async-start | bytes 6291456 | tf_op jit(solution)/shard_map/reduce_scatter | solution.py:173
Sparse Core Ops, SparseCore 0:
  582.7 65.0 reduce-scatter.1
where the time goes:
time: 663 us; the launch traced here: 655 us
  other arithmetic  241 us (36%)
  matrix products  228 us (34%)
  waiting for transfers between devices  119 us (18%)
  local copies, waits for them, and re-layouts  34.1 us (5%)
  starting transfers between devices  17.9 us (3%)
  between operations  14.5 us (2%)
    sub x16, other arithmetic, add_mode(): return (totals[0] + scale * denom_real, totals[1] - scale * denom_imag)  191 us
    dot_general x10, matrix products, contract(): return jnp.einsum(form, left, right, precision=precise)  190 us
    reduce_scatter x1, waiting for transfers between devices, body(): lax.psum_scatter(jnp.dot(mixed, out_weight, preferred_element_type=jnp.fl...  65.2 us
    all_to_all x1, waiting for transfers between devices, body(): lax.all_to_all(convolved, 'ctx', split_axis=0, concat_axis=1, tiled=True)  53.5 us
    add x1, other arithmetic, body(): filtered + short_filter[:, lag, :][None] * joined[SHORT - 1 - lag:SHORT -...  17.3 us
    dot_general x2, matrix products, narrow_section(): jnp.einsum('ka,abc->kbc', lower, grid, preferred_element_type=jnp.float32)  16.8 us
    unnamed x17, local copies, waits for them, and re-layouts  14.5 us
    dot_general x1, matrix products, body(): jnp.dot(mixed, out_weight, preferred_element_type=jnp.float32)  13.9 us
  transfers between devices with their start and end apart: 4, of which 2 were waited for; matrix products, arithmetic and copies ran while one was open for 32% of the time, Pallas kernels for 0%

commit v1 on v0

v1 whole, which is shorter than its diff:
```python
import math

import jax
import jax.numpy as jnp
from jax import lax
from jax.experimental import pallas as pl
from jax.experimental.pallas import tpu as pltpu
from jax.sharding import PartitionSpec as P

SHORT = 3
ORDER = 16
LANES = 128
SUBS = 8
KEEP_SCALE = 8.0 / 7.0
COL_CHUNKS = 4


def rates_of(mix, length):
    return jnp.exp(-((1.0 - mix) * math.log(length) + mix * math.log(30.0)))


def row(table, index):
    return jnp.broadcast_to(table[index : index + 1, :], (SUBS, table.shape[1]))


def gate_kernel(tokens, half, step_rows, width, info, key_ref, value_ref, edge_ref, taps_ref, mix_ref,
                gated_ref, start_ref, end_ref, key_rows, value_rows):
    block = pl.program_id(0)
    lane = lax.broadcasted_iota(jnp.int32, (SUBS, LANES), 1)
    sub = lax.broadcasted_iota(jnp.int32, (SUBS, LANES), 0)
    for group in range(width // LANES):
        cols = slice(group * LANES, (group + 1) * LANES)
        key_rows[SUBS:, :] = key_ref[:, cols].astype(jnp.float32)
        value_rows[SUBS:, :] = value_ref[:, cols].astype(jnp.float32)
        key_rows[SUBS - 2 : SUBS, :] = edge_ref[0, :, cols]
        value_rows[SUBS - 2 : SUBS, :] = edge_ref[1, :, cols]
        taps = taps_ref[:, cols]
        key_taps = [row(taps, 3 + lag) * KEEP_SCALE for lag in range(SHORT)]
        value_taps = [row(taps, 6 + lag) for lag in range(SHORT)]
        rates = rates_of(mix_ref[:, cols], tokens)
        decay = jnp.exp(-rates)
        decays = [row(decay, r) for r in range(ORDER)]
        channel = info[2] + block * width + group * LANES + lane
        carried = None
        for part in range(2):
            base = SUBS + part * half
            first = info[1] + part * half + sub * step_rows
            bits = info[0] + first * jnp.int32(-1640531535) + channel * jnp.int32(-2048144777)

            def load(rows, at):
                return rows[pl.ds(at, SUBS, stride=step_rows), :]

            def pair(j, carry):
                states, k1, k2, v1, v2, bits = carry
                values = []
                for u in range(2):
                    k0 = load(key_rows, base + 2 * j + u)
                    v0 = load(value_rows, base + 2 * j + u)
                    keyed = key_taps[0] * k0 + key_taps[1] * k1 + key_taps[2] * k2
                    valued = value_taps[0] * v0 + value_taps[1] * v1 + value_taps[2] * v2
                    h = bits
                    h = h ^ lax.shift_right_logical(h, jnp.full_like(h, 16))
                    h = h * jnp.int32(2146121005)
                    h = h ^ lax.shift_right_logical(h, jnp.full_like(h, 15))
                    h = h * jnp.int32(-2073254261)
                    keep = (h & jnp.int32(-536870912)) != 0
                    values.append(jnp.where(keep, keyed * valued, 0.0))
                    k1, k2, v1, v2 = k0, k1, v0, v1
                    bits = bits + jnp.int32(-1640531535)
                rounded = jnp.concatenate(values, axis=0).astype(jnp.bfloat16)
                gated_ref[pl.ds(pl.multiple_of(part * half + j * 2 * SUBS, 2 * SUBS), 2 * SUBS), cols] = rounded
                wide = rounded.astype(jnp.float32)
                g0, g1 = wide[:SUBS], wide[SUBS:]
                states = tuple((x * a + g0) * a + g1 for x, a in zip(states, decays))
                return (states, k1, k2, v1, v2, bits)

            zero = jnp.zeros((SUBS, LANES), jnp.float32)
            init = (
                (zero,) * ORDER,
                load(key_rows, base - 1),
                load(key_rows, base - 2),
                load(value_rows, base - 1),
                load(value_rows, base - 2),
                bits,
            )
            states = lax.fori_loop(0, step_rows // 2, pair, init)[0]
            ends = []
            for r in range(ORDER):
                rate = row(rates, r)
                x = states[r]
                for d in (1, 2, 4):
                    factor = jnp.where(sub >= d, jnp.exp(-rate * float(d * step_rows)), 0.0)
                    x = x + factor * pltpu.roll(x, d, 0)
                before = jnp.where(sub >= 1, pltpu.roll(x, 1, 0), 0.0)
                last = jnp.broadcast_to(x[SUBS - 1 : SUBS, :], (SUBS, LANES))
                if part == 1:
                    before = before + jnp.exp(-rate * (sub * step_rows).astype(jnp.float32)) * carried[r]
                    last = last + jnp.exp(-rate * float(half)) * carried[r]
                    end_ref[r : r + 1, cols] = last[0:1, :]
                start_ref[part, r, :, cols] = before
                ends.append(last)
            carried = ends


def mix_kernel(tokens, half, step_rows, width, info, gated_ref, query_ref, edge_ref, taps_ref, mix_ref, residue_ref,
               skip_ref, start_ref, into_ref, mixed_ref, query_rows, mixed_rows, gains):
    sub = lax.broadcasted_iota(jnp.int32, (SUBS, LANES), 0)
    offset = (info[0] * half + sub * step_rows).astype(jnp.float32)
    for group in range(width // LANES):
        cols = slice(group * LANES, (group + 1) * LANES)
        query_rows[SUBS:, :] = query_ref[:, cols].astype(jnp.float32)
        query_rows[SUBS - 2 : SUBS, :] = edge_ref[0, :, cols]
        taps = taps_ref[:, cols]
        query_taps = [row(taps, lag) for lag in range(SHORT)]
        skip = row(skip_ref[:, cols], 0)
        rates = rates_of(mix_ref[:, cols], tokens)
        decay = jnp.exp(-rates)
        decays = [row(decay, r) for r in range(ORDER)]
        residue = residue_ref[:, cols]
        into = into_ref[:, cols]
        states = []
        for r in range(ORDER):
            gains[r] = row(residue, r)
            states.append(start_ref[0, r, :, cols] + jnp.exp(-row(rates, r) * offset) * row(into, r))

        def load(at):
            return query_rows[pl.ds(at, SUBS, stride=step_rows), :]

        def pair(j, carry):
            states, q1, q2 = carry
            wide = gated_ref[pl.ds(pl.multiple_of(j * 2 * SUBS, 2 * SUBS), 2 * SUBS), cols].astype(jnp.float32)
            for u in range(2):
                g = wide[u * SUBS : (u + 1) * SUBS]
                q0 = load(SUBS + 2 * j + u)
                query = query_taps[0] * q0 + query_taps[1] * q1 + query_taps[2] * q2
                states = tuple(x * a + g for x, a in zip(states, decays))
                terms = [x * gains[r] for r, x in enumerate(states)] + [skip * g]
                while len(terms) > 1:
                    terms = [sum(terms[k : k + 2][1:], terms[k]) for k in range(0, len(terms), 2)]
                mixed_rows[pl.ds(2 * j + u, SUBS, stride=step_rows), :] = query * terms[0]
                q1, q2 = q0, q1
            return (states, q1, q2)

        lax.fori_loop(0, step_rows // 2, pair, (tuple(states), load(SUBS - 1), load(SUBS - 2)))
        mixed_ref[:, cols] = mixed_rows[...].astype(jnp.bfloat16)


def gate(info, planes, edge, taps, mix, tokens):
    rows, channels = planes.shape[1:]
    width = 2 * LANES
    half = rows // 2
    step_rows = half // SUBS
    body = lambda *refs: gate_kernel(tokens, half, step_rows, width, *refs)
    return pl.pallas_call(
        body,
        out_shape=(
            jax.ShapeDtypeStruct((rows, channels), jnp.bfloat16),
            jax.ShapeDtypeStruct((2, ORDER, SUBS, channels), jnp.float32),
            jax.ShapeDtypeStruct((ORDER, channels), jnp.float32),
        ),
        grid_spec=pltpu.PrefetchScalarGridSpec(
            num_scalar_prefetch=1,
            grid=(channels // width,),
            in_specs=[
                pl.BlockSpec((None, rows, width), lambda b, s: (1, 0, b)),
                pl.BlockSpec((None, rows, width), lambda b, s: (2, 0, b)),
                pl.BlockSpec((2, 2, width), lambda b, s: (0, 0, b)),
                pl.BlockSpec((9, width), lambda b, s: (0, b)),
                pl.BlockSpec((ORDER, width), lambda b, s: (0, b)),
            ],
            out_specs=(
                pl.BlockSpec((rows, width), lambda b, s: (0, b)),
                pl.BlockSpec((2, ORDER, SUBS, width), lambda b, s: (0, 0, 0, b)),
                pl.BlockSpec((ORDER, width), lambda b, s: (0, b)),
            ),
            scratch_shapes=[pltpu.VMEM((SUBS + rows, LANES), jnp.float32)] * 2,
        ),
        name="gate",
        cost_estimate=pl.CostEstimate(flops=80 * rows * channels, bytes_accessed=8 * rows * channels, transcendentals=0),
    )(info, planes, planes, edge, taps, mix)


def blend(which, gated, planes, edges, taps, mix, residue, skip, start, into, tokens):
    rows, channels = gated.shape
    width = 2 * LANES
    half = rows // 2
    step_rows = half // SUBS
    body = lambda *refs: mix_kernel(tokens, half, step_rows, width, *refs)
    return pl.pallas_call(
        body,
        out_shape=jax.ShapeDtypeStruct((half, channels), jnp.bfloat16),
        grid_spec=pltpu.PrefetchScalarGridSpec(
            num_scalar_prefetch=1,
            grid=(channels // width,),
            in_specs=[
                pl.BlockSpec((half, width), lambda b, s: (s[0], b)),
                pl.BlockSpec((None, half, width), lambda b, s: (0, s[0], b)),
                pl.BlockSpec((1, 2, width), lambda b, s: (s[0], 0, b)),
                pl.BlockSpec((9, width), lambda b, s: (0, b)),
                pl.BlockSpec((ORDER, width), lambda b, s: (0, b)),
                pl.BlockSpec((ORDER, width), lambda b, s: (0, b)),
                pl.BlockSpec((1, width), lambda b, s: (0, b)),
                pl.BlockSpec((1, ORDER, SUBS, width), lambda b, s: (s[0], 0, 0, b)),
                pl.BlockSpec((ORDER, width), lambda b, s: (0, b)),
            ],
            out_specs=pl.BlockSpec((half, width), lambda b, s: (0, b)),
            scratch_shapes=[
                pltpu.VMEM((SUBS + half, LANES), jnp.float32),
                pltpu.VMEM((half, LANES), jnp.float32),
                pltpu.VMEM((ORDER, SUBS, LANES), jnp.float32),
            ],
        ),
        name="blend",
        cost_estimate=pl.CostEstimate(flops=80 * half * channels, bytes_accessed=8 * half * channels, transcendentals=0),
    )(which, gated, planes, edges, taps, mix, residue, skip, start, into)


def state_before(end, mix, tokens, rows, index, count):
    rates = rates_of(mix, tokens)
    total = end
    into = jnp.zeros_like(end)
    size = 1
    while size < count:
        other = lax.ppermute(total, "ctx", [(i, i ^ size) for i in range(count)])
        upper = (index // size) % 2 == 1
        inside = (index % size).astype(jnp.float32)
        into = into + jnp.where(upper, jnp.exp(-rates * (inside * rows)), 0.0) * other
        across = jnp.exp(-rates * float(rows * size))
        total = jnp.where(upper, across * other + total, across * total + other)
        size *= 2
    return into


def body(features, short_filter, mode_residue, decay_mix, skip_gain, counter, out_weight):
    rows = features.shape[0]
    channels = features.shape[2]
    count = lax.axis_size("ctx")
    tokens = rows * count
    index = lax.axis_index("ctx")
    side = lax.axis_index("ch")
    half = rows // 2
    planes = jnp.transpose(features, (1, 0, 2))
    edge = lax.ppermute(planes[:, rows - (SHORT - 1) :], "ctx", [(i, i + 1) for i in range(count - 1)])
    edge = edge.astype(jnp.float32)
    taps = short_filter.reshape(9, channels)
    info = jnp.stack([counter[0], counter[1] + index * rows, side * channels]).astype(jnp.int32)
    gated, start, end = gate(info, planes, edge[1:], taps, decay_mix, tokens)
    into = state_before(end, decay_mix, tokens, rows, index, count)
    edges = jnp.stack([edge[0], planes[0, half - (SHORT - 1) : half].astype(jnp.float32)])

    def mixed_of(which, after):
        return blend(which.reshape(1), gated, planes, edges, taps, decay_mix, mode_residue, skip_gain[None], start, after, tokens)

    swap = [(0, 1), (1, 0)]
    cols = out_weight.shape[1] // COL_CHUNKS
    sent = mixed_of(1 - side, into)
    received = []
    for c in range(COL_CHUNKS):
        part = jnp.dot(sent, out_weight[:, c * cols : (c + 1) * cols], preferred_element_type=jnp.float32)
        part = part.astype(jnp.bfloat16)
        received.append(lax.ppermute(part, "ch", swap))
    into, part = lax.optimization_barrier((into, part))
    kept = mixed_of(side, into)
    outs = []
    for c in range(COL_CHUNKS):
        part = jnp.dot(kept, out_weight[:, c * cols : (c + 1) * cols], preferred_element_type=jnp.float32)
        outs.append((part + received[c].astype(jnp.float32)).astype(jnp.bfloat16))
    return jnp.concatenate(outs, axis=1)


def solution(mesh):
    placed = (
        P(("dp", "ctx"), None, "ch"),
        P(None, None, "ch"),
        P(None, "ch"),
        P(None, "ch"),
        P("ch"),
        P("dp"),
        P("ch", None),
    )
    return jax.shard_map(
        body, mesh=mesh, in_specs=placed, out_specs=P(("dp", "ctx", "ch"), None), check_vma=False
    )
```

time: 663 us -> 132 us (0.20); the launches traced: 655 us -> 131 us
  other arithmetic: 241 us -> 6.07 us
  matrix products: 228 us -> 30 us
  waiting for transfers between devices: 119 us -> 27.1 us
  Pallas kernels: 0 us -> 47.1 us
  local copies, waits for them, and re-layouts: 34.1 us -> 4.51 us
  between operations: 14.5 us -> 0.84 us
    dot_general x15 -> x8, matrix products: 228 us -> 30 us  [the longest x4 15.7 us: body(): jnp.dot(sent, out_weight[:, c * cols:(c + 1) * cols], preferred_element_t...]
    sub x16 -> x0, other arithmetic: 191 us -> none  [add_mode(): return (totals[0] + scale * denom_real, totals[1] - scale * denom_imag)]
    reduce_scatter x1 -> x0, waiting for transfers between devices: 65.2 us -> none  [body(): lax.psum_scatter(jnp.dot(mixed, out_weight, preferred_element_type=jnp.fl...]
    all_to_all x2 -> x0, waiting for transfers between devices: 53.5 us -> none  [the longest x1 53.5 us: body(): lax.all_to_all(convolved, 'ctx', split_axis=0, concat_axis=1, tiled=True)]
    pallas_call x0 -> x3, Pallas kernels: none -> 47.1 us  [the longest x2 23.6 us: blend(): pl.pallas_call(body, out_shape=jax.ShapeDtypeStruct((half, channels), jnp...]
    ppermute x1 -> x9, waiting for transfers between devices: 0.01 us -> 27.1 us  [the longest x4 14.1 us: body(): received.append(lax.ppermute(part, 'ch', swap))]
    convert_element_type x3 -> x1, other arithmetic: 21.7 us -> 0.77 us  [body(): planes[0, half - (SHORT - 1):half].astype(jnp.float32)]
    add x2 -> x1, other arithmetic: 17.9 us -> 0.79 us  [state_before(): into + jnp.where(upper, jnp.exp(-rates * (inside * rows)), 0.0) * other]
  transfers between devices with their start and end apart: 4 -> 9, of which waited for: 2 -> 5; matrix products, arithmetic and copies ran while one was open for 32% -> 18% of each run, Pallas kernels for 0% -> 9%
where the time goes in v1:
time: 132 us; the launch traced here: 131 us
  Pallas kernels  47.1 us (36%)
  matrix products  30 us (23%)
  waiting for transfers between devices  27.1 us (21%)
  starting transfers between devices  15.8 us (12%)
  other arithmetic  6.07 us (5%)
  local copies, waits for them, and re-layouts  4.51 us (3%)
    pallas_call x2, Pallas kernels, blend(): pl.pallas_call(body, out_shape=jax.ShapeDtypeStruct((half, channels), jnp...  23.6 us
    pallas_call x1, Pallas kernels, gate(): pl.pallas_call(body, out_shape=(jax.ShapeDtypeStruct((rows, channels), jn...  23.5 us
    dot_general x4, matrix products, body(): jnp.dot(sent, out_weight[:, c * cols:(c + 1) * cols], preferred_element_t...  15.7 us
    dot_general x4, matrix products, body(): jnp.dot(kept, out_weight[:, c * cols:(c + 1) * cols], preferred_element_t...  14.3 us
    ppermute x4, waiting for transfers between devices, body(): received.append(lax.ppermute(part, 'ch', swap))  14.1 us
    ppermute x4, waiting for transfers between devices, state_before(): other = lax.ppermute(total, 'ctx', [(i, i ^ size) for i in range(count)])  13 us
    ppermute x4, starting transfers between devices, state_before(): other = lax.ppermute(total, 'ctx', [(i, i ^ size) for i in range(count)])  10.4 us
    ppermute x4, starting transfers between devices, body(): received.append(lax.ppermute(part, 'ch', swap))  4.13 us
  transfers between devices with their start and end apart: 9, of which 5 were waited for; matrix products, arithmetic and copies ran while one was open for 18% of the time, Pallas kernels for 9%

profile of v1, /device:TPU:0, one launch (start us, length us, event | category | flops | bytes accessed | tf_op | source)
XLA Modules:
  0.0 131.5 jit_solution(6676681360100594642)
XLA Ops:
  0.0 0.9 slice.44
  0.9 1.3 collective-permute-start
  2.2 1.4 %fusion.28 = (s32[1]{0:T(128)}, s32[1]{0:T(128)}) fusion(s32[2]{0:T(128)} %param.12), kind=kLoop, calls=%fused_computation.33 | loop fusion | bytes 16 | tf_op jit(solution)/shard_map/slice | solution.py:246
  4.2 1.3 pad_add_fusion.refs_0_
  5.5 1.6 %reshape.10.refs_4_ = f32[9,2048]{1,0:T(8,128)} reshape(f32[3,3,2048]{2,1,0:T(4,128)} %param.8) | data formatting | bytes 147456 | tf_op jit(solution)/shard_map/reshape | solution.py:245
  7.7 23.5 %gate.1 = (bf16[512,2048]{1,0:T(8,128)(2,1)}, f32[2,16,8,2048]{3,2,1,0:T(8,128)}, f32[16,2048]{1,0:T(8,128)}) custom-call(s32[3]{0:T(128)} %pad_add_fusion.refs_0_, bf16[3,512,2048]{2,1,0:T(8,128)(2,1)} %bitcast.16, bf16[3,512,2048]{2,1,0:T(8,128)(2,1)} %bitcast.17, f32[2,2,2048]{2,1,0:T(2,128)} %slice.45.refs_3_, f32[9,2048]{1,0:T(8,128)} %reshape.10.refs_4_, ...), custom_call_target="tpu_custom_call" | custom-call | flops 83886080 | bytes 8388608 | tf_op jit(solution)/shard_map/gate/pallas_call | solution.py:154
  31.2 4.7 %collective-permute-start.1 = (f32[16,2048]{1,0:T(8,128)}, f32[16,2048]{1,0:T(8,128)S(1)}, u32[]{:S(2)}, u32[]{:S(2)}) collective-permute-start(f32[16,2048]{1,0:T(8,128)} %get-tuple-element.11), channel_id=1, source_target_pairs={{0,8},{8,0},{16,24},{24,16},{32,40},{40,32},{48,56},{56,48},{64,72... | collective-permute-start | bytes 393224 | tf_op jit(solution)/shard_map/ppermute | solution.py:224
  35.9 1.2 collective-permute-done.1
  37.1 1.0 add_select_fusion.2
  38.8 6.6 %collective-permute-done.2 = f32[16,2048]{1,0:T(8,128)S(1)} collective-permute-done((f32[16,2048]{1,0:T(8,128)S(1)}, f32[16,2048]{1,0:T(8,128)S(1)}, u32[]{:S(2)}, u32[]{:S(2)}) %collective-permute-start.2) | collective-permute-done | bytes 131104 | tf_op jit(solution)/shard_map/ppermute | solution.py:224
  45.5 1.7 %collective-permute-start.3 = (f32[16,2048]{1,0:T(8,128)S(1)}, f32[16,2048]{1,0:T(8,128)S(1)}, u32[]{:S(2)}, u32[]{:S(2)}) collective-permute-start(f32[16,2048]{1,0:T(8,128)S(1)} %add_select_fusion.1), channel_id=1, source_target_pairs={{0,32},{8,40},{16,48},{24,56},{32,0},{40,8},{48,16},{56,24},{64,96... | collective-permute-start | bytes 393224 | tf_op jit(solution)/shard_map/ppermute | solution.py:224
  47.2 0.8 slice_convert_fusion
  48.0 2.5 %collective-permute-done.3 = f32[16,2048]{1,0:T(8,128)S(1)} collective-permute-done((f32[16,2048]{1,0:T(8,128)S(1)}, f32[16,2048]{1,0:T(8,128)S(1)}, u32[]{:S(2)}, u32[]{:S(2)}) %collective-permute-start.3) | collective-permute-done | bytes 131104 | tf_op jit(solution)/shard_map/ppermute | solution.py:224
  50.6 3.3 %collective-permute-start.4 = (f32[16,2048]{1,0:T(8,128)S(1)}, f32[16,2048]{1,0:T(8,128)S(1)}, u32[]{:S(2)}, u32[]{:S(2)}) collective-permute-start(f32[16,2048]{1,0:T(8,128)S(1)} %add_select_fusion), channel_id=1, source_target_pairs={{0,64},{8,72},{16,80},{24,88},{32,96},{40,104},{48,112},{56,120},{... | collective-permute-start | bytes 393224 | tf_op jit(solution)/shard_map/ppermute | solution.py:224
  54.5 2.7 %collective-permute-done.4 = f32[16,2048]{1,0:T(8,128)S(1)} collective-permute-done((f32[16,2048]{1,0:T(8,128)S(1)}, f32[16,2048]{1,0:T(8,128)S(1)}, u32[]{:S(2)}, u32[]{:S(2)}) %collective-permute-start.4) | collective-permute-done | bytes 131104 | tf_op jit(solution)/shard_map/ppermute | solution.py:224
  57.2 0.8 multiply_add_fusion.refs_9_
  58.0 11.8 %blend.2 = bf16[256,2048]{1,0:T(8,128)(2,1)} custom-call(s32[1]{0:T(128)} %bitcast.6.refs_0_, bf16[512,2048]{1,0:T(8,128)(2,1)} %get-tuple-element.9.refs_1_, bf16[3,512,2048]{2,1,0:T(8,128)(2,1)} %bitcast.19, f32[2,2,2048]{2,1,0:T(2,128)} %pad_maximum_fusion.1.refs_3_, f32[9,2048]{1,0:T(8,128)} %reshape.10.refs_4_, f32[16,2048]{1,0:T(8,128)} %refs_5_.5, ...), custom_call_target="tpu_custom_call" | custom-call | flops 41943040 | bytes 4194304 | tf_op jit(solution)/shard_map/blend/pallas_call | solution.py:189
  69.8 3.8 %fusion.16 = bf16[256,1024]{1,0:T(8,128)(2,1)S(1)} fusion(bf16[256,2048]{1,0:T(8,128)(2,1)} %blend.2, bf16[2048,4096]{1,0:T(8,128)(2,1)} %param.13), kind=kOutput, calls=%fused_computation.17 | convolution fusion | flops 1074003968 | bytes 5767168 | tf_op jit(solution)/shard_map/dot_general | solution.py:259
  73.6 4.2 %fusion.19 = bf16[256,1024]{1,0:T(8,128)(2,1)} fusion(bf16[256,2048]{1,0:T(8,128)(2,1)S(1)} %copy-done.2, bf16[2048,4096]{1,0:T(8,128)(2,1)} %param.13), kind=kOutput, calls=%fused_computation.18 | convolution fusion | flops 1074003968 | bytes 5767168 | tf_op jit(solution)/shard_map/dot_general | solution.py:259
  77.9 1.0 collective-permute-start.5
  78.9 4.2 %fusion.22 = bf16[256,1024]{1,0:T(8,128)(2,1)} fusion(bf16[256,2048]{1,0:T(8,128)(2,1)S(1)} %copy-done.2, bf16[2048,4096]{1,0:T(8,128)(2,1)} %param.13), kind=kOutput, calls=%fused_computation.19 | convolution fusion | flops 1074003968 | bytes 5767168 | tf_op jit(solution)/shard_map/dot_general | solution.py:259
  83.1 1.0 collective-permute-start.6
  84.1 3.4 %fusion.25 = bf16[256,1024]{1,0:T(8,128)(2,1)S(1)} fusion(bf16[256,2048]{1,0:T(8,128)(2,1)S(1)} %copy-done.2, bf16[2048,4096]{1,0:T(8,128)(2,1)} %param.13), kind=kOutput, calls=%fused_computation.20 | convolution fusion | flops 1074003968 | bytes 5767168 | tf_op jit(solution)/shard_map/dot_general | solution.py:259
  87.6 1.1 collective-permute-start.8
  88.7 1.0 collective-permute-start.7
  89.7 11.8 %blend.3 = bf16[256,2048]{1,0:T(8,128)(2,1)} custom-call(s32[1]{0:T(128)} %bitcast.refs_0_, bf16[512,2048]{1,0:T(8,128)(2,1)} %get-tuple-element.9.refs_1_, bf16[3,512,2048]{2,1,0:T(8,128)(2,1)} %bitcast.20, f32[2,2,2048]{2,1,0:T(2,128)} %pad_maximum_fusion.1.refs_3_, f32[9,2048]{1,0:T(8,128)} %reshape.10.refs_4_, f32[16,2048]{1,0:T(8,128)} %refs_5_.5, ...), custom_call_target="tpu_custom_call" | custom-call | flops 41943040 | bytes 4194304 | tf_op jit(solution)/shard_map/blend/pallas_call | solution.py:189
  101.5 3.8 %add_convert_fusion.3 = bf16[256,1024]{1,0:T(8,128)(2,1)S(1)} fusion(bf16[256,1024]{1,0:T(8,128)(2,1)S(1)} %collective-permute-done.5, bf16[256,2048]{1,0:T(8,128)(2,1)} %blend.3, bf16[2048,4096]{1,0:T(8,128)(2,1)} %param.13), kind=kOutput, calls=%fused_computation.24 | convolution fusion | flops 1074528256 | bytes 6291456 | tf_op jit(solution)/shard_map/dot_general | solution.py:266
  105.4 3.4 %add_convert_fusion.2 = bf16[256,1024]{1,0:T(8,128)(2,1)S(1)} fusion(bf16[256,1024]{1,0:T(8,128)(2,1)S(1)} %collective-permute-done.6, bf16[256,2048]{1,0:T(8,128)(2,1)S(1)} %copy-done.1, bf16[2048,4096]{1,0:T(8,128)(2,1)} %param.13), kind=kOutput, calls=%fused_computation.23 | convolution fusion | flops 1074528256 | bytes 6291456 | tf_op jit(solution)/shard_map/dot_general | solution.py:266
  108.8 14.1 %collective-permute-done.7 = bf16[256,1024]{1,0:T(8,128)(2,1)} collective-permute-done((bf16[256,1024]{1,0:T(8,128)(2,1)S(1)}, bf16[256,1024]{1,0:T(8,128)(2,1)}, u32[]{:S(2)}, u32[]{:S(2)}) %collective-permute-start.7) | collective-permute-done | bytes 524320 | tf_op jit(solution)/shard_map/ppermute | solution.py:261
  122.9 3.6 %add_convert_fusion.1 = bf16[256,1024]{1,0:T(8,128)(2,1)S(1)} fusion(bf16[256,1024]{1,0:T(8,128)(2,1)} %collective-permute-done.7, bf16[256,2048]{1,0:T(8,128)(2,1)S(1)} %copy-done.1, bf16[2048,4096]{1,0:T(8,128)(2,1)} %param.13), kind=kOutput, calls=%fused_computation.22 | convolution fusion | flops 1074528256 | bytes 6291456 | tf_op jit(solution)/shard_map/dot_general | solution.py:266
  126.5 3.4 %add_convert_fusion = bf16[256,1024]{1,0:T(8,128)(2,1)S(1)} fusion(bf16[256,1024]{1,0:T(8,128)(2,1)S(1)} %collective-permute-done.8, bf16[256,2048]{1,0:T(8,128)(2,1)S(1)} %copy-done.1, bf16[2048,4096]{1,0:T(8,128)(2,1)} %param.13), kind=kOutput, calls=%fused_computation.21 | convolution fusion | flops 1074528256 | bytes 6291456 | tf_op jit(solution)/shard_map/dot_general | solution.py:266
  130.0 1.5 %pad_maximum_fusion = bf16[256,4096]{1,0:T(8,128)(2,1)} fusion(bf16[256,1024]{1,0:T(8,128)(2,1)S(1)} %add_convert_fusion, bf16[256,1024]{1,0:T(8,128)(2,1)S(1)} %add_convert_fusion.1, bf16[256,1024]{1,0:T(8,128)(2,1)S(1)} %add_convert_fusion.2, bf16[256,1024]{1,0:T(8,128)(2,1)S(1)} %add_convert_fusion.3), kind=kLoop, calls=%fused_computation.16 | loop fusion | flops 8388608 | bytes 4194304 | tf_op jit(solution)/shard_map/concatenate | solution.py:268
  (16 shorter events, 2.1 us)
Async XLA Ops:
  0.9 6.2 %collective-permute-start = (bf16[3,2,2048]{2,1,0:T(2,128)(2,1)S(1)}, bf16[3,2,2048]{2,1,0:T(2,128)(2,1)S(1)}, u32[]{:S(2)}, u32[]{:S(2)}) collective-permute-start(bf16[3,2,2048]{2,1,0:T(2,128)(2,1)S(1)} %slice.44), channel_id=1, source_target_pairs={{0,8},{8,16},{16,24},{24,32},{32,40},{40,48},{48,56},{56,64},{64,7... | collective-permute-start | bytes 73736 | tf_op jit(solution)/shard_map/ppermute | solution.py:243
  7.7 29.4 %copy-start = (f32[16,2048]{1,0:T(8,128)S(1)}, f32[16,2048]{1,0:T(8,128)}, u32[]{:S(2)}) copy-start(f32[16,2048]{1,0:T(8,128)} %refs_5_.5) | copy-start | bytes 393220
  31.2 5.9 %collective-permute-start.1 = (f32[16,2048]{1,0:T(8,128)}, f32[16,2048]{1,0:T(8,128)S(1)}, u32[]{:S(2)}, u32[]{:S(2)}) collective-permute-start(f32[16,2048]{1,0:T(8,128)} %get-tuple-element.11), channel_id=1, source_target_pairs={{0,8},{8,0},{16,24},{24,16},{32,40},{40,32},{48,56},{56,48},{64,72... | collective-permute-start | bytes 393224 | tf_op jit(solution)/shard_map/ppermute | solution.py:224
  38.1 7.3 %collective-permute-start.2 = (f32[16,2048]{1,0:T(8,128)S(1)}, f32[16,2048]{1,0:T(8,128)S(1)}, u32[]{:S(2)}, u32[]{:S(2)}) collective-permute-start(f32[16,2048]{1,0:T(8,128)S(1)} %add_select_fusion.2), channel_id=1, source_target_pairs={{0,16},{8,24},{16,0},{24,8},{32,48},{40,56},{48,32},{56,40},{64,80... | collective-permute-start | bytes 393224 | tf_op jit(solution)/shard_map/ppermute | solution.py:224
  45.5 5.0 %collective-permute-start.3 = (f32[16,2048]{1,0:T(8,128)S(1)}, f32[16,2048]{1,0:T(8,128)S(1)}, u32[]{:S(2)}, u32[]{:S(2)}) collective-permute-start(f32[16,2048]{1,0:T(8,128)S(1)} %add_select_fusion.1), channel_id=1, source_target_pairs={{0,32},{8,40},{16,48},{24,56},{32,0},{40,8},{48,16},{56,24},{64,96... | collective-permute-start | bytes 393224 | tf_op jit(solution)/shard_map/ppermute | solution.py:224
  50.6 6.6 %collective-permute-start.4 = (f32[16,2048]{1,0:T(8,128)S(1)}, f32[16,2048]{1,0:T(8,128)S(1)}, u32[]{:S(2)}, u32[]{:S(2)}) collective-permute-start(f32[16,2048]{1,0:T(8,128)S(1)} %add_select_fusion), channel_id=1, source_target_pairs={{0,64},{8,72},{16,80},{24,88},{32,96},{40,104},{48,112},{56,120},{... | collective-permute-start | bytes 393224 | tf_op jit(solution)/shard_map/ppermute | solution.py:224
  69.8 3.9 %copy-start.2 = (bf16[256,2048]{1,0:T(8,128)(2,1)S(1)}, bf16[256,2048]{1,0:T(8,128)(2,1)}, u32[]{:S(2)}) copy-start(bf16[256,2048]{1,0:T(8,128)(2,1)} %blend.2) | copy-start | bytes 3145732
  77.9 23.6 %collective-permute-start.5 = (bf16[256,1024]{1,0:T(8,128)(2,1)}, bf16[256,1024]{1,0:T(8,128)(2,1)S(1)}, u32[]{:S(2)}, u32[]{:S(2)}) collective-permute-start(bf16[256,1024]{1,0:T(8,128)(2,1)} %fusion.19), channel_id=1, source_target_pairs={{0,4},{4,0},{1,5},{5,1},{2,6},{6,2},{3,7},{7,3},{8,12},{12,8},{9,1... | collective-permute-start | bytes 1572872 | tf_op jit(solution)/shard_map/ppermute | solution.py:261
  83.1 22.2 %collective-permute-start.6 = (bf16[256,1024]{1,0:T(8,128)(2,1)}, bf16[256,1024]{1,0:T(8,128)(2,1)S(1)}, u32[]{:S(2)}, u32[]{:S(2)}) collective-permute-start(bf16[256,1024]{1,0:T(8,128)(2,1)} %fusion.22), channel_id=1, source_target_pairs={{0,4},{4,0},{1,5},{5,1},{2,6},{6,2},{3,7},{7,3},{8,12},{12,8},{9,1... | collective-permute-start | bytes 1572872 | tf_op jit(solution)/shard_map/ppermute | solution.py:261
  87.6 38.9 %collective-permute-start.8 = (bf16[256,1024]{1,0:T(8,128)(2,1)S(1)}, bf16[256,1024]{1,0:T(8,128)(2,1)S(1)}, u32[]{:S(2)}, u32[]{:S(2)}) collective-permute-start(bf16[256,1024]{1,0:T(8,128)(2,1)S(1)} %fusion.16), channel_id=1, source_target_pairs={{0,4},{4,0},{1,5},{5,1},{2,6},{6,2},{3,7},{7,3},{8,12},{12,8},{9,1... | collective-permute-start | bytes 1572872 | tf_op jit(solution)/shard_map/ppermute | solution.py:261
  88.7 34.3 %collective-permute-start.7 = (bf16[256,1024]{1,0:T(8,128)(2,1)S(1)}, bf16[256,1024]{1,0:T(8,128)(2,1)}, u32[]{:S(2)}, u32[]{:S(2)}) collective-permute-start(bf16[256,1024]{1,0:T(8,128)(2,1)S(1)} %fusion.25), channel_id=1, source_target_pairs={{0,4},{4,0},{1,5},{5,1},{2,6},{6,2},{3,7},{7,3},{8,12},{12,8},{9,1... | collective-permute-start | bytes 1572872 | tf_op jit(solution)/shard_map/ppermute | solution.py:261
  101.5 3.9 %copy-start.1 = (bf16[256,2048]{1,0:T(8,128)(2,1)S(1)}, bf16[256,2048]{1,0:T(8,128)(2,1)}, u32[]{:S(2)}) copy-start(bf16[256,2048]{1,0:T(8,128)(2,1)} %blend.3) | copy-start | bytes 3145732

commit v2 on v1

v2 whole, which is shorter than its diff:
```python
import math

import jax
import jax.numpy as jnp
from jax import lax
from jax.experimental import pallas as pl
from jax.experimental.pallas import tpu as pltpu
from jax.sharding import PartitionSpec as P


SHORT = 3
ORDER = 16
LANES = 128
SUBS = 8
WIDTH = 2 * LANES
KEEP_SCALE = 8.0 / 7.0
SEND_COLS = 512
TILE_COLS = 256
BASE = 40
GAP = 4
QUAD = 4


def rates_of(mix, length):
    return jnp.exp(-((1.0 - mix) * math.log(length) + mix * math.log(30.0)))


def row(table, index):
    return jnp.broadcast_to(table[index : index + 1, :], (SUBS, table.shape[1]))


def spread(rows, source, cols, count, step):
    for n in range(count):
        at = BASE + n * (step + GAP)
        rows[at : at + step, :] = source[n * step : (n + 1) * step, cols].astype(jnp.float32)


def across(rows, at, step):
    return rows[pl.ds(at, SUBS, stride=step + GAP), :]


def lanes_of(block, group):
    return pl.ds(pl.multiple_of(block * WIDTH + group * LANES, LANES), LANES)


def state_of(own_ref, got_ref, core, group):
    blocks = pl.num_programs(0) // 2
    block = pl.program_id(0)
    lanes = lanes_of(block % blocks, group)
    return jnp.where(block // blocks == core, own_ref[:, lanes], got_ref[:, lanes])


def fill(table, values):
    for r in range(ORDER):
        table[r] = row(values, r)


def gate_kernel(tokens, half, step, counter, place, key_ref, value_ref, edge_ref, taps_ref, mix_ref,
                gated_ref, start_ref, mine_ref, other_ref, key_rows, value_rows, decays, taps):
    block = pl.program_id(0)
    lane = lax.broadcasted_iota(jnp.int32, (SUBS, LANES), 1)
    sub = lax.broadcasted_iota(jnp.int32, (SUBS, LANES), 0)
    is_mine = (block * 2) // pl.num_programs(0) == place[2]
    for group in range(WIDTH // LANES):
        cols = slice(group * LANES, (group + 1) * LANES)
        for rows, source, f in ((key_rows, key_ref, 1), (value_rows, value_ref, 2)):
            spread(rows, source, cols, 2 * SUBS, step)
            rows[BASE - GAP - 2 : BASE - GAP, :] = edge_ref[f, :, lanes_of(block, group)].astype(jnp.float32)
        for lag in range(SHORT):
            taps[lag] = row(taps_ref[1, :, cols], lag) * KEEP_SCALE
            taps[SHORT + lag] = row(taps_ref[2, :, cols], lag)
        rates = rates_of(mix_ref[:, cols], tokens)
        fill(decays, jnp.exp(-rates))
        jumps = {d: jnp.exp(-rates * float(d * step)) for d in (1, 2, 4)}
        whole = jnp.exp(-rates * float(half))
        channel = place[1] + block * WIDTH + group * LANES + lane
        carried = None
        for part in range(2):
            base = BASE + part * SUBS * (step + GAP)
            first = counter[1] + place[0] + part * half + sub * step
            bits = counter[0] + first * jnp.int32(-1640531535) + channel * jnp.int32(-2048144777)

            def quad(j, carry):
                states, k1, k2, v1, v2, bits = carry
                values = []
                for u in range(QUAD):
                    k0 = across(key_rows, base + QUAD * j + u, step)
                    v0 = across(value_rows, base + QUAD * j + u, step)
                    keyed = taps[0] * k0 + taps[1] * k1 + taps[2] * k2
                    valued = taps[3] * v0 + taps[4] * v1 + taps[5] * v2
                    h = bits + jnp.int32(-1640531535) * u
                    h = h ^ lax.shift_right_logical(h, jnp.full_like(h, 16))
                    h = h * jnp.int32(2146121005)
                    h = h ^ lax.shift_right_logical(h, jnp.full_like(h, 15))
                    h = h * jnp.int32(-2073254261)
                    keep = (h & jnp.int32(-536870912)) != 0
                    values.append(jnp.where(keep, keyed * valued, 0.0))
                    k1, k2, v1, v2 = k0, k1, v0, v1
                wides = []
                for u in range(0, QUAD, 2):
                    rounded = jnp.concatenate(values[u : u + 2], axis=0).astype(jnp.bfloat16)
                    at = pl.multiple_of(part * half + (QUAD * j + u) * SUBS, 2 * SUBS)
                    gated_ref[block, pl.ds(at, 2 * SUBS), cols] = rounded
                    wide = rounded.astype(jnp.float32)
                    wides += [wide[:SUBS], wide[SUBS:]]
                after = []
                for r, x in enumerate(states):
                    a = decays[r]
                    for g in wides:
                        x = x * a + g
                    after.append(x)
                return (tuple(after), k1, k2, v1, v2, bits + jnp.int32((-1640531535 * QUAD + 2**31) % 2**32 - 2**31))

            zero = jnp.zeros((SUBS, LANES), jnp.float32)
            init = (
                (zero,) * ORDER,
                across(key_rows, base - GAP - 1, step),
                across(key_rows, base - GAP - 2, step),
                across(value_rows, base - GAP - 1, step),
                across(value_rows, base - GAP - 2, step),
                bits,
            )
            states = lax.fori_loop(0, step // QUAD, quad, init)[0]
            ends = []
            for r in range(ORDER):
                x = states[r]
                for d in (1, 2, 4):
                    x = x + row(jumps[d], r) * jnp.where(sub >= d, pltpu.roll(x, d, 0), 0.0)
                before = jnp.where(sub >= 1, pltpu.roll(x, 1, 0), 0.0)
                last = jnp.broadcast_to(x[SUBS - 1 : SUBS, :], (SUBS, LANES))
                if part == 1:
                    rate = row(rates, r)
                    before = before + jnp.exp(-rate * (sub * step).astype(jnp.float32)) * carried[r]
                    last = last + row(whole, r) * carried[r]
                start_ref[part, block, r, :, cols] = before
                ends.append(last)
            carried = ends
        end = jnp.concatenate([last[0:1, :] for last in carried], axis=0)

        @pl.when(is_mine)
        def _():
            mine_ref[:, cols] = end

        @pl.when(jnp.logical_not(is_mine))
        def _():
            other_ref[:, cols] = end


def query_setup(tokens, step, side_half, cols, lanes, query_ref, tail_ref, edge_ref, taps_ref, mix_ref, query_rows, decays, taps):
    spread(query_rows, query_ref, cols, SUBS, step)
    tail = tail_ref[tail_ref.shape[0] - SUBS :, cols].astype(jnp.float32)[SUBS - 2 :]
    edge = edge_ref[0, :, lanes].astype(jnp.float32)
    query_rows[BASE - GAP - 2 : BASE - GAP, :] = jnp.where(side_half == 0, edge, tail)
    for lag in range(SHORT):
        taps[lag] = row(taps_ref[0, :, cols], lag)
    rates = rates_of(mix_ref[:, cols], tokens)
    fill(decays, jnp.exp(-rates))
    return rates


def scan_quad(step, j, carry, gated_ref, block, base, cols, query_rows, decays, gains, taps, skip, emit):
    states, q1, q2 = carry
    values = []
    for u in range(0, QUAD, 2):
        at = pl.multiple_of(base + (QUAD * j + u) * SUBS, 2 * SUBS)
        wide = gated_ref[block, pl.ds(at, 2 * SUBS), cols].astype(jnp.float32)
        values += [wide[:SUBS], wide[SUBS:]]
    totals = [skip * g for g in values]
    after = []
    for r, x in enumerate(states):
        a = decays[r]
        c = gains[r]
        for u, g in enumerate(values):
            x = x * a + g
            totals[u] = totals[u] + x * c
        after.append(x)
    for u in range(QUAD):
        q0 = across(query_rows, BASE + QUAD * j + u, step)
        emit(u, taps[0] * q0 + taps[1] * q1 + taps[2] * q2, totals[u])
        q1, q2 = q0, q1
    return (tuple(after), q1, q2)


def gather(mixed_ref, mixed_rows, cols, step):
    for n in range(SUBS):
        at = n * (step + GAP)
        mixed_ref[n * step : (n + 1) * step, cols] = mixed_rows[at : at + step, :].astype(jnp.bfloat16)


def local_kernel(tokens, half, step, at, which, gated_ref, query_ref, tail_ref, edge_ref, taps_ref, mix_ref, residue_ref,
                 skip_ref, start_ref, *rest):
    local_ref, filtered_ref, query_rows, decays, gains, taps = rest[-6:]
    block = at + pl.program_id(0)
    base = which[0] * half
    for group in range(WIDTH // LANES):
        cols = slice(group * LANES, (group + 1) * LANES)
        lanes = lanes_of(block, group)
        query_setup(tokens, step, which[0], cols, lanes, query_ref, tail_ref, edge_ref, taps_ref, mix_ref, query_rows, decays, taps)
        fill(gains, residue_ref[:, cols])
        skip = row(skip_ref[:, cols], 0)

        def quad(j, carry):
            def emit(u, query, total):
                spot = pl.ds(pl.multiple_of((QUAD * j + u) * SUBS, SUBS), SUBS)
                local_ref[block, spot, cols] = total
                filtered_ref[block, spot, cols] = query

            return scan_quad(step, j, carry, gated_ref, block, base, cols, query_rows, decays, gains, taps, skip, emit)

        states = tuple(start_ref[which[0], block, r, :, cols] for r in range(ORDER))
        q1, q2 = across(query_rows, BASE - GAP - 1, step), across(query_rows, BASE - GAP - 2, step)
        lax.fori_loop(0, step // QUAD, quad, (states, q1, q2))


def blend_kernel(tokens, half, step, which, gated_ref, query_ref, tail_ref, edge_ref, taps_ref, mix_ref, residue_ref,
                 skip_ref, start_ref, own_ref, got_ref, mixed_ref, query_rows, decays, gains, taps, mixed_rows):
    sub = lax.broadcasted_iota(jnp.int32, (SUBS, LANES), 0)
    block = pl.program_id(0)
    base = which[0] * half
    offset = (base + sub * step).astype(jnp.float32)
    for group in range(WIDTH // LANES):
        cols = slice(group * LANES, (group + 1) * LANES)
        lanes = lanes_of(pl.program_id(0), group)
        rates = query_setup(tokens, step, which[0], cols, lanes, query_ref, tail_ref, edge_ref, taps_ref, mix_ref, query_rows, decays, taps)
        fill(gains, residue_ref[:, cols])
        skip = row(skip_ref[:, cols], 0)
        into = state_of(own_ref, got_ref, which[1], group)

        def quad(j, carry):
            def emit(u, query, total):
                mixed_rows[pl.ds(QUAD * j + u, SUBS, stride=step + GAP), :] = query * total

            return scan_quad(step, j, carry, gated_ref, block, base, cols, query_rows, decays, gains, taps, skip, emit)

        states = tuple(
            start_ref[which[0], block, r, :, cols] + jnp.exp(-row(rates, r) * offset) * row(into, r) for r in range(ORDER)
        )
        q1, q2 = across(query_rows, BASE - GAP - 1, step), across(query_rows, BASE - GAP - 2, step)
        lax.fori_loop(0, step // QUAD, quad, (states, q1, q2))
        gather(mixed_ref, mixed_rows, cols, step)


def carry_kernel(tokens, half, step, which, local_ref, filtered_ref, mix_ref, residue_ref, own_ref, got_ref,
                 mixed_ref, decays, mixed_rows):
    sub = lax.broadcasted_iota(jnp.int32, (SUBS, LANES), 0)
    block = pl.program_id(0)
    offset = (which[0] * half + sub * step + 1).astype(jnp.float32)
    for group in range(WIDTH // LANES):
        cols = slice(group * LANES, (group + 1) * LANES)
        rates = rates_of(mix_ref[:, cols], tokens)
        fill(decays, jnp.exp(-rates))
        into = state_of(own_ref, got_ref, which[1], group) * residue_ref[:, cols]

        def quad(j, states):
            totals = [None] * QUAD
            after = []
            for r, x in enumerate(states):
                a = decays[r]
                for u in range(QUAD):
                    totals[u] = x if totals[u] is None else totals[u] + x
                    x = x * a
                after.append(x)
            for u in range(QUAD):
                at = pl.multiple_of((QUAD * j + u) * SUBS, SUBS)
                spot = pl.ds(at, SUBS)
                value = filtered_ref[block, spot, cols] * (local_ref[block, spot, cols] + totals[u])
                mixed_rows[pl.ds(QUAD * j + u, SUBS, stride=step + GAP), :] = value
            return tuple(after)

        states = tuple(jnp.exp(-row(rates, r) * offset) * row(into, r) for r in range(ORDER))
        lax.fori_loop(0, step // QUAD, quad, states)
        gather(mixed_ref, mixed_rows, cols, step)


def project_kernel(mixed_ref, weight_ref, out_ref):
    out_ref[...] = jnp.dot(mixed_ref[...], weight_ref[...], preferred_element_type=jnp.float32).astype(out_ref.dtype)


def combine_kernel(own_ref, got_ref, *rest):
    rest[-1][...] = (own_ref[...] + got_ref[...].astype(jnp.float32)).astype(jnp.bfloat16)


def table(count=ORDER):
    return pltpu.VMEM((count, SUBS, LANES), jnp.float32)


def room(mib):
    return pltpu.CompilerParams(vmem_limit_bytes=mib * 2**20)


def cost(vectors, moved):
    return pl.CostEstimate(flops=vectors, bytes_accessed=moved, transcendentals=0)


def gate(counter, place, planes, edge, taps, mix, tokens):
    rows, channels = planes.shape[1:]
    half = rows // 2
    step = half // SUBS
    blocks = channels // WIDTH
    spread_rows = BASE + 2 * SUBS * (step + GAP)
    first = lambda b, owner: jnp.clip(b - owner * (blocks // 2), 0, blocks // 2 - 1)
    return pl.pallas_call(
        lambda *refs: gate_kernel(tokens, half, step, *refs),
        out_shape=(
            pltpu.VMEM((blocks, rows, WIDTH), jnp.bfloat16),
            pltpu.VMEM((2, blocks, ORDER, SUBS, WIDTH), jnp.float32),
            jax.ShapeDtypeStruct((ORDER, channels // 2), jnp.float32),
            jax.ShapeDtypeStruct((ORDER, channels // 2), jnp.float32),
        ),
        grid_spec=pltpu.PrefetchScalarGridSpec(
            num_scalar_prefetch=2,
            grid=(blocks,),
            in_specs=[
                pl.BlockSpec((None, rows, WIDTH), lambda b, c, s: (1, 0, b)),
                pl.BlockSpec((None, rows, WIDTH), lambda b, c, s: (2, 0, b)),
                pl.BlockSpec(memory_space=pltpu.VMEM),
                pl.BlockSpec((3, SHORT, WIDTH), lambda b, c, s: (0, 0, b)),
                pl.BlockSpec((ORDER, WIDTH), lambda b, c, s: (0, b)),
            ],
            out_specs=(
                pl.BlockSpec(memory_space=pltpu.VMEM),
                pl.BlockSpec(memory_space=pltpu.VMEM),
                pl.BlockSpec((ORDER, WIDTH), lambda b, c, s: (0, first(b, s[2]))),
                pl.BlockSpec((ORDER, WIDTH), lambda b, c, s: (0, first(b, 1 - s[2]))),
            ),
            scratch_shapes=[pltpu.VMEM((spread_rows, LANES), jnp.float32)] * 2 + [table(), table(2 * SHORT)],
        ),
        name="gate",
        compiler_params=room(16),
        cost_estimate=cost(15 * 10**9, 4 * rows * channels),
    )(counter, place, planes, planes, edge, taps, mix)


def scan_specs(half, at):
    tail = half // 16 - 1
    return [
        pl.BlockSpec(memory_space=pltpu.VMEM),
        pl.BlockSpec((None, half, WIDTH), lambda b, s: (0, s[0], at + b)),
        pl.BlockSpec((None, 16, WIDTH), lambda b, s: (0, tail, at + b)),
        pl.BlockSpec(memory_space=pltpu.VMEM),
        pl.BlockSpec((3, SHORT, WIDTH), lambda b, s: (0, 0, at + b)),
        pl.BlockSpec((ORDER, WIDTH), lambda b, s: (0, at + b)),
        pl.BlockSpec((ORDER, WIDTH), lambda b, s: (0, at + b)),
        pl.BlockSpec((1, WIDTH), lambda b, s: (0, at + b)),
        pl.BlockSpec(memory_space=pltpu.VMEM),
    ]


def scan_scratch(step):
    return [pltpu.VMEM((BASE + SUBS * (step + GAP), LANES), jnp.float32), table(), table(), table(SHORT)]


def local(which, operands, tokens, piece, pieces, before):
    blocks, rows = operands[0].shape[:2]
    half = rows // 2
    step = half // SUBS
    shape = pltpu.VMEM((blocks, half, WIDTH), jnp.float32)
    blocks = blocks // pieces
    at = piece * blocks
    out = pl.BlockSpec(memory_space=pltpu.VMEM)
    return pl.pallas_call(
        lambda *refs: local_kernel(tokens, half, step, at, *refs),
        out_shape=(shape, shape),
        grid_spec=pltpu.PrefetchScalarGridSpec(
            num_scalar_prefetch=1,
            grid=(blocks,),
            in_specs=scan_specs(half, at) + [pl.BlockSpec(memory_space=pltpu.VMEM)] * len(before),
            out_specs=(out, out),
            scratch_shapes=scan_scratch(step),
        ),
        input_output_aliases={1 + len(operands) + k: k for k in range(len(before))},
        name="local",
        compiler_params=room(16),
        cost_estimate=cost(10**10 // pieces, half * blocks * WIDTH),
    )(which, *operands, *before)


def carry(which, parts, mix, residue, own, got, tokens):
    blocks, half = parts[0].shape[:2]
    channels = blocks * WIDTH
    step = half // SUBS
    block = pl.BlockSpec((half, WIDTH), lambda b, s: (0, b))
    mode = pl.BlockSpec((ORDER, WIDTH), lambda b, s: (0, b))
    return pl.pallas_call(
        lambda *refs: carry_kernel(tokens, half, step, *refs),
        out_shape=jax.ShapeDtypeStruct((half, channels), jnp.bfloat16),
        grid_spec=pltpu.PrefetchScalarGridSpec(
            num_scalar_prefetch=1,
            grid=(blocks,),
            in_specs=[pl.BlockSpec(memory_space=pltpu.VMEM)] * 2 + [mode, mode] + [pl.BlockSpec(memory_space=pltpu.VMEM)] * 2,
            out_specs=block,
            scratch_shapes=[table(), pltpu.VMEM((SUBS * (step + GAP), LANES), jnp.float32)],
        ),
        name="carry",
        compiler_params=room(16),
        cost_estimate=cost(5 * 10**9, half * channels),
    )(which, *parts, mix, residue, own, got)


def blend(which, operands, own, got, tokens):
    blocks, rows = operands[0].shape[:2]
    channels = blocks * WIDTH
    half = rows // 2
    step = half // SUBS
    return pl.pallas_call(
        lambda *refs: blend_kernel(tokens, half, step, *refs),
        out_shape=jax.ShapeDtypeStruct((half, channels), jnp.bfloat16),
        grid_spec=pltpu.PrefetchScalarGridSpec(
            num_scalar_prefetch=1,
            grid=(blocks,),
            in_specs=scan_specs(half, 0) + [pl.BlockSpec(memory_space=pltpu.VMEM)] * 2,
            out_specs=pl.BlockSpec((half, WIDTH), lambda b, s: (0, b)),
            scratch_shapes=scan_scratch(step) + [pltpu.VMEM((SUBS * (step + GAP), LANES), jnp.float32)],
        ),
        name="blend",
        compiler_params=room(16),
        cost_estimate=cost(9 * 10**9, 2 * half * channels),
    )(which, *operands, own, got)


def project(mixed, weight, first, cols, dtype):
    rows, depth = mixed.shape
    at = first // TILE_COLS
    return pl.pallas_call(
        project_kernel,
        out_shape=jax.ShapeDtypeStruct((rows, cols), dtype),
        grid=(cols // TILE_COLS,),
        in_specs=[
            pl.BlockSpec((rows, depth), lambda n: (0, 0)),
            pl.BlockSpec((depth, TILE_COLS), lambda n: (0, at + n)),
        ],
        out_specs=pl.BlockSpec((rows, TILE_COLS), lambda n: (0, n)),
        compiler_params=room(16),
        cost_estimate=cost(2 * rows * depth * cols, 2 * (rows * depth + depth * cols)),
    )(mixed, weight)


def combine(own, got, first, before):
    rows, cols = got.shape
    at = first // cols
    block = pl.BlockSpec((rows, cols), lambda n: (0, at))
    return pl.pallas_call(
        combine_kernel,
        out_shape=jax.ShapeDtypeStruct(own.shape, jnp.bfloat16),
        grid=(1,),
        in_specs=[block, pl.BlockSpec(memory_space=pltpu.VMEM)]
        + [pl.BlockSpec(memory_space=pl.ANY)] * len(before),
        out_specs=block,
        input_output_aliases={2: 0} if before else {},
        name="combine",
        compiler_params=room(8),
        cost_estimate=cost(rows * cols, 8 * rows * cols),
    )(own, got, *before)


def states_before(mine, other, mix, tokens, rows, index, count, between):
    core = index % 2
    width = mine.shape[1]
    rates = rates_of(lax.dynamic_slice_in_dim(mix, core * width, width, 1), tokens)
    decay = lambda chunks: jnp.exp(-rates * float(rows * chunks))
    steps = [decay(n) for n in (1, 2, 4)]
    assert count == 16

    def ring(value, pairs):
        return lax.ppermute(value, "ctx", pairs)

    sibling = ring(other, [(i, i ^ 1) for i in range(count)])
    early = jnp.where(core == 0, mine, sibling)
    late = jnp.where(core == 0, sibling, mine)
    chip = steps[0] * early + late
    beside = ring(chip, [(i, i ^ 2) for i in range(count)])
    between(0)
    between(1)
    upper = (index // 2) % 2 == 1
    group = jnp.where(upper, steps[1] * beside + chip, steps[1] * chip + beside)
    ring_at = index // 4
    odd = ring_at % 2 == 1
    near = ring(group, [(i, i ^ 4) for i in range(count)])
    between(2)
    couple = jnp.where(odd, steps[2] * near + group, steps[2] * group + near)
    far = ring(couple, [(i, (3 - i // 4) * 4 + i % 4) for i in range(count)])
    between(3)
    state = jnp.where(ring_at >= 2, jnp.where(odd, steps[2] * far, far), 0.0) + jnp.where(odd, near, 0.0)
    state = jnp.where(upper, steps[1] * state + beside, state)
    following = steps[0] * state + early
    own = jnp.where(core == 0, state, following)
    sent = jnp.where(core == 0, following, state)
    return own, ring(sent, [(i, i ^ 1) for i in range(count)])


def body(features, short_filter, mode_residue, decay_mix, skip_gain, counter, out_weight):
    rows = features.shape[0]
    channels = features.shape[2]
    count = lax.axis_size("ctx")
    tokens = rows * count
    index = lax.axis_index("ctx")
    side = lax.axis_index("ch")
    planes = jnp.transpose(features, (1, 0, 2))
    far_memory = lambda x: pltpu.with_memory_space_constraint(x, pltpu.HBM)
    edge = lax.ppermute(planes[:, rows - (SHORT - 1) :], "ctx", [(i, i + 1) for i in range(count - 1)])
    slot = jnp.arange(4, dtype=jnp.int32)

    def scalars(*values):
        out = jnp.zeros((4,), jnp.int32)
        for k, value in enumerate(values):
            out = jnp.where(slot == k, value, out)
        return out

    place = scalars(index * rows, side * channels, index % 2)
    to_send = scalars(1 - side, index % 2)
    to_keep = scalars(side, index % 2)
    planes, taps, mix, residue, skip = map(far_memory, (planes, short_filter, decay_mix, mode_residue, skip_gain[None]))
    gated, start, mine, other = gate(counter, place, planes, edge, taps, mix, tokens)
    operands = (gated, planes, planes, edge, taps, mix, residue, skip, start)
    parts = [()]

    def between(piece):
        parts[0] = local(to_send, operands, tokens, piece, 4, parts[0])

    own, got = states_before(mine, other, decay_mix, tokens, rows, index, count, between)
    sent = carry(to_send, parts[0], mix, residue, own, got, tokens)
    outs = out_weight.shape[1]
    received = []
    for first in range(0, outs, SEND_COLS):
        part = project(sent, out_weight, first, SEND_COLS, jnp.bfloat16)
        received.append(lax.ppermute(part, "ch", [(0, 1), (1, 0)]))
    own, part = lax.optimization_barrier((own, part))
    kept = blend(to_keep, operands, own, got, tokens)
    total = project(kept, out_weight, 0, outs, jnp.float32)
    done = ()
    for k, first in enumerate(range(0, outs, SEND_COLS)):
        done = (combine(total, received[k], first, done),)
    return done[0]


def solution(mesh):
    placed = (
        P(("dp", "ctx"), None, "ch"),
        P(None, None, "ch"),
        P(None, "ch"),
        P(None, "ch"),
        P("ch"),
        P("dp"),
        P("ch", None),
    )

    return jax.shard_map(body, mesh=mesh, in_specs=placed, out_specs=P(("dp", "ctx", "ch"), None), check_vma=False)
```

time: 132 us -> 112 us (0.85)
  matrix products: 30 us -> 0 us
  Pallas kernels: 47.1 us -> 70.1 us
  waiting for transfers between devices: 27.1 us -> 15 us
  starting transfers between devices: 15.8 us -> 23.8 us
  other arithmetic: 6.07 us -> 0.25 us
  local copies, waits for them, and re-layouts: 4.51 us -> 1.62 us
    dot_general x8 -> x0, matrix products: 30 us -> none  [the longest x4 15.7 us: body(): jnp.dot(sent, out_weight[:, c * cols:(c + 1) * cols], preferred_element_t...]
    pallas_call x3 -> x24, Pallas kernels: 47.1 us -> 70.1 us  [the longest x9 19.9 us: project(): pl.pallas_call(project_kernel, out_shape=jax.ShapeDtypeStruct((rows, cols...]
    ppermute x8 -> x13, waiting for transfers between devices: 27.1 us -> 14.3 us  [the longest x8 13.4 us: body(): received.append(lax.ppermute(part, 'ch', [(0, 1), (1, 0)]))]
    ppermute x8 -> x13, starting transfers between devices: 14.5 us -> 22.5 us  [the longest x5 13.1 us: ring(): return lax.ppermute(value, 'ctx', pairs)]
    slice x3 -> x0, local copies, waits for them, and re-layouts: 2 us -> none  [the longest x1 1.38 us: body(): counter[0]]
    another operation x2 -> x0, other arithmetic: 1.89 us -> none  [the longest x1 1.27 us: body(): jnp.stack([counter[0], counter[1] + index * rows, side * channels])]
    reshape x1 -> x0, local copies, waits for them, and re-layouts: 1.58 us -> none  [body(): taps = short_filter.reshape(9, channels)]
    concatenate x1 -> x0, other arithmetic: 1.49 us -> none  [body(): return jnp.concatenate(outs, axis=1)]
  transfers between devices with their start and end apart: 9 -> 14, of which waited for: 5 -> 6; matrix products, arithmetic and copies ran while one was open for 18% -> 0% of each run, Pallas kernels for 9% -> 38%
where the time goes in v2:
time: 112 us; the launch traced here: 111 us
  Pallas kernels  70.1 us (63%)
  starting transfers between devices  23.8 us (21%)
  waiting for transfers between devices  15 us (13%)
  local copies, waits for them, and re-layouts  1.62 us (1%)
    pallas_call x9, Pallas kernels, project(): pl.pallas_call(project_kernel, out_shape=jax.ShapeDtypeStruct((rows, cols...  19.9 us
    pallas_call x1, Pallas kernels, gate(): pl.pallas_call(lambda *refs: gate_kernel(tokens, half, step, *refs), out_...  14.3 us
    pallas_call x4, Pallas kernels, local(): pl.pallas_call(lambda *refs: local_kernel(tokens, half, step, at, *refs),...  13.9 us
    ppermute x8, waiting for transfers between devices, body(): received.append(lax.ppermute(part, 'ch', [(0, 1), (1, 0)]))  13.4 us
    ppermute x5, starting transfers between devices, ring(): return lax.ppermute(value, 'ctx', pairs)  13.1 us
    pallas_call x1, Pallas kernels, blend(): pl.pallas_call(lambda *refs: blend_kernel(tokens, half, step, *refs), out...  9.51 us
    ppermute x8, starting transfers between devices, body(): received.append(lax.ppermute(part, 'ch', [(0, 1), (1, 0)]))  9.41 us
    pallas_call x1, Pallas kernels, carry(): pl.pallas_call(lambda *refs: carry_kernel(tokens, half, step, *refs), out...  6.48 us
  transfers between devices with their start and end apart: 14, of which 6 were waited for; matrix products, arithmetic and copies ran while one was open for 0% of the time, Pallas kernels for 38%

profile of v2, /device:TPU:0, one launch (start us, length us, event | category | flops | bytes accessed | tf_op | source)
XLA Modules:
  0.0 111.2 jit_solution(17466448324869998223)
XLA Ops:
  0.0 0.9 slice.4
  0.9 1.3 %collective-permute-start = (bf16[3,2,2048]{2,1,0:T(2,128)(2,1)S(1)}, bf16[3,2,2048]{2,1,0:T(2,128)(2,1)S(1)}, u32[]{:S(2)}, u32[]{:S(2)}) collective-permute-start(bf16[3,2,2048]{2,1,0:T(2,128)(2,1)S(1)} %slice.4), channel_id=1, source_target_pairs={{0,8},{8,16},{16,24},{24,32},{32,40},{40,48},{48,56},{56,64},{64,7... | collective-permute-start | bytes 73736 | tf_op jit(solution)/shard_map/ppermute | solution.py:500
  3.7 14.3 %gate.1 = (bf16[8,512,256]{2,1,0:T(8,128)(2,1)S(1)}, f32[2,8,16,8,256]{4,3,2,1,0:T(8,128)S(1)}, f32[16,1024]{1,0:T(8,128)S(1)}, f32[16,1024]{1,0:T(8,128)S(1)}) custom-call(s32[2]{0:T(128)S(1)} %copy-done, s32[4]{0:T(128)S(1)} %compare_select_fusion.refs_1_, bf16[3,512,2048]{2,1,0:T(8,128)(2,1)} %bitcast.5, bf16[3,512,2048]{2,1,0:T(8,128)(2,1)} %bitcast.6, ...), custom_call_target="tpu_custom_call" | custom-call | flops 15000000512 | bytes 4194304 | tf_op jit(solution)/shard_map/gate/pallas_call | solution.py:302
  18.0 4.9 %collective-permute-start.1 = (f32[16,1024]{1,0:T(8,128)S(1)}, f32[16,1024]{1,0:T(8,128)S(1)}, u32[]{:S(2)}, u32[]{:S(2)}) collective-permute-start(f32[16,1024]{1,0:T(8,128)S(1)} %get-tuple-element.21), channel_id=1, source_target_pairs={{0,8},{8,0},{16,24},{24,16},{32,40},{40,32},{48,56},{56,48},{64,72... | collective-permute-start | bytes 196616 | tf_op jit(solution)/shard_map/ppermute | solution.py:465
  23.9 4.1 %collective-permute-start.2 = (f32[16,1024]{1,0:T(8,128)S(1)}, f32[16,1024]{1,0:T(8,128)S(1)}, u32[]{:S(2)}, u32[]{:S(2)}) collective-permute-start(f32[16,1024]{1,0:T(8,128)S(1)} %select_add_fusion), channel_id=1, source_target_pairs={{0,16},{8,24},{16,0},{24,8},{32,48},{40,56},{48,32},{56,40},{64,80... | collective-permute-start | bytes 196616 | tf_op jit(solution)/shard_map/ppermute | solution.py:465
  28.0 3.4 %local.4 = (f32[8,256,256]{2,1,0:T(8,128)S(1)}, f32[8,256,256]{2,1,0:T(8,128)S(1)}) custom-call(s32[4]{0:T(128)S(1)} %select_select_fusion.refs_0_, bf16[8,512,256]{2,1,0:T(8,128)(2,1)S(1)} %get-tuple-element.18.refs_1_, bf16[3,512,2048]{2,1,0:T(8,128)(2,1)} %bitcast.7, bf16[3,512,2048]{2,1,0:T(8,128)(2,1)} %bitcast.8, ...), custom_call_target="tpu_custom_call" | custom-call | flops 2500000000 | bytes 131072 | tf_op jit(solution)/shard_map/local/pallas_call | solution.py:361
  31.5 1.7 %collective-permute-start.3 = (f32[16,1024]{1,0:T(8,128)S(1)}, f32[16,1024]{1,0:T(8,128)S(1)}, u32[]{:S(2)}, u32[]{:S(2)}) collective-permute-start(f32[16,1024]{1,0:T(8,128)S(1)} %add_select_fusion.2), channel_id=1, source_target_pairs={{0,32},{8,40},{16,48},{24,56},{32,0},{40,8},{48,16},{56,24},{64,96... | collective-permute-start | bytes 196616 | tf_op jit(solution)/shard_map/ppermute | solution.py:465
  33.2 3.4 %local.5 = (f32[8,256,256]{2,1,0:T(8,128)S(1)}, f32[8,256,256]{2,1,0:T(8,128)S(1)}) custom-call(s32[4]{0:T(128)S(1)} %select_select_fusion.refs_0_, bf16[8,512,256]{2,1,0:T(8,128)(2,1)S(1)} %get-tuple-element.18.refs_1_, bf16[3,512,2048]{2,1,0:T(8,128)(2,1)} %bitcast.9, ...), custom_call_target="tpu_custom_call", output_to_operand_aliasing={{0}: (10, {}), {1}: (11, {})} | custom-call | flops 2500000000 | bytes 131072 | tf_op jit(solution)/shard_map/local/pallas_call | solution.py:361
  36.7 2.3 %collective-permute-start.4 = (f32[16,1024]{1,0:T(8,128)S(1)}, f32[16,1024]{1,0:T(8,128)S(1)}, u32[]{:S(2)}, u32[]{:S(2)}) collective-permute-start(f32[16,1024]{1,0:T(8,128)S(1)} %add_select_fusion.1), channel_id=1, source_target_pairs={{0,96},{8,104},{16,112},{24,120},{32,64},{40,72},{48,80},{56,88},{... | collective-permute-start | bytes 196616 | tf_op jit(solution)/shard_map/ppermute | solution.py:465
  39.0 3.4 %local.6 = (f32[8,256,256]{2,1,0:T(8,128)S(1)}, f32[8,256,256]{2,1,0:T(8,128)S(1)}) custom-call(s32[4]{0:T(128)S(1)} %select_select_fusion.refs_0_, bf16[8,512,256]{2,1,0:T(8,128)(2,1)S(1)} %get-tuple-element.18.refs_1_, bf16[3,512,2048]{2,1,0:T(8,128)(2,1)} %bitcast.11, ...), custom_call_target="tpu_custom_call", output_to_operand_aliasing={{0}: (10, {}), {1}: (11, {})} | custom-call | flops 2500000000 | bytes 131072 | tf_op jit(solution)/shard_map/local/pallas_call | solution.py:361
  42.6 3.7 %local.7 = (f32[8,256,256]{2,1,0:T(8,128)S(1)}, f32[8,256,256]{2,1,0:T(8,128)S(1)}) custom-call(s32[4]{0:T(128)S(1)} %select_select_fusion.refs_0_, bf16[8,512,256]{2,1,0:T(8,128)(2,1)S(1)} %get-tuple-element.18.refs_1_, bf16[3,512,2048]{2,1,0:T(8,128)(2,1)} %bitcast.13, ...), custom_call_target="tpu_custom_call", output_to_operand_aliasing={{0}: (10, {}), {1}: (11, {})} | custom-call | flops 2500000000 | bytes 131072 | tf_op jit(solution)/shard_map/local/pallas_call | solution.py:361
  46.4 6.5 %carry.1.mixed_ref = bf16[256,2048]{1,0:T(8,128)(2,1)S(1)} custom-call(s32[4]{0:T(128)S(1)} %select_select_fusion.refs_0_, f32[8,256,256]{2,1,0:T(8,128)S(1)} %get-tuple-element.28.refs_1_, f32[8,256,256]{2,1,0:T(8,128)S(1)} %get-tuple-element.29.refs_2_, f32[16,2048]{1,0:T(8,128)} %refs_6_.11, f32[16,2048]{1,0:T(8,128)} %refs_7_.9, ...), custom_call_target="tpu_custom_call" | custom-call | flops 5000000000 | bytes 524288 | tf_op jit(solution)/shard_map/carry/pallas_call | solution.py:384
  52.9 1.3 %shard_map.73 = bf16[256,512]{1,0:T(8,128)(2,1)S(1)} custom-call(bf16[256,2048]{1,0:T(8,128)(2,1)S(1)} %carry.1.mixed_ref, bf16[2048,4096]{1,0:T(8,128)(2,1)S(1)} %bitcast.3), custom_call_target="tpu_custom_call" | custom-call | flops 536870912 | bytes 3145728 | tf_op jit(solution)/shard_map/pallas_call | solution.py:424
  54.2 1.3 %shard_map.81 = bf16[256,512]{1,0:T(8,128)(2,1)S(1)} custom-call(bf16[256,2048]{1,0:T(8,128)(2,1)S(1)} %carry.1.mixed_ref, bf16[2048,4096]{1,0:T(8,128)(2,1)S(1)} %bitcast.3), custom_call_target="tpu_custom_call" | custom-call | flops 536870912 | bytes 3145728 | tf_op jit(solution)/shard_map/pallas_call | solution.py:424
  55.5 1.3 %shard_map.80 = bf16[256,512]{1,0:T(8,128)(2,1)S(1)} custom-call(bf16[256,2048]{1,0:T(8,128)(2,1)S(1)} %carry.1.mixed_ref, bf16[2048,4096]{1,0:T(8,128)(2,1)S(1)} %bitcast.3), custom_call_target="tpu_custom_call" | custom-call | flops 536870912 | bytes 3145728 | tf_op jit(solution)/shard_map/pallas_call | solution.py:424
  56.7 1.3 %shard_map.79 = bf16[256,512]{1,0:T(8,128)(2,1)S(1)} custom-call(bf16[256,2048]{1,0:T(8,128)(2,1)S(1)} %carry.1.mixed_ref, bf16[2048,4096]{1,0:T(8,128)(2,1)S(1)} %bitcast.3), custom_call_target="tpu_custom_call" | custom-call | flops 536870912 | bytes 3145728 | tf_op jit(solution)/shard_map/pallas_call | solution.py:424
  58.0 1.3 %shard_map.75 = bf16[256,512]{1,0:T(8,128)(2,1)S(1)} custom-call(bf16[256,2048]{1,0:T(8,128)(2,1)S(1)} %carry.1.mixed_ref, bf16[2048,4096]{1,0:T(8,128)(2,1)S(1)} %bitcast.3), custom_call_target="tpu_custom_call" | custom-call | flops 536870912 | bytes 3145728 | tf_op jit(solution)/shard_map/pallas_call | solution.py:424
  59.3 1.4 %collective-permute-start.6 = (bf16[256,512]{1,0:T(8,128)(2,1)S(1)}, bf16[256,512]{1,0:T(8,128)(2,1)S(1)}, u32[]{:S(2)}, u32[]{:S(2)}) collective-permute-start(bf16[256,512]{1,0:T(8,128)(2,1)S(1)} %shard_map.73), channel_id=1, source_target_pairs={{0,4},{4,0},{1,5},{5,1},{2,6},{6,2},{3,7},{7,3},{8,12},{12,8},{9,1... | collective-permute-start | bytes 786440 | tf_op jit(solution)/shard_map/ppermute | solution.py:526
  61.4 1.3 %collective-permute-start.11 = (bf16[256,512]{1,0:T(8,128)(2,1)S(1)}, bf16[256,512]{1,0:T(8,128)(2,1)S(1)}, u32[]{:S(2)}, u32[]{:S(2)}) collective-permute-start(bf16[256,512]{1,0:T(8,128)(2,1)S(1)} %shard_map.79), channel_id=1, source_target_pairs={{0,4},{4,0},{1,5},{5,1},{2,6},{6,2},{3,7},{7,3},{8,12},{12,8},{9,1... | collective-permute-start | bytes 786440 | tf_op jit(solution)/shard_map/ppermute | solution.py:526
  63.4 1.3 %collective-permute-start.13 = (bf16[256,512]{1,0:T(8,128)(2,1)S(1)}, bf16[256,512]{1,0:T(8,128)(2,1)S(1)}, u32[]{:S(2)}, u32[]{:S(2)}) collective-permute-start(bf16[256,512]{1,0:T(8,128)(2,1)S(1)} %shard_map.81), channel_id=1, source_target_pairs={{0,4},{4,0},{1,5},{5,1},{2,6},{6,2},{3,7},{7,3},{8,12},{12,8},{9,1... | collective-permute-start | bytes 786440 | tf_op jit(solution)/shard_map/ppermute | solution.py:526
  64.7 9.5 %blend.1.mixed_ref = bf16[256,2048]{1,0:T(8,128)(2,1)S(1)} custom-call(s32[4]{0:T(128)S(1)} %select_select_fusion.1.refs_0_, bf16[8,512,256]{2,1,0:T(8,128)(2,1)S(1)} %get-tuple-element.18.refs_1_, bf16[3,512,2048]{2,1,0:T(8,128)(2,1)} %bitcast.15, bf16[3,512,2048]{2,1,0:T(8,128)(2,1)} %bitcast.16, bf16[3,2,2048]{2,1,0:T(2,128)(2,1)S(1)} %collective-permute-done.refs_4_, ...), custom_call_target="tpu_custom_call" | custom-call | flops 8999999488 | bytes 1048576 | tf_op jit(solution)/shard_map/blend/pallas_call | solution.py:405
  74.2 1.3 %shard_map.78 = bf16[256,512]{1,0:T(8,128)(2,1)S(1)} custom-call(bf16[256,2048]{1,0:T(8,128)(2,1)S(1)} %carry.1.mixed_ref, bf16[2048,4096]{1,0:T(8,128)(2,1)S(1)} %bitcast.3), custom_call_target="tpu_custom_call" | custom-call | flops 536870912 | bytes 3145728 | tf_op jit(solution)/shard_map/pallas_call | solution.py:424
  75.5 1.3 %shard_map.77 = bf16[256,512]{1,0:T(8,128)(2,1)S(1)} custom-call(bf16[256,2048]{1,0:T(8,128)(2,1)S(1)} %carry.1.mixed_ref, bf16[2048,4096]{1,0:T(8,128)(2,1)S(1)} %bitcast.3), custom_call_target="tpu_custom_call" | custom-call | flops 536870912 | bytes 3145728 | tf_op jit(solution)/shard_map/pallas_call | solution.py:424
  76.8 1.3 %shard_map.76 = bf16[256,512]{1,0:T(8,128)(2,1)S(1)} custom-call(bf16[256,2048]{1,0:T(8,128)(2,1)S(1)} %carry.1.mixed_ref, bf16[2048,4096]{1,0:T(8,128)(2,1)S(1)} %bitcast.3), custom_call_target="tpu_custom_call" | custom-call | flops 536870912 | bytes 3145728 | tf_op jit(solution)/shard_map/pallas_call | solution.py:424
  78.1 1.7 %collective-permute-done.11.got_ref = bf16[256,512]{1,0:T(8,128)(2,1)S(1)} collective-permute-done((bf16[256,512]{1,0:T(8,128)(2,1)S(1)}, bf16[256,512]{1,0:T(8,128)(2,1)S(1)}, u32[]{:S(2)}, u32[]{:S(2)}) %collective-permute-start.11) | collective-permute-done | bytes 262176 | tf_op jit(solution)/shard_map/ppermute | solution.py:526
  79.8 1.3 %collective-permute-start.8 = (bf16[256,512]{1,0:T(8,128)(2,1)S(1)}, bf16[256,512]{1,0:T(8,128)(2,1)S(1)}, u32[]{:S(2)}, u32[]{:S(2)}) collective-permute-start(bf16[256,512]{1,0:T(8,128)(2,1)S(1)} %shard_map.76), channel_id=1, source_target_pairs={{0,4},{4,0},{1,5},{5,1},{2,6},{6,2},{3,7},{7,3},{8,12},{12,8},{9,1... | collective-permute-start | bytes 786440 | tf_op jit(solution)/shard_map/ppermute | solution.py:526
  81.1 4.3 %collective-permute-done.12.got_ref = bf16[256,512]{1,0:T(8,128)(2,1)S(1)} collective-permute-done((bf16[256,512]{1,0:T(8,128)(2,1)S(1)}, bf16[256,512]{1,0:T(8,128)(2,1)S(1)}, u32[]{:S(2)}, u32[]{:S(2)}) %collective-permute-start.12) | collective-permute-done | bytes 262176 | tf_op jit(solution)/shard_map/ppermute | solution.py:526
  85.4 1.3 %collective-permute-start.9 = (bf16[256,512]{1,0:T(8,128)(2,1)S(1)}, bf16[256,512]{1,0:T(8,128)(2,1)S(1)}, u32[]{:S(2)}, u32[]{:S(2)}) collective-permute-start(bf16[256,512]{1,0:T(8,128)(2,1)S(1)} %shard_map.77), channel_id=1, source_target_pairs={{0,4},{4,0},{1,5},{5,1},{2,6},{6,2},{3,7},{7,3},{8,12},{12,8},{9,1... | collective-permute-start | bytes 786440 | tf_op jit(solution)/shard_map/ppermute | solution.py:526
  86.7 4.3 %collective-permute-done.13.got_ref = bf16[256,512]{1,0:T(8,128)(2,1)S(1)} collective-permute-done((bf16[256,512]{1,0:T(8,128)(2,1)S(1)}, bf16[256,512]{1,0:T(8,128)(2,1)S(1)}, u32[]{:S(2)}, u32[]{:S(2)}) %collective-permute-start.13) | collective-permute-done | bytes 262176 | tf_op jit(solution)/shard_map/ppermute | solution.py:526
  91.0 1.3 %collective-permute-start.10 = (bf16[256,512]{1,0:T(8,128)(2,1)S(1)}, bf16[256,512]{1,0:T(8,128)(2,1)S(1)}, u32[]{:S(2)}, u32[]{:S(2)}) collective-permute-start(bf16[256,512]{1,0:T(8,128)(2,1)S(1)} %shard_map.78), channel_id=1, source_target_pairs={{0,4},{4,0},{1,5},{5,1},{2,6},{6,2},{3,7},{7,3},{8,12},{12,8},{9,1... | collective-permute-start | bytes 786440 | tf_op jit(solution)/shard_map/ppermute | solution.py:526
  92.3 9.8 %shard_map.74.own_ref = f32[256,4096]{1,0:T(8,128)S(1)} custom-call(bf16[256,2048]{1,0:T(8,128)(2,1)S(1)} %blend.1.mixed_ref, bf16[2048,4096]{1,0:T(8,128)(2,1)S(1)} %bitcast.3), custom_call_target="tpu_custom_call" | custom-call | flops 4294967296 | bytes 17825792 | tf_op jit(solution)/shard_map/pallas_call | solution.py:424
  104.3 3.1 %collective-permute-done.10.got_ref = bf16[256,512]{1,0:T(8,128)(2,1)S(1)} collective-permute-done((bf16[256,512]{1,0:T(8,128)(2,1)S(1)}, bf16[256,512]{1,0:T(8,128)(2,1)S(1)}, u32[]{:S(2)}, u32[]{:S(2)}) %collective-permute-start.10) | collective-permute-done | bytes 262176 | tf_op jit(solution)/shard_map/ppermute | solution.py:526
  (47 shorter events, 10.1 us)
Async XLA Ops:
  0.9 2.1 %collective-permute-start = (bf16[3,2,2048]{2,1,0:T(2,128)(2,1)S(1)}, bf16[3,2,2048]{2,1,0:T(2,128)(2,1)S(1)}, u32[]{:S(2)}, u32[]{:S(2)}) collective-permute-start(bf16[3,2,2048]{2,1,0:T(2,128)(2,1)S(1)} %slice.4), channel_id=1, source_target_pairs={{0,8},{8,16},{16,24},{24,32},{32,40},{40,48},{48,56},{56,64},{64,7... | collective-permute-start | bytes 73736 | tf_op jit(solution)/shard_map/ppermute | solution.py:500
  3.1 0.7 copy-start
  3.7 20.1 %copy-start.1 = (f32[16,2048]{1,0:T(8,128)S(1)}, f32[16,2048]{1,0:T(8,128)}, u32[]{:S(2)}) copy-start(f32[16,2048]{1,0:T(8,128)} %refs_6_.11) | copy-start | bytes 393220
  18.0 5.8 %collective-permute-start.1 = (f32[16,1024]{1,0:T(8,128)S(1)}, f32[16,1024]{1,0:T(8,128)S(1)}, u32[]{:S(2)}, u32[]{:S(2)}) collective-permute-start(f32[16,1024]{1,0:T(8,128)S(1)} %get-tuple-element.21), channel_id=1, source_target_pairs={{0,8},{8,0},{16,24},{24,16},{32,40},{40,32},{48,56},{56,48},{64,72... | collective-permute-start | bytes 196616 | tf_op jit(solution)/shard_map/ppermute | solution.py:465
  23.9 7.6 %collective-permute-start.2 = (f32[16,1024]{1,0:T(8,128)S(1)}, f32[16,1024]{1,0:T(8,128)S(1)}, u32[]{:S(2)}, u32[]{:S(2)}) collective-permute-start(f32[16,1024]{1,0:T(8,128)S(1)} %select_add_fusion), channel_id=1, source_target_pairs={{0,16},{8,24},{16,0},{24,8},{32,48},{40,56},{48,32},{56,40},{64,80... | collective-permute-start | bytes 196616 | tf_op jit(solution)/shard_map/ppermute | solution.py:465
  28.0 3.4 %copy-start.2 = (f32[16,2048]{1,0:T(8,128)S(1)}, f32[16,2048]{1,0:T(8,128)}, u32[]{:S(2)}) copy-start(f32[16,2048]{1,0:T(8,128)} %refs_6_.11) | copy-start | bytes 393220
  31.5 5.1 %collective-permute-start.3 = (f32[16,1024]{1,0:T(8,128)S(1)}, f32[16,1024]{1,0:T(8,128)S(1)}, u32[]{:S(2)}, u32[]{:S(2)}) collective-permute-start(f32[16,1024]{1,0:T(8,128)S(1)} %add_select_fusion.2), channel_id=1, source_target_pairs={{0,32},{8,40},{16,48},{24,56},{32,0},{40,8},{48,16},{56,24},{64,96... | collective-permute-start | bytes 196616 | tf_op jit(solution)/shard_map/ppermute | solution.py:465
  33.2 3.4 %copy-start.3 = (f32[16,2048]{1,0:T(8,128)S(1)}, f32[16,2048]{1,0:T(8,128)}, u32[]{:S(2)}) copy-start(f32[16,2048]{1,0:T(8,128)} %refs_6_.11) | copy-start | bytes 393220
  36.7 5.8 %collective-permute-start.4 = (f32[16,1024]{1,0:T(8,128)S(1)}, f32[16,1024]{1,0:T(8,128)S(1)}, u32[]{:S(2)}, u32[]{:S(2)}) collective-permute-start(f32[16,1024]{1,0:T(8,128)S(1)} %add_select_fusion.1), channel_id=1, source_target_pairs={{0,96},{8,104},{16,112},{24,120},{32,64},{40,72},{48,80},{56,88},{... | collective-permute-start | bytes 196616 | tf_op jit(solution)/shard_map/ppermute | solution.py:465
  39.0 3.4 %copy-start.4 = (f32[16,2048]{1,0:T(8,128)S(1)}, f32[16,2048]{1,0:T(8,128)}, u32[]{:S(2)}) copy-start(f32[16,2048]{1,0:T(8,128)} %refs_6_.11) | copy-start | bytes 393220
  42.5 3.9 %collective-permute-start.5 = (f32[16,1024]{1,0:T(8,128)S(1)}, f32[16,1024]{1,0:T(8,128)S(1)}, u32[]{:S(2)}, u32[]{:S(2)}) collective-permute-start(f32[16,1024]{1,0:T(8,128)S(1)} %get-tuple-element.31), channel_id=1, source_target_pairs={{0,8},{8,0},{16,24},{24,16},{32,40},{40,32},{48,56},{56,48},{64,72... | collective-permute-start | bytes 196616 | tf_op jit(solution)/shard_map/ppermute | solution.py:465
  42.6 10.3 %slice-start = ((s8[16777216]{0:T(1024)(128)(4,1)}), s8[4194304]{0:T(1024)(128)(4,1)S(1)}, s32[]{:S(2)}) async-start(s8[16777216]{0:T(1024)(128)(4,1)} %bitcast.2), calls=%async_computation | async-start | bytes 8388608
  42.6 10.3 %slice-start.1 = ((s8[16777216]{0:T(1024)(128)(4,1)}), s8[4194304]{0:T(1024)(128)(4,1)S(1)}, s32[]{:S(2)}) async-start(s8[16777216]{0:T(1024)(128)(4,1)} %bitcast.2), calls=%async_computation.1 | async-start | bytes 8388608
  42.6 10.3 %slice-start.2 = ((s8[16777216]{0:T(1024)(128)(4,1)}), s8[4194304]{0:T(1024)(128)(4,1)S(1)}, s32[]{:S(2)}) async-start(s8[16777216]{0:T(1024)(128)(4,1)} %bitcast.2), calls=%async_computation.2 | async-start | bytes 8388608
  46.4 6.5 %slice-start.3 = ((s8[16777216]{0:T(1024)(128)(4,1)}), s8[4194304]{0:T(1024)(128)(4,1)S(1)}, s32[]{:S(2)}) async-start(s8[16777216]{0:T(1024)(128)(4,1)} %bitcast.2), calls=%async_computation.3 | async-start | bytes 8388608
  59.3 51.1 %collective-permute-start.6 = (bf16[256,512]{1,0:T(8,128)(2,1)S(1)}, bf16[256,512]{1,0:T(8,128)(2,1)S(1)}, u32[]{:S(2)}, u32[]{:S(2)}) collective-permute-start(bf16[256,512]{1,0:T(8,128)(2,1)S(1)} %shard_map.73), channel_id=1, source_target_pairs={{0,4},{4,0},{1,5},{5,1},{2,6},{6,2},{3,7},{7,3},{8,12},{12,8},{9,1... | collective-permute-start | bytes 786440 | tf_op jit(solution)/shard_map/ppermute | solution.py:526
  60.7 49.0 %collective-permute-start.7 = (bf16[256,512]{1,0:T(8,128)(2,1)S(1)}, bf16[256,512]{1,0:T(8,128)(2,1)S(1)}, u32[]{:S(2)}, u32[]{:S(2)}) collective-permute-start(bf16[256,512]{1,0:T(8,128)(2,1)S(1)} %shard_map.75), channel_id=1, source_target_pairs={{0,4},{4,0},{1,5},{5,1},{2,6},{6,2},{3,7},{7,3},{8,12},{12,8},{9,1... | collective-permute-start | bytes 786440 | tf_op jit(solution)/shard_map/ppermute | solution.py:526
  61.4 18.4 %collective-permute-start.11 = (bf16[256,512]{1,0:T(8,128)(2,1)S(1)}, bf16[256,512]{1,0:T(8,128)(2,1)S(1)}, u32[]{:S(2)}, u32[]{:S(2)}) collective-permute-start(bf16[256,512]{1,0:T(8,128)(2,1)S(1)} %shard_map.79), channel_id=1, source_target_pairs={{0,4},{4,0},{1,5},{5,1},{2,6},{6,2},{3,7},{7,3},{8,12},{12,8},{9,1... | collective-permute-start | bytes 786440 | tf_op jit(solution)/shard_map/ppermute | solution.py:526
  62.7 22.7 %collective-permute-start.12 = (bf16[256,512]{1,0:T(8,128)(2,1)S(1)}, bf16[256,512]{1,0:T(8,128)(2,1)S(1)}, u32[]{:S(2)}, u32[]{:S(2)}) collective-permute-start(bf16[256,512]{1,0:T(8,128)(2,1)S(1)} %shard_map.80), channel_id=1, source_target_pairs={{0,4},{4,0},{1,5},{5,1},{2,6},{6,2},{3,7},{7,3},{8,12},{12,8},{9,1... | collective-permute-start | bytes 786440 | tf_op jit(solution)/shard_map/ppermute | solution.py:526
  63.4 27.6 %collective-permute-start.13 = (bf16[256,512]{1,0:T(8,128)(2,1)S(1)}, bf16[256,512]{1,0:T(8,128)(2,1)S(1)}, u32[]{:S(2)}, u32[]{:S(2)}) collective-permute-start(bf16[256,512]{1,0:T(8,128)(2,1)S(1)} %shard_map.81), channel_id=1, source_target_pairs={{0,4},{4,0},{1,5},{5,1},{2,6},{6,2},{3,7},{7,3},{8,12},{12,8},{9,1... | collective-permute-start | bytes 786440 | tf_op jit(solution)/shard_map/ppermute | solution.py:526
  79.8 29.1 %collective-permute-start.8 = (bf16[256,512]{1,0:T(8,128)(2,1)S(1)}, bf16[256,512]{1,0:T(8,128)(2,1)S(1)}, u32[]{:S(2)}, u32[]{:S(2)}) collective-permute-start(bf16[256,512]{1,0:T(8,128)(2,1)S(1)} %shard_map.76), channel_id=1, source_target_pairs={{0,4},{4,0},{1,5},{5,1},{2,6},{6,2},{3,7},{7,3},{8,12},{12,8},{9,1... | collective-permute-start | bytes 786440 | tf_op jit(solution)/shard_map/ppermute | solution.py:526
  85.4 22.8 %collective-permute-start.9 = (bf16[256,512]{1,0:T(8,128)(2,1)S(1)}, bf16[256,512]{1,0:T(8,128)(2,1)S(1)}, u32[]{:S(2)}, u32[]{:S(2)}) collective-permute-start(bf16[256,512]{1,0:T(8,128)(2,1)S(1)} %shard_map.77), channel_id=1, source_target_pairs={{0,4},{4,0},{1,5},{5,1},{2,6},{6,2},{3,7},{7,3},{8,12},{12,8},{9,1... | collective-permute-start | bytes 786440 | tf_op jit(solution)/shard_map/ppermute | solution.py:526
  91.0 16.4 %collective-permute-start.10 = (bf16[256,512]{1,0:T(8,128)(2,1)S(1)}, bf16[256,512]{1,0:T(8,128)(2,1)S(1)}, u32[]{:S(2)}, u32[]{:S(2)}) collective-permute-start(bf16[256,512]{1,0:T(8,128)(2,1)S(1)} %shard_map.78), channel_id=1, source_target_pairs={{0,4},{4,0},{1,5},{5,1},{2,6},{6,2},{3,7},{7,3},{8,12},{12,8},{9,1... | collective-permute-start | bytes 786440 | tf_op jit(solution)/shard_map/ppermute | solution.py:526

commit v3 on v2

v3 whole, which is shorter than its diff:
```python
import math

import jax
import jax.numpy as jnp
from jax import lax
from jax.experimental import pallas as pl
from jax.experimental.pallas import tpu as pltpu
from jax.sharding import PartitionSpec as P


SHORT = 3
ORDER = 16
LANES = 128
SUBS = 8
WIDTH = 2 * LANES
KEEP_SCALE = 8.0 / 7.0
TILE_COLS = 256
BASE = 40
GAP = 4
QUAD = 4
GATE_STEPS = 8


def rates_of(mix, length):
    return jnp.exp(-((1.0 - mix) * math.log(length) + mix * math.log(30.0)))


def row(table, index):
    return jnp.broadcast_to(table[index : index + 1, :], (SUBS, table.shape[1]))


def spread(rows, source, first, cols, count, step):
    for n in range(count):
        at = BASE + n * (step + GAP)
        spot = pl.ds(pl.multiple_of(first + n * step, step), step)
        rows[at : at + step, :] = source[spot, cols].astype(jnp.float32)


def across(rows, at, step):
    return rows[pl.ds(at, SUBS, stride=step + GAP), :]


def chunks_of(outs):
    sizes = [TILE_COLS] + [2 * TILE_COLS] * ((outs - TILE_COLS) // (2 * TILE_COLS))
    sizes += [TILE_COLS] * ((outs - sum(sizes)) // TILE_COLS)
    return [(sum(sizes[:k]), size) for k, size in enumerate(sizes)]


def lanes_of(group):
    return pl.ds(pl.multiple_of(group * LANES, LANES), LANES)


def state_of(own_ref, got_ref, core, group, groups):
    lanes = lanes_of(group % (groups // 2))
    return jnp.where(group // (groups // 2) == core, own_ref[:, lanes], got_ref[:, lanes])


def fill(table, values):
    for r in range(ORDER):
        table[r] = row(values, r)


def gate_kernel(tokens, half, step, counter, place, key_ref, value_ref, edge_ref, taps_ref, mix_ref,
                gated_ref, start_ref, mine_ref, other_ref, key_rows, value_rows, decays, taps):
    block = pl.program_id(0)
    lane = lax.broadcasted_iota(jnp.int32, (SUBS, LANES), 1)
    sub = lax.broadcasted_iota(jnp.int32, (SUBS, LANES), 0)
    is_mine = (block * 2) // pl.num_programs(0) == place[2]
    for group in range(WIDTH // LANES):
        cols = slice(group * LANES, (group + 1) * LANES)
        place_of = block * (WIDTH // LANES) + group
        for rows, source, f in ((key_rows, key_ref, 1), (value_rows, value_ref, 2)):
            spread(rows, source, 0, cols, 2 * SUBS, step)
            rows[BASE - GAP - 2 : BASE - GAP, :] = edge_ref[f, :, lanes_of(place_of)].astype(jnp.float32)
        for lag in range(SHORT):
            taps[lag] = row(taps_ref[1, :, cols], lag) * KEEP_SCALE
            taps[SHORT + lag] = row(taps_ref[2, :, cols], lag)
        rates = rates_of(mix_ref[:, cols], tokens)
        fill(decays, jnp.exp(-rates))
        jumps = {d: jnp.exp(-rates * float(d * step)) for d in (1, 2, 4)}
        whole = jnp.exp(-rates * float(half))
        channel = place[1] + block * WIDTH + group * LANES + lane
        carried = None
        for part in range(2):
            base = BASE + part * SUBS * (step + GAP)
            first = counter[1] + place[0] + part * half + sub * step
            bits = counter[0] + first * jnp.int32(-1640531535) + channel * jnp.int32(-2048144777)

            def quad(j, carry):
                states, k1, k2, v1, v2, bits = carry
                values = []
                for u in range(GATE_STEPS):
                    k0 = across(key_rows, base + GATE_STEPS * j + u, step)
                    v0 = across(value_rows, base + GATE_STEPS * j + u, step)
                    keyed = taps[0] * k0 + taps[1] * k1 + taps[2] * k2
                    valued = taps[3] * v0 + taps[4] * v1 + taps[5] * v2
                    h = bits + jnp.int32(-1640531535) * u
                    h = h ^ lax.shift_right_logical(h, jnp.full_like(h, 16))
                    h = h * jnp.int32(2146121005)
                    h = h ^ lax.shift_right_logical(h, jnp.full_like(h, 15))
                    h = h * jnp.int32(-2073254261)
                    keep = (h & jnp.int32(-536870912)) != 0
                    values.append(jnp.where(keep, keyed * valued, 0.0))
                    k1, k2, v1, v2 = k0, k1, v0, v1
                wides = []
                for u in range(0, GATE_STEPS, 2):
                    rounded = jnp.concatenate(values[u : u + 2], axis=0).astype(jnp.bfloat16)
                    at = pl.multiple_of(part * half + (GATE_STEPS * j + u) * SUBS, 2 * SUBS)
                    gated_ref[place_of, pl.ds(at, 2 * SUBS), :] = rounded
                    wide = rounded.astype(jnp.float32)
                    wides += [wide[:SUBS], wide[SUBS:]]
                after = []
                for r, x in enumerate(states):
                    a = decays[r]
                    for g in wides:
                        x = x * a + g
                    after.append(x)
                return (tuple(after), k1, k2, v1, v2, bits + jnp.int32((-1640531535 * GATE_STEPS + 2**31) % 2**32 - 2**31))

            zero = jnp.zeros((SUBS, LANES), jnp.float32)
            init = (
                (zero,) * ORDER,
                across(key_rows, base - GAP - 1, step),
                across(key_rows, base - GAP - 2, step),
                across(value_rows, base - GAP - 1, step),
                across(value_rows, base - GAP - 2, step),
                bits,
            )
            states = lax.fori_loop(0, step // GATE_STEPS, quad, init)[0]
            ends = []
            for r in range(ORDER):
                x = states[r]
                for d in (1, 2, 4):
                    x = x + row(jumps[d], r) * jnp.where(sub >= d, pltpu.roll(x, d, 0), 0.0)
                before = jnp.where(sub >= 1, pltpu.roll(x, 1, 0), 0.0)
                last = jnp.broadcast_to(x[SUBS - 1 : SUBS, :], (SUBS, LANES))
                if part == 1:
                    rate = row(rates, r)
                    before = before + jnp.exp(-rate * (sub * step).astype(jnp.float32)) * carried[r]
                    last = last + row(whole, r) * carried[r]
                start_ref[part, place_of, r] = before
                ends.append(last)
            carried = ends
        end = jnp.concatenate([last[0:1, :] for last in carried], axis=0)

        @pl.when(is_mine)
        def _():
            mine_ref[:, cols] = end

        @pl.when(jnp.logical_not(is_mine))
        def _():
            other_ref[:, cols] = end


def query_setup(tokens, half, step, which, lanes, planes_ref, edge_ref, taps_ref, mix_ref, query_rows, decays, taps):
    spread(query_rows, planes_ref.at[0], which * half, lanes, SUBS, step)
    tail = planes_ref[0, half - 2 * SUBS : half, lanes].astype(jnp.float32)[2 * SUBS - 2 :]
    edge = edge_ref[0, :, lanes].astype(jnp.float32)
    query_rows[BASE - GAP - 2 : BASE - GAP, :] = jnp.where(which == 0, edge, tail)
    for lag in range(SHORT):
        taps[lag] = row(taps_ref[0, :, lanes], lag)
    rates = rates_of(mix_ref[:, lanes], tokens)
    fill(decays, jnp.exp(-rates))
    return rates


def scan_quad(step, j, carry, gated_ref, base, query_rows, decays, gains, taps, skip, emit):
    states, q1, q2 = carry
    values = []
    for u in range(0, QUAD, 2):
        at = pl.multiple_of(base + (QUAD * j + u) * SUBS, 2 * SUBS)
        wide = gated_ref[pl.ds(at, 2 * SUBS), :].astype(jnp.float32)
        values += [wide[:SUBS], wide[SUBS:]]
    totals = [skip * g for g in values]
    after = []
    for r, x in enumerate(states):
        a = decays[r]
        c = gains[r]
        for u, g in enumerate(values):
            x = x * a + g
            totals[u] = totals[u] + x * c
        after.append(x)
    for u in range(QUAD):
        q0 = across(query_rows, BASE + QUAD * j + u, step)
        emit(u, taps[0] * q0 + taps[1] * q1 + taps[2] * q2, totals[u])
        q1, q2 = q0, q1
    return (tuple(after), q1, q2)


def gather(mixed_ref, mixed_rows, lanes, step):
    for n in range(SUBS):
        at = n * (step + GAP)
        mixed_ref[n * step : (n + 1) * step, lanes] = mixed_rows[at : at + step, :].astype(jnp.bfloat16)


def local_kernel(tokens, half, step, first, last, which, gated_ref, planes_ref, edge_ref, taps_ref, mix_ref,
                 residue_ref, skip_ref, start_ref, *rest):
    local_ref, filtered_ref, query_rows, decays, gains, taps = rest[-6:]

    @pl.loop(first, last)
    def _(group):
        lanes = lanes_of(group)
        query_setup(tokens, half, step, which[0], lanes, planes_ref, edge_ref, taps_ref, mix_ref, query_rows, decays, taps)
        fill(gains, residue_ref[:, lanes])
        skip = row(skip_ref[:, lanes], 0)

        def quad(j, carry):
            def emit(u, query, total):
                spot = pl.ds(pl.multiple_of((QUAD * j + u) * SUBS, SUBS), SUBS)
                local_ref[group, spot, :] = total
                filtered_ref[group, spot, :] = query

            return scan_quad(step, j, carry, gated_ref.at[group], which[0] * half, query_rows, decays, gains, taps, skip, emit)

        states = tuple(start_ref[which[0], group, r] for r in range(ORDER))
        q1, q2 = across(query_rows, BASE - GAP - 1, step), across(query_rows, BASE - GAP - 2, step)
        lax.fori_loop(0, step // QUAD, quad, (states, q1, q2))


def blend_kernel(tokens, half, step, groups, which, gated_ref, planes_ref, edge_ref, taps_ref, mix_ref, residue_ref,
                 skip_ref, start_ref, own_ref, got_ref, mixed_ref, query_rows, decays, gains, taps, mixed_rows):
    sub = lax.broadcasted_iota(jnp.int32, (SUBS, LANES), 0)
    offset = (which[0] * half + sub * step).astype(jnp.float32)

    @pl.loop(0, groups)
    def _(group):
        lanes = lanes_of(group)
        rates = query_setup(tokens, half, step, which[0], lanes, planes_ref, edge_ref, taps_ref, mix_ref, query_rows, decays, taps)
        fill(gains, residue_ref[:, lanes])
        skip = row(skip_ref[:, lanes], 0)
        into = state_of(own_ref, got_ref, which[1], group, groups)

        def quad(j, carry):
            def emit(u, query, total):
                mixed_rows[pl.ds(QUAD * j + u, SUBS, stride=step + GAP), :] = query * total

            return scan_quad(step, j, carry, gated_ref.at[group], which[0] * half, query_rows, decays, gains, taps, skip, emit)

        states = tuple(
            start_ref[which[0], group, r] + jnp.exp(-row(rates, r) * offset) * row(into, r) for r in range(ORDER)
        )
        q1, q2 = across(query_rows, BASE - GAP - 1, step), across(query_rows, BASE - GAP - 2, step)
        lax.fori_loop(0, step // QUAD, quad, (states, q1, q2))
        gather(mixed_ref, mixed_rows, lanes, step)


def carry_kernel(tokens, half, step, groups, mine, which, local_ref, filtered_ref, mix_ref, residue_ref, state_ref, *rest):
    mixed_ref, decays, mixed_rows = rest[-3:]
    sub = lax.broadcasted_iota(jnp.int32, (SUBS, LANES), 0)
    offset = (which[0] * half + sub * step + 1).astype(jnp.float32)

    base = (which[1] if mine else 1 - which[1]) * groups

    @pl.loop(0, groups)
    def _(at):
        group = base + at
        lanes = lanes_of(group)
        rates = rates_of(mix_ref[:, lanes], tokens)
        fill(decays, jnp.exp(-rates))
        into = state_ref[:, lanes_of(at)] * residue_ref[:, lanes]

        def quad(j, states):
            totals = [None] * QUAD
            after = []
            for r, x in enumerate(states):
                a = decays[r]
                for u in range(QUAD):
                    totals[u] = x if totals[u] is None else totals[u] + x
                    x = x * a
                after.append(x)
            for u in range(QUAD):
                spot = pl.ds(pl.multiple_of((QUAD * j + u) * SUBS, SUBS), SUBS)
                value = filtered_ref[group, spot, :] * (local_ref[group, spot, :] + totals[u])
                mixed_rows[pl.ds(QUAD * j + u, SUBS, stride=step + GAP), :] = value
            return tuple(after)

        states = tuple(jnp.exp(-row(rates, r) * offset) * row(into, r) for r in range(ORDER))
        lax.fori_loop(0, step // QUAD, quad, states)
        gather(mixed_ref, mixed_rows, lanes, step)


def project_kernel(mixed_ref, weight_ref, out_ref):
    out_ref[...] = jnp.dot(mixed_ref[...], weight_ref[...], preferred_element_type=jnp.float32).astype(out_ref.dtype)


def combine_kernel(own_ref, got_ref, *rest):
    lanes = pl.ds(pl.multiple_of(pl.program_id(0) * TILE_COLS, TILE_COLS), TILE_COLS)
    rest[-1][...] = (own_ref[...] + got_ref[:, lanes].astype(jnp.float32)).astype(jnp.bfloat16)


def table(count=ORDER):
    return pltpu.VMEM((count, SUBS, LANES), jnp.float32)


def room(mib):
    return pltpu.CompilerParams(vmem_limit_bytes=mib * 2**20)


def cost(vectors, moved):
    return pl.CostEstimate(flops=vectors, bytes_accessed=moved, transcendentals=0)


def gate(counter, place, planes, edge, taps, mix, tokens):
    rows, channels = planes.shape[1:]
    half = rows // 2
    step = half // SUBS
    blocks = channels // WIDTH
    spread_rows = BASE + 2 * SUBS * (step + GAP)
    first = lambda b, owner: jnp.clip(b - owner * (blocks // 2), 0, blocks // 2 - 1)
    return pl.pallas_call(
        lambda *refs: gate_kernel(tokens, half, step, *refs),
        out_shape=(
            pltpu.VMEM((channels // LANES, rows, LANES), jnp.bfloat16),
            pltpu.VMEM((2, channels // LANES, ORDER, SUBS, LANES), jnp.float32),
            jax.ShapeDtypeStruct((ORDER, channels // 2), jnp.float32),
            jax.ShapeDtypeStruct((ORDER, channels // 2), jnp.float32),
        ),
        grid_spec=pltpu.PrefetchScalarGridSpec(
            num_scalar_prefetch=2,
            grid=(blocks,),
            in_specs=[
                pl.BlockSpec((None, rows, WIDTH), lambda b, c, s: (1, 0, b)),
                pl.BlockSpec((None, rows, WIDTH), lambda b, c, s: (2, 0, b)),
                pl.BlockSpec(memory_space=pltpu.VMEM),
                pl.BlockSpec((3, SHORT, WIDTH), lambda b, c, s: (0, 0, b)),
                pl.BlockSpec((ORDER, WIDTH), lambda b, c, s: (0, b)),
            ],
            out_specs=(
                pl.BlockSpec(memory_space=pltpu.VMEM),
                pl.BlockSpec(memory_space=pltpu.VMEM),
                pl.BlockSpec((ORDER, WIDTH), lambda b, c, s: (0, first(b, s[2]))),
                pl.BlockSpec((ORDER, WIDTH), lambda b, c, s: (0, first(b, 1 - s[2]))),
            ),
            scratch_shapes=[pltpu.VMEM((spread_rows, LANES), jnp.float32)] * 2 + [table(), table(2 * SHORT)],
        ),
        name="gate",
        compiler_params=room(16),
        cost_estimate=cost(15 * 10**9, 4 * rows * channels),
    )(counter, place, planes, planes, edge, taps, mix)


def scan_scratch(step):
    return [pltpu.VMEM((BASE + SUBS * (step + GAP), LANES), jnp.float32), table(), table(), table(SHORT)]


def resident(kernel, which, operands, out_shape, scratch, aliases, time):
    several = isinstance(out_shape, tuple)
    place = pl.BlockSpec(memory_space=pltpu.VMEM)
    return pl.pallas_call(
        kernel,
        out_shape=out_shape,
        grid_spec=pltpu.PrefetchScalarGridSpec(
            num_scalar_prefetch=1,
            grid=(1,),
            in_specs=[place] * len(operands),
            out_specs=(place,) * len(out_shape) if several else place,
            scratch_shapes=scratch,
        ),
        input_output_aliases=aliases,
        compiler_params=room(16),
        cost_estimate=cost(int(time * 10**9), 2**20),
    )(which, *operands)


def local(which, operands, tokens, first, last, before):
    groups, rows = operands[0].shape[:2]
    half = rows // 2
    step = half // SUBS
    shape = pltpu.VMEM((groups, half, LANES), jnp.float32)
    first, last = first * groups // 4, last * groups // 4
    return resident(
        lambda *refs: local_kernel(tokens, half, step, first, last, *refs), which, (*operands, *before), (shape, shape),
        scan_scratch(step), {1 + len(operands) + k: k for k in range(len(before))}, 0.55 * (last - first),
    )


def carry(which, parts, mix, residue, state, mine, before, tokens):
    groups, half = parts[0].shape[:2]
    step = half // SUBS
    return resident(
        lambda *refs: carry_kernel(tokens, half, step, groups // 2, mine, *refs), which,
        (*parts, mix, residue, state, *before), pltpu.VMEM((half, groups * LANES), jnp.bfloat16),
        [table(), pltpu.VMEM((SUBS * (step + GAP), LANES), jnp.float32)], {6: 0} if before else {}, 2.5,
    )


def blend(which, operands, own, got, tokens):
    groups, rows = operands[0].shape[:2]
    half = rows // 2
    step = half // SUBS
    return resident(
        lambda *refs: blend_kernel(tokens, half, step, groups, *refs), which, (*operands, own, got),
        jax.ShapeDtypeStruct((half, groups * LANES), jnp.bfloat16),
        scan_scratch(step) + [pltpu.VMEM((SUBS * (step + GAP), LANES), jnp.float32)], {}, 9,
    )


def project(mixed, weight, first, cols, dtype):
    rows, depth = mixed.shape
    at = first // TILE_COLS
    return pl.pallas_call(
        project_kernel,
        out_shape=jax.ShapeDtypeStruct((rows, cols), dtype),
        grid=(cols // TILE_COLS,),
        in_specs=[
            pl.BlockSpec((rows, depth), lambda n: (0, 0)),
            pl.BlockSpec((depth, TILE_COLS), lambda n: (0, at + n)),
        ],
        out_specs=pl.BlockSpec((rows, TILE_COLS), lambda n: (0, n)),
        compiler_params=room(16),
        cost_estimate=cost(2 * rows * depth * cols, 2 * (rows * depth + depth * cols)),
    )(mixed, weight)


def combine(own, got, first, before):
    rows, cols = got.shape
    at = first // TILE_COLS
    block = pl.BlockSpec((rows, TILE_COLS), lambda n: (0, at + n))
    return pl.pallas_call(
        combine_kernel,
        out_shape=jax.ShapeDtypeStruct(own.shape, jnp.bfloat16),
        grid=(cols // TILE_COLS,),
        in_specs=[block, pl.BlockSpec(memory_space=pltpu.VMEM)]
        + [pl.BlockSpec(memory_space=pl.ANY)] * len(before),
        out_specs=block,
        input_output_aliases={2: 0} if before else {},
        name="combine",
        compiler_params=room(8),
        cost_estimate=cost(rows * cols, 8 * rows * cols),
    )(own, got, *before)


def states_before(mine, other, mix, tokens, rows, index, count, between):
    core = index % 2
    width = mine.shape[1]
    rates = rates_of(lax.dynamic_slice_in_dim(mix, core * width, width, 1), tokens)
    decay = lambda chunks: jnp.exp(-rates * float(rows * chunks))
    steps = [decay(n) for n in (1, 2, 4)]
    assert count == 16

    def ring(value, pairs):
        return lax.ppermute(value, "ctx", pairs)

    sibling = ring(other, [(i, i ^ 1) for i in range(count)])
    early = jnp.where(core == 0, mine, sibling)
    late = jnp.where(core == 0, sibling, mine)
    chip = steps[0] * early + late
    beside = ring(chip, [(i, i ^ 2) for i in range(count)])
    between(0)
    upper = (index // 2) % 2 == 1
    group = jnp.where(upper, steps[1] * beside + chip, steps[1] * chip + beside)
    ring_at = index // 4
    odd = ring_at % 2 == 1
    near = ring(group, [(i, i ^ 4) for i in range(count)])
    between(1)
    couple = jnp.where(odd, steps[2] * near + group, steps[2] * group + near)
    far = ring(couple, [(i, (3 - i // 4) * 4 + i % 4) for i in range(count)])
    between(2)
    state = jnp.where(ring_at >= 2, jnp.where(odd, steps[2] * far, far), 0.0) + jnp.where(odd, near, 0.0)
    state = jnp.where(upper, steps[1] * state + beside, state)
    following = steps[0] * state + early
    own = jnp.where(core == 0, state, following)
    sent = jnp.where(core == 0, following, state)
    return own, ring(sent, [(i, i ^ 1) for i in range(count)])


def body(features, short_filter, mode_residue, decay_mix, skip_gain, counter, out_weight):
    rows = features.shape[0]
    channels = features.shape[2]
    count = lax.axis_size("ctx")
    tokens = rows * count
    index = lax.axis_index("ctx")
    side = lax.axis_index("ch")
    planes = jnp.transpose(features, (1, 0, 2))
    far_memory = lambda x: pltpu.with_memory_space_constraint(x, pltpu.HBM)
    edge = lax.ppermute(planes[:, rows - (SHORT - 1) :], "ctx", [(i, i + 1) for i in range(count - 1)])
    slot = jnp.arange(4, dtype=jnp.int32)

    def scalars(*values):
        out = jnp.zeros((4,), jnp.int32)
        for k, value in enumerate(values):
            out = jnp.where(slot == k, value, out)
        return out

    place = scalars(index * rows, side * channels, index % 2)
    to_send = scalars(1 - side, index % 2)
    to_keep = scalars(side, index % 2)
    gated, start, mine, other = gate(
        far_memory(counter), place, far_memory(planes), edge, far_memory(short_filter), far_memory(decay_mix), tokens
    )
    operands = (gated, planes, edge, short_filter, decay_mix, mode_residue, skip_gain[None], start)
    parts = [()]

    def between(piece):
        first, last = ((0, 2), (2, 3), (3, 4))[piece]
        parts[0] = local(to_send, operands, tokens, first, last, parts[0])

    own, got = states_before(mine, other, decay_mix, tokens, rows, index, count, between)
    sent = carry(to_send, parts[0], decay_mix, mode_residue, own, True, (), tokens)
    sent = carry(to_send, parts[0], decay_mix, mode_residue, got, False, (sent,), tokens)
    outs = out_weight.shape[1]
    received = []
    for first, cols in chunks_of(outs):
        part = project(sent, out_weight, first, cols, jnp.bfloat16)
        received.append(lax.ppermute(part, "ch", [(0, 1), (1, 0)]))
    own, part = lax.optimization_barrier((own, part))
    kept = blend(to_keep, operands, own, got, tokens)
    total = project(kept, out_weight, 0, outs, jnp.float32)
    done = ()
    for k, (first, _) in enumerate(chunks_of(outs)):
        done = (combine(total, received[k], first, done),)
    return done[0]


def solution(mesh):
    placed = (
        P(("dp", "ctx"), None, "ch"),
        P(None, None, "ch"),
        P(None, "ch"),
        P(None, "ch"),
        P("ch"),
        P("dp"),
        P("ch", None),
    )

    return jax.shard_map(body, mesh=mesh, in_specs=placed, out_specs=P(("dp", "ctx", "ch"), None), check_vma=False)
```

time: 112 us -> 101 us (0.902)
  Pallas kernels: 70.1 us -> 62.4 us
  waiting for transfers between devices: 15 us -> 12.5 us
    pallas_call x6, Pallas kernels: 29.9 us -> 22.5 us  [resident(): pl.pallas_call(kernel, out_shape=out_shape, grid_spec=pltpu.PrefetchScala...]
    ppermute x8 -> x9, waiting for transfers between devices: 13.4 us -> 10.6 us  [body(): received.append(lax.ppermute(part, 'ch', [(0, 1), (1, 0)]))]
    pallas_call x8 -> x9, Pallas kernels: 5.99 us -> 6.93 us  [combine(): pl.pallas_call(combine_kernel, out_shape=jax.ShapeDtypeStruct(own.shape,...]
    pallas_call x9 -> x10, Pallas kernels: 19.9 us -> 19.5 us  [project(): pl.pallas_call(project_kernel, out_shape=jax.ShapeDtypeStruct((rows, cols...]
    ppermute x8 -> x9, starting transfers between devices: 9.41 us -> 9.39 us  [body(): received.append(lax.ppermute(part, 'ch', [(0, 1), (1, 0)]))]
  transfers between devices with their start and end apart: 14 -> 15, of which waited for: 6 -> 6; matrix products, arithmetic and copies ran while one was open for 0% -> 0% of each run, Pallas kernels for 38% -> 44%
where the time goes in v3:
time: 101 us; the launch traced here: 100 us
  Pallas kernels  62.4 us (62%)
  starting transfers between devices  24 us (24%)
  waiting for transfers between devices  12.5 us (12%)
    pallas_call x6, Pallas kernels, resident(): pl.pallas_call(kernel, out_shape=out_shape, grid_spec=pltpu.PrefetchScala...  22.5 us
    pallas_call x10, Pallas kernels, project(): pl.pallas_call(project_kernel, out_shape=jax.ShapeDtypeStruct((rows, cols...  19.5 us
    pallas_call x1, Pallas kernels, gate(): pl.pallas_call(lambda *refs: gate_kernel(tokens, half, step, *refs), out_...  13.5 us
    ppermute x5, starting transfers between devices, ring(): return lax.ppermute(value, 'ctx', pairs)  13.3 us
    ppermute x9, waiting for transfers between devices, body(): received.append(lax.ppermute(part, 'ch', [(0, 1), (1, 0)]))  10.6 us
    ppermute x9, starting transfers between devices, body(): received.append(lax.ppermute(part, 'ch', [(0, 1), (1, 0)]))  9.39 us
    pallas_call x9, Pallas kernels, combine(): pl.pallas_call(combine_kernel, out_shape=jax.ShapeDtypeStruct(own.shape,...  6.93 us
  transfers between devices with their start and end apart: 15, of which 6 were waited for; matrix products, arithmetic and copies ran while one was open for 0% of the time, Pallas kernels for 44%

profile of v3, /device:TPU:0, one launch (start us, length us, event | category | flops | bytes accessed | tf_op | source)
XLA Modules:
  0.0 100.5 jit_solution(9694097002743256904)
XLA Ops:
  0.0 0.9 slice.4
  0.9 1.3 %collective-permute-start = (bf16[3,2,2048]{2,1,0:T(2,128)(2,1)S(1)}, bf16[3,2,2048]{2,1,0:T(2,128)(2,1)S(1)}, u32[]{:S(2)}, u32[]{:S(2)}) collective-permute-start(bf16[3,2,2048]{2,1,0:T(2,128)(2,1)S(1)} %slice.4), channel_id=1, source_target_pairs={{0,8},{8,16},{16,24},{24,32},{32,40},{40,48},{48,56},{56,64},{64,7... | collective-permute-start | bytes 73736 | tf_op jit(solution)/shard_map/ppermute | solution.py:476
  3.1 13.5 %gate.1 = (bf16[16,512,128]{2,1,0:T(8,128)(2,1)S(1)}, f32[2,16,16,8,128]{4,3,2,1,0:T(8,128)S(1)}, f32[16,1024]{1,0:T(8,128)S(1)}, f32[16,1024]{1,0:T(8,128)S(1)}) custom-call(s32[2]{0:T(128)} %refs_0_.1, s32[4]{0:T(128)S(1)} %compare_select_fusion.refs_1_, bf16[3,512,2048]{2,1,0:T(8,128)(2,1)} %bitcast.5, bf16[3,512,2048]{2,1,0:T(8,128)(2,1)} %bitcast.6, ...), custom_call_target="tpu_custom_call" | custom-call | flops 15000000512 | bytes 4194304 | tf_op jit(solution)/shard_map/gate/pallas_call | solution.py:310
  16.6 4.8 %collective-permute-start.1 = (f32[16,1024]{1,0:T(8,128)S(1)}, f32[16,1024]{1,0:T(8,128)S(1)}, u32[]{:S(2)}, u32[]{:S(2)}) collective-permute-start(f32[16,1024]{1,0:T(8,128)S(1)} %get-tuple-element.19), channel_id=1, source_target_pairs={{0,8},{8,0},{16,24},{24,16},{32,40},{40,32},{48,56},{56,48},{64,72... | collective-permute-start | bytes 196616 | tf_op jit(solution)/shard_map/ppermute | solution.py:442
  22.3 3.6 %collective-permute-start.2 = (f32[16,1024]{1,0:T(8,128)S(1)}, f32[16,1024]{1,0:T(8,128)S(1)}, u32[]{:S(2)}, u32[]{:S(2)}) collective-permute-start(f32[16,1024]{1,0:T(8,128)S(1)} %select_add_fusion), channel_id=1, source_target_pairs={{0,16},{8,24},{16,0},{24,8},{32,48},{40,56},{48,32},{56,40},{64,80... | collective-permute-start | bytes 196616 | tf_op jit(solution)/shard_map/ppermute | solution.py:442
  26.0 4.2 %shard_map.73 = (f32[16,256,128]{2,1,0:T(8,128)S(1)}, f32[16,256,128]{2,1,0:T(8,128)S(1)}) custom-call(s32[4]{0:T(128)S(1)} %select_select_fusion.refs_0_, bf16[16,512,128]{2,1,0:T(8,128)(2,1)S(1)} %get-tuple-element.16.refs_1_, bf16[3,512,2048]{2,1,0:T(8,128)(2,1)S(1)} %bitcast.9, bf16[3,2,2048]{2,1,0:T(2,128)(2,1)S(1)} %collective-permute-done.refs_4_.refs_3_, ...), custom_call_target="tpu_custom_call" | custom-call | flops 4400000000 | bytes 1048576 | tf_op jit(solution)/shard_map/pallas_call | solution.py:349
  30.3 1.7 %collective-permute-start.3 = (f32[16,1024]{1,0:T(8,128)S(1)}, f32[16,1024]{1,0:T(8,128)S(1)}, u32[]{:S(2)}, u32[]{:S(2)}) collective-permute-start(f32[16,1024]{1,0:T(8,128)S(1)} %add_select_fusion.2), channel_id=1, source_target_pairs={{0,32},{8,40},{16,48},{24,56},{32,0},{40,8},{48,16},{56,24},{64,96... | collective-permute-start | bytes 196616 | tf_op jit(solution)/shard_map/ppermute | solution.py:442
  31.9 2.4 %shard_map.74 = (f32[16,256,128]{2,1,0:T(8,128)S(1)}, f32[16,256,128]{2,1,0:T(8,128)S(1)}) custom-call(s32[4]{0:T(128)S(1)} %select_select_fusion.refs_0_, bf16[16,512,128]{2,1,0:T(8,128)(2,1)S(1)} %get-tuple-element.16.refs_1_, bf16[3,512,2048]{2,1,0:T(8,128)(2,1)S(1)} %bitcast.10, ...), custom_call_target="tpu_custom_call", output_to_operand_aliasing={{0}: (9, {}), {1}: (10, {})} | custom-call | flops 2200000000 | bytes 1048576 | tf_op jit(solution)/shard_map/pallas_call | solution.py:349
  34.7 3.1 %collective-permute-start.4 = (f32[16,1024]{1,0:T(8,128)S(1)}, f32[16,1024]{1,0:T(8,128)S(1)}, u32[]{:S(2)}, u32[]{:S(2)}) collective-permute-start(f32[16,1024]{1,0:T(8,128)S(1)} %add_select_fusion.1), channel_id=1, source_target_pairs={{0,96},{8,104},{16,112},{24,120},{32,64},{40,72},{48,80},{56,88},{... | collective-permute-start | bytes 196616 | tf_op jit(solution)/shard_map/ppermute | solution.py:442
  37.8 2.4 %shard_map.75 = (f32[16,256,128]{2,1,0:T(8,128)S(1)}, f32[16,256,128]{2,1,0:T(8,128)S(1)}) custom-call(s32[4]{0:T(128)S(1)} %select_select_fusion.refs_0_, bf16[16,512,128]{2,1,0:T(8,128)(2,1)S(1)} %get-tuple-element.16.refs_1_, bf16[3,512,2048]{2,1,0:T(8,128)(2,1)S(1)} %bitcast.11, ...), custom_call_target="tpu_custom_call", output_to_operand_aliasing={{0}: (9, {}), {1}: (10, {})} | custom-call | flops 2200000000 | bytes 1048576 | tf_op jit(solution)/shard_map/pallas_call | solution.py:349
  40.4 2.6 %shard_map.76.refs_6_ = bf16[256,2048]{1,0:T(8,128)(2,1)S(1)} custom-call(s32[4]{0:T(128)S(1)} %select_select_fusion.refs_0_, f32[16,256,128]{2,1,0:T(8,128)S(1)} %get-tuple-element.24.refs_1_, f32[16,256,128]{2,1,0:T(8,128)S(1)} %get-tuple-element.25.refs_2_, f32[16,2048]{1,0:T(8,128)S(1)} %copy-done, f32[16,2048]{1,0:T(8,128)S(1)} %copy-done.1, ...), custom_call_target="tpu_custom_call" | custom-call | flops 2500000000 | bytes 1048576 | tf_op jit(solution)/shard_map/pallas_call | solution.py:349
  43.1 2.6 %shard_map.77.mixed_ref = bf16[256,2048]{1,0:T(8,128)(2,1)S(1)} custom-call(s32[4]{0:T(128)S(1)} %select_select_fusion.refs_0_, f32[16,256,128]{2,1,0:T(8,128)S(1)} %get-tuple-element.24.refs_1_, f32[16,256,128]{2,1,0:T(8,128)S(1)} %get-tuple-element.25.refs_2_, f32[16,2048]{1,0:T(8,128)S(1)} %copy-done, ...), custom_call_target="tpu_custom_call", output_to_operand_aliasing={{}: (6, {})} | custom-call | flops 2500000000 | bytes 1048576 | tf_op jit(solution)/shard_map/pallas_call | solution.py:349
  46.7 1.1 %collective-permute-start.6 = (bf16[256,256]{1,0:T(8,128)(2,1)S(1)}, bf16[256,256]{1,0:T(8,128)(2,1)S(1)}, u32[]{:S(2)}, u32[]{:S(2)}) collective-permute-start(bf16[256,256]{1,0:T(8,128)(2,1)S(1)} %shard_map.78), channel_id=1, source_target_pairs={{0,4},{4,0},{1,5},{5,1},{2,6},{6,2},{3,7},{7,3},{8,12},{12,8},{9,1... | collective-permute-start | bytes 393224 | tf_op jit(solution)/shard_map/ppermute | solution.py:505
  47.8 1.3 %shard_map.87 = bf16[256,512]{1,0:T(8,128)(2,1)S(1)} custom-call(bf16[256,2048]{1,0:T(8,128)(2,1)S(1)} %shard_map.77.mixed_ref, bf16[2048,4096]{1,0:T(8,128)(2,1)S(1)} %bitcast.3), custom_call_target="tpu_custom_call" | custom-call | flops 536870912 | bytes 3145728 | tf_op jit(solution)/shard_map/pallas_call | solution.py:401
  49.1 1.3 %shard_map.86 = bf16[256,512]{1,0:T(8,128)(2,1)S(1)} custom-call(bf16[256,2048]{1,0:T(8,128)(2,1)S(1)} %shard_map.77.mixed_ref, bf16[2048,4096]{1,0:T(8,128)(2,1)S(1)} %bitcast.3), custom_call_target="tpu_custom_call" | custom-call | flops 536870912 | bytes 3145728 | tf_op jit(solution)/shard_map/pallas_call | solution.py:401
  50.3 1.3 %shard_map.85 = bf16[256,512]{1,0:T(8,128)(2,1)S(1)} custom-call(bf16[256,2048]{1,0:T(8,128)(2,1)S(1)} %shard_map.77.mixed_ref, bf16[2048,4096]{1,0:T(8,128)(2,1)S(1)} %bitcast.3), custom_call_target="tpu_custom_call" | custom-call | flops 536870912 | bytes 3145728 | tf_op jit(solution)/shard_map/pallas_call | solution.py:401
  51.6 1.1 %collective-permute-start.14 = (bf16[256,256]{1,0:T(8,128)(2,1)S(1)}, bf16[256,256]{1,0:T(8,128)(2,1)S(1)}, u32[]{:S(2)}, u32[]{:S(2)}) collective-permute-start(bf16[256,256]{1,0:T(8,128)(2,1)S(1)} %shard_map.88), channel_id=1, source_target_pairs={{0,4},{4,0},{1,5},{5,1},{2,6},{6,2},{3,7},{7,3},{8,12},{12,8},{9,1... | collective-permute-start | bytes 393224 | tf_op jit(solution)/shard_map/ppermute | solution.py:505
  52.7 1.0 collective-permute-start.11
  53.7 1.0 %collective-permute-start.12 = (bf16[256,512]{1,0:T(8,128)(2,1)S(1)}, bf16[256,512]{1,0:T(8,128)(2,1)S(1)}, u32[]{:S(2)}, u32[]{:S(2)}) collective-permute-start(bf16[256,512]{1,0:T(8,128)(2,1)S(1)} %shard_map.86), channel_id=1, source_target_pairs={{0,4},{4,0},{1,5},{5,1},{2,6},{6,2},{3,7},{7,3},{8,12},{12,8},{9,1... | collective-permute-start | bytes 786440 | tf_op jit(solution)/shard_map/ppermute | solution.py:505
  54.7 1.0 collective-permute-start.13
  55.7 8.2 %shard_map.79.mixed_ref = bf16[256,2048]{1,0:T(8,128)(2,1)S(1)} custom-call(s32[4]{0:T(128)S(1)} %select_select_fusion.1.refs_0_, bf16[16,512,128]{2,1,0:T(8,128)(2,1)S(1)} %get-tuple-element.16.refs_1_, bf16[3,512,2048]{2,1,0:T(8,128)(2,1)S(1)} %bitcast.12, bf16[3,2,2048]{2,1,0:T(2,128)(2,1)S(1)} %collective-permute-done.refs_4_.refs_3_, ...), custom_call_target="tpu_custom_call" | custom-call | flops 8999999488 | bytes 1048576 | tf_op jit(solution)/shard_map/pallas_call | solution.py:349
  64.0 1.3 %shard_map.84 = bf16[256,512]{1,0:T(8,128)(2,1)S(1)} custom-call(bf16[256,2048]{1,0:T(8,128)(2,1)S(1)} %shard_map.77.mixed_ref, bf16[2048,4096]{1,0:T(8,128)(2,1)S(1)} %bitcast.3), custom_call_target="tpu_custom_call" | custom-call | flops 536870912 | bytes 3145728 | tf_op jit(solution)/shard_map/pallas_call | solution.py:401
  65.2 1.3 %shard_map.83 = bf16[256,512]{1,0:T(8,128)(2,1)S(1)} custom-call(bf16[256,2048]{1,0:T(8,128)(2,1)S(1)} %shard_map.77.mixed_ref, bf16[2048,4096]{1,0:T(8,128)(2,1)S(1)} %bitcast.3), custom_call_target="tpu_custom_call" | custom-call | flops 536870912 | bytes 3145728 | tf_op jit(solution)/shard_map/pallas_call | solution.py:401
  66.5 1.3 %shard_map.82 = bf16[256,512]{1,0:T(8,128)(2,1)S(1)} custom-call(bf16[256,2048]{1,0:T(8,128)(2,1)S(1)} %shard_map.77.mixed_ref, bf16[2048,4096]{1,0:T(8,128)(2,1)S(1)} %bitcast.3), custom_call_target="tpu_custom_call" | custom-call | flops 536870912 | bytes 3145728 | tf_op jit(solution)/shard_map/pallas_call | solution.py:401
  67.8 1.3 %shard_map.81 = bf16[256,512]{1,0:T(8,128)(2,1)S(1)} custom-call(bf16[256,2048]{1,0:T(8,128)(2,1)S(1)} %shard_map.77.mixed_ref, bf16[2048,4096]{1,0:T(8,128)(2,1)S(1)} %bitcast.3), custom_call_target="tpu_custom_call" | custom-call | flops 536870912 | bytes 3145728 | tf_op jit(solution)/shard_map/pallas_call | solution.py:401
  69.1 1.1 %collective-permute-start.7 = (bf16[256,512]{1,0:T(8,128)(2,1)S(1)}, bf16[256,512]{1,0:T(8,128)(2,1)S(1)}, u32[]{:S(2)}, u32[]{:S(2)}) collective-permute-start(bf16[256,512]{1,0:T(8,128)(2,1)S(1)} %shard_map.81), channel_id=1, source_target_pairs={{0,4},{4,0},{1,5},{5,1},{2,6},{6,2},{3,7},{7,3},{8,12},{12,8},{9,1... | collective-permute-start | bytes 786440 | tf_op jit(solution)/shard_map/ppermute | solution.py:505
  70.2 1.0 collective-permute-start.8
  71.2 1.0 %collective-permute-start.9 = (bf16[256,512]{1,0:T(8,128)(2,1)S(1)}, bf16[256,512]{1,0:T(8,128)(2,1)S(1)}, u32[]{:S(2)}, u32[]{:S(2)}) collective-permute-start(bf16[256,512]{1,0:T(8,128)(2,1)S(1)} %shard_map.83), channel_id=1, source_target_pairs={{0,4},{4,0},{1,5},{5,1},{2,6},{6,2},{3,7},{7,3},{8,12},{12,8},{9,1... | collective-permute-start | bytes 786440 | tf_op jit(solution)/shard_map/ppermute | solution.py:505
  72.2 2.7 %collective-permute-done.13.got_ref = bf16[256,512]{1,0:T(8,128)(2,1)S(1)} collective-permute-done((bf16[256,512]{1,0:T(8,128)(2,1)S(1)}, bf16[256,512]{1,0:T(8,128)(2,1)S(1)}, u32[]{:S(2)}, u32[]{:S(2)}) %collective-permute-start.13) | collective-permute-done | bytes 262176 | tf_op jit(solution)/shard_map/ppermute | solution.py:505
  74.9 1.0 %collective-permute-start.10 = (bf16[256,512]{1,0:T(8,128)(2,1)S(1)}, bf16[256,512]{1,0:T(8,128)(2,1)S(1)}, u32[]{:S(2)}, u32[]{:S(2)}) collective-permute-start(bf16[256,512]{1,0:T(8,128)(2,1)S(1)} %shard_map.84), channel_id=1, source_target_pairs={{0,4},{4,0},{1,5},{5,1},{2,6},{6,2},{3,7},{7,3},{8,12},{12,8},{9,1... | collective-permute-start | bytes 786440 | tf_op jit(solution)/shard_map/ppermute | solution.py:505
  75.9 9.8 %shard_map.80.own_ref = f32[256,4096]{1,0:T(8,128)S(1)} custom-call(bf16[256,2048]{1,0:T(8,128)(2,1)S(1)} %shard_map.79.mixed_ref, bf16[2048,4096]{1,0:T(8,128)(2,1)S(1)} %bitcast.3), custom_call_target="tpu_custom_call" | custom-call | flops 4294967296 | bytes 17825792 | tf_op jit(solution)/shard_map/pallas_call | solution.py:401
  88.7 7.9 %collective-permute-done.10.got_ref = bf16[256,512]{1,0:T(8,128)(2,1)S(1)} collective-permute-done((bf16[256,512]{1,0:T(8,128)(2,1)S(1)}, bf16[256,512]{1,0:T(8,128)(2,1)S(1)}, u32[]{:S(2)}, u32[]{:S(2)}) %collective-permute-start.10) | collective-permute-done | bytes 262176 | tf_op jit(solution)/shard_map/ppermute | solution.py:505
  (54 shorter events, 10.2 us)
Async XLA Ops:
  0.9 2.1 %collective-permute-start = (bf16[3,2,2048]{2,1,0:T(2,128)(2,1)S(1)}, bf16[3,2,2048]{2,1,0:T(2,128)(2,1)S(1)}, u32[]{:S(2)}, u32[]{:S(2)}) collective-permute-start(bf16[3,2,2048]{2,1,0:T(2,128)(2,1)S(1)} %slice.4), channel_id=1, source_target_pairs={{0,8},{8,16},{16,24},{24,32},{32,40},{40,48},{48,56},{56,64},{64,7... | collective-permute-start | bytes 73736 | tf_op jit(solution)/shard_map/ppermute | solution.py:476
  2.3 23.6 %slice-start.4 = ((s8[6291456]{0:T(1024)(128)(4,1)}), s8[2097152]{0:T(1024)(128)(4,1)S(1)}, s32[]{:S(2)}) async-start(s8[6291456]{0:T(1024)(128)(4,1)} %bitcast.7), calls=%async_computation.4 | async-start | bytes 4194304
  2.3 19.9 %copy-start = (f32[16,2048]{1,0:T(8,128)S(1)}, f32[16,2048]{1,0:T(8,128)}, u32[]{:S(2)}) copy-start(f32[16,2048]{1,0:T(8,128)} %refs_5_.9) | copy-start | bytes 393220
  2.4 23.6 %slice-start.5 = ((s8[6291456]{0:T(1024)(128)(4,1)}), s8[4194304]{0:T(1024)(128)(4,1)S(1)}, s32[]{:S(2)}) async-start(s8[6291456]{0:T(1024)(128)(4,1)} %bitcast.7), calls=%async_computation.5 | async-start | bytes 8388608
  2.4 23.6 %copy-start.1 = (f32[16,2048]{1,0:T(8,128)S(1)}, f32[16,2048]{1,0:T(8,128)}, u32[]{:S(2)}) copy-start(f32[16,2048]{1,0:T(8,128)} %refs_6_.9) | copy-start | bytes 393220
  2.4 23.6 %copy-start.2 = (f32[3,3,2048]{2,1,0:T(4,128)S(1)}, f32[3,3,2048]{2,1,0:T(4,128)}, u32[]{:S(2)}) copy-start(f32[3,3,2048]{2,1,0:T(4,128)} %refs_4_.11) | copy-start | bytes 221188
  2.4 23.6 %copy-start.3 = (f32[2048]{0:T(1024)S(1)}, f32[2048]{0:T(1024)}, u32[]{:S(2)}) copy-start(f32[2048]{0:T(1024)} %param.11) | copy-start | bytes 24580
  16.6 5.7 %collective-permute-start.1 = (f32[16,1024]{1,0:T(8,128)S(1)}, f32[16,1024]{1,0:T(8,128)S(1)}, u32[]{:S(2)}, u32[]{:S(2)}) collective-permute-start(f32[16,1024]{1,0:T(8,128)S(1)} %get-tuple-element.19), channel_id=1, source_target_pairs={{0,8},{8,0},{16,24},{24,16},{32,40},{40,32},{48,56},{56,48},{64,72... | collective-permute-start | bytes 196616 | tf_op jit(solution)/shard_map/ppermute | solution.py:442
  22.3 7.9 %collective-permute-start.2 = (f32[16,1024]{1,0:T(8,128)S(1)}, f32[16,1024]{1,0:T(8,128)S(1)}, u32[]{:S(2)}, u32[]{:S(2)}) collective-permute-start(f32[16,1024]{1,0:T(8,128)S(1)} %select_add_fusion), channel_id=1, source_target_pairs={{0,16},{8,24},{16,0},{24,8},{32,48},{40,56},{48,32},{56,40},{64,80... | collective-permute-start | bytes 196616 | tf_op jit(solution)/shard_map/ppermute | solution.py:442
  30.3 4.3 %collective-permute-start.3 = (f32[16,1024]{1,0:T(8,128)S(1)}, f32[16,1024]{1,0:T(8,128)S(1)}, u32[]{:S(2)}, u32[]{:S(2)}) collective-permute-start(f32[16,1024]{1,0:T(8,128)S(1)} %add_select_fusion.2), channel_id=1, source_target_pairs={{0,32},{8,40},{16,48},{24,56},{32,0},{40,8},{48,16},{56,24},{64,96... | collective-permute-start | bytes 196616 | tf_op jit(solution)/shard_map/ppermute | solution.py:442
  34.7 5.6 %collective-permute-start.4 = (f32[16,1024]{1,0:T(8,128)S(1)}, f32[16,1024]{1,0:T(8,128)S(1)}, u32[]{:S(2)}, u32[]{:S(2)}) collective-permute-start(f32[16,1024]{1,0:T(8,128)S(1)} %add_select_fusion.1), channel_id=1, source_target_pairs={{0,96},{8,104},{16,112},{24,120},{32,64},{40,72},{48,80},{56,88},{... | collective-permute-start | bytes 196616 | tf_op jit(solution)/shard_map/ppermute | solution.py:442
  37.8 8.0 %slice-start = ((s8[16777216]{0:T(1024)(128)(4,1)}), s8[4194304]{0:T(1024)(128)(4,1)S(1)}, s32[]{:S(2)}) async-start(s8[16777216]{0:T(1024)(128)(4,1)} %bitcast.2), calls=%async_computation | async-start | bytes 8388608
  37.8 8.0 %slice-start.1 = ((s8[16777216]{0:T(1024)(128)(4,1)}), s8[4194304]{0:T(1024)(128)(4,1)S(1)}, s32[]{:S(2)}) async-start(s8[16777216]{0:T(1024)(128)(4,1)} %bitcast.2), calls=%async_computation.1 | async-start | bytes 8388608
  40.3 2.8 %collective-permute-start.5 = (f32[16,1024]{1,0:T(8,128)S(1)}, f32[16,1024]{1,0:T(8,128)S(1)}, u32[]{:S(2)}, u32[]{:S(2)}) collective-permute-start(f32[16,1024]{1,0:T(8,128)S(1)} %get-tuple-element.27), channel_id=1, source_target_pairs={{0,8},{8,0},{16,24},{24,16},{32,40},{40,32},{48,56},{56,48},{64,72... | collective-permute-start | bytes 196616 | tf_op jit(solution)/shard_map/ppermute | solution.py:442
  40.4 5.3 %slice-start.2 = ((s8[16777216]{0:T(1024)(128)(4,1)}), s8[4194304]{0:T(1024)(128)(4,1)S(1)}, s32[]{:S(2)}) async-start(s8[16777216]{0:T(1024)(128)(4,1)} %bitcast.2), calls=%async_computation.2 | async-start | bytes 8388608
  43.1 2.7 %slice-start.3 = ((s8[16777216]{0:T(1024)(128)(4,1)}), s8[4194304]{0:T(1024)(128)(4,1)S(1)}, s32[]{:S(2)}) async-start(s8[16777216]{0:T(1024)(128)(4,1)} %bitcast.2), calls=%async_computation.3 | async-start | bytes 8388608
  46.7 53.1 %collective-permute-start.6 = (bf16[256,256]{1,0:T(8,128)(2,1)S(1)}, bf16[256,256]{1,0:T(8,128)(2,1)S(1)}, u32[]{:S(2)}, u32[]{:S(2)}) collective-permute-start(bf16[256,256]{1,0:T(8,128)(2,1)S(1)} %shard_map.78), channel_id=1, source_target_pairs={{0,4},{4,0},{1,5},{5,1},{2,6},{6,2},{3,7},{7,3},{8,12},{12,8},{9,1... | collective-permute-start | bytes 393224 | tf_op jit(solution)/shard_map/ppermute | solution.py:505
  51.6 17.5 %collective-permute-start.14 = (bf16[256,256]{1,0:T(8,128)(2,1)S(1)}, bf16[256,256]{1,0:T(8,128)(2,1)S(1)}, u32[]{:S(2)}, u32[]{:S(2)}) collective-permute-start(bf16[256,256]{1,0:T(8,128)(2,1)S(1)} %shard_map.88), channel_id=1, source_target_pairs={{0,4},{4,0},{1,5},{5,1},{2,6},{6,2},{3,7},{7,3},{8,12},{12,8},{9,1... | collective-permute-start | bytes 393224 | tf_op jit(solution)/shard_map/ppermute | solution.py:505
  52.7 17.5 %collective-permute-start.11 = (bf16[256,512]{1,0:T(8,128)(2,1)S(1)}, bf16[256,512]{1,0:T(8,128)(2,1)S(1)}, u32[]{:S(2)}, u32[]{:S(2)}) collective-permute-start(bf16[256,512]{1,0:T(8,128)(2,1)S(1)} %shard_map.85), channel_id=1, source_target_pairs={{0,4},{4,0},{1,5},{5,1},{2,6},{6,2},{3,7},{7,3},{8,12},{12,8},{9,1... | collective-permute-start | bytes 786440 | tf_op jit(solution)/shard_map/ppermute | solution.py:505
  53.7 17.5 %collective-permute-start.12 = (bf16[256,512]{1,0:T(8,128)(2,1)S(1)}, bf16[256,512]{1,0:T(8,128)(2,1)S(1)}, u32[]{:S(2)}, u32[]{:S(2)}) collective-permute-start(bf16[256,512]{1,0:T(8,128)(2,1)S(1)} %shard_map.86), channel_id=1, source_target_pairs={{0,4},{4,0},{1,5},{5,1},{2,6},{6,2},{3,7},{7,3},{8,12},{12,8},{9,1... | collective-permute-start | bytes 786440 | tf_op jit(solution)/shard_map/ppermute | solution.py:505
  54.7 20.2 %collective-permute-start.13 = (bf16[256,512]{1,0:T(8,128)(2,1)S(1)}, bf16[256,512]{1,0:T(8,128)(2,1)S(1)}, u32[]{:S(2)}, u32[]{:S(2)}) collective-permute-start(bf16[256,512]{1,0:T(8,128)(2,1)S(1)} %shard_map.87), channel_id=1, source_target_pairs={{0,4},{4,0},{1,5},{5,1},{2,6},{6,2},{3,7},{7,3},{8,12},{12,8},{9,1... | collective-permute-start | bytes 786440 | tf_op jit(solution)/shard_map/ppermute | solution.py:505
  69.1 29.9 %collective-permute-start.7 = (bf16[256,512]{1,0:T(8,128)(2,1)S(1)}, bf16[256,512]{1,0:T(8,128)(2,1)S(1)}, u32[]{:S(2)}, u32[]{:S(2)}) collective-permute-start(bf16[256,512]{1,0:T(8,128)(2,1)S(1)} %shard_map.81), channel_id=1, source_target_pairs={{0,4},{4,0},{1,5},{5,1},{2,6},{6,2},{3,7},{7,3},{8,12},{12,8},{9,1... | collective-permute-start | bytes 786440 | tf_op jit(solution)/shard_map/ppermute | solution.py:505
  70.2 28.0 %collective-permute-start.8 = (bf16[256,512]{1,0:T(8,128)(2,1)S(1)}, bf16[256,512]{1,0:T(8,128)(2,1)S(1)}, u32[]{:S(2)}, u32[]{:S(2)}) collective-permute-start(bf16[256,512]{1,0:T(8,128)(2,1)S(1)} %shard_map.82), channel_id=1, source_target_pairs={{0,4},{4,0},{1,5},{5,1},{2,6},{6,2},{3,7},{7,3},{8,12},{12,8},{9,1... | collective-permute-start | bytes 786440 | tf_op jit(solution)/shard_map/ppermute | solution.py:505
  71.2 26.2 %collective-permute-start.9 = (bf16[256,512]{1,0:T(8,128)(2,1)S(1)}, bf16[256,512]{1,0:T(8,128)(2,1)S(1)}, u32[]{:S(2)}, u32[]{:S(2)}) collective-permute-start(bf16[256,512]{1,0:T(8,128)(2,1)S(1)} %shard_map.83), channel_id=1, source_target_pairs={{0,4},{4,0},{1,5},{5,1},{2,6},{6,2},{3,7},{7,3},{8,12},{12,8},{9,1... | collective-permute-start | bytes 786440 | tf_op jit(solution)/shard_map/ppermute | solution.py:505
  74.9 21.7 %collective-permute-start.10 = (bf16[256,512]{1,0:T(8,128)(2,1)S(1)}, bf16[256,512]{1,0:T(8,128)(2,1)S(1)}, u32[]{:S(2)}, u32[]{:S(2)}) collective-permute-start(bf16[256,512]{1,0:T(8,128)(2,1)S(1)} %shard_map.84), channel_id=1, source_target_pairs={{0,4},{4,0},{1,5},{5,1},{2,6},{6,2},{3,7},{7,3},{8,12},{12,8},{9,1... | collective-permute-start | bytes 786440 | tf_op jit(solution)/shard_map/ppermute | solution.py:505

commit v4 on v3

--- a/solution.py
+++ b/solution.py
@@ -60,11 +60,47 @@
         table[r] = row(values, r)
 
 
-def gate_kernel(tokens, half, step, counter, place, key_ref, value_ref, edge_ref, taps_ref, mix_ref,
-                gated_ref, start_ref, mine_ref, other_ref, key_rows, value_rows, decays, taps):
-    block = pl.program_id(0)
+def mask_kernel(half, step, counter, place, mask_ref):
     lane = lax.broadcasted_iota(jnp.int32, (SUBS, LANES), 1)
     sub = lax.broadcasted_iota(jnp.int32, (SUBS, LANES), 0)
+
+    @pl.loop(0, mask_ref.shape[0])
+    def _(group):
+        channel = place[1] + group * LANES + lane
+        for part in range(2):
+            first = counter[1] + place[0] + part * half + sub * step
+            bits = counter[0] + first * jnp.int32(-1640531535) + channel * jnp.int32(-2048144777)
+
+            def several(j, bits):
+                for u in range(GATE_STEPS):
+                    h = bits + jnp.int32((-1640531535 * u + 2**31) % 2**32 - 2**31)
+                    h = h ^ lax.shift_right_logical(h, jnp.full_like(h, 16))
+                    h = h * jnp.int32(2146121005)
+                    h = h ^ lax.shift_right_logical(h, jnp.full_like(h, 15))
+                    h = h * jnp.int32(-2073254261)
+                    keep = (h & jnp.int32(-536870912)) != 0
+                    at = pl.multiple_of(part * half + (GATE_STEPS * j + u) * SUBS, SUBS)
+                    mask_ref[group, pl.ds(at, SUBS), :] = jnp.where(keep, 1.0, 0.0)
+                return bits + jnp.int32((-1640531535 * GATE_STEPS + 2**31) % 2**32 - 2**31)
+
+            lax.fori_loop(0, step // GATE_STEPS, several, bits)
+
+
+def totals_of(values, sub):
+    for bit in (1, 2, 4):
+        even = (sub & bit) == 0
+        values = [
+            jnp.where(even, a, b) + pltpu.roll(jnp.where(even, b, a), bit, 0)
+            for a, b in zip(values[::2], values[1::2])
+        ]
+    return values[0]
+
+
+def gate_kernel(tokens, half, step, place, mask_ref, key_ref, value_ref, edge_ref, taps_ref, mix_ref,
+                gated_ref, start_ref, middle_ref, mine_ref, other_ref, key_rows, value_rows, decays, taps):
+    block = pl.program_id(0)
+    sub = lax.broadcasted_iota(jnp.int32, (SUBS, LANES), 0)
+    later = ((SUBS - 1 - sub) * step).astype(jnp.float32)
     is_mine = (block * 2) // pl.num_programs(0) == place[2]
     for group in range(WIDTH // LANES):
         cols = slice(group * LANES, (group + 1) * LANES)
@@ -77,30 +113,21 @@
             taps[SHORT + lag] = row(taps_ref[2, :, cols], lag)
         rates = rates_of(mix_ref[:, cols], tokens)
         fill(decays, jnp.exp(-rates))
-        jumps = {d: jnp.exp(-rates * float(d * step)) for d in (1, 2, 4)}
-        whole = jnp.exp(-rates * float(half))
-        channel = place[1] + block * WIDTH + group * LANES + lane
-        carried = None
+        weights = [jnp.exp(-row(rates, r) * later) for r in range(ORDER)]
+        ends = []
         for part in range(2):
             base = BASE + part * SUBS * (step + GAP)
-            first = counter[1] + place[0] + part * half + sub * step
-            bits = counter[0] + first * jnp.int32(-1640531535) + channel * jnp.int32(-2048144777)
 
             def quad(j, carry):
-                states, k1, k2, v1, v2, bits = carry
+                states, k1, k2, v1, v2 = carry
                 values = []
                 for u in range(GATE_STEPS):
                     k0 = across(key_rows, base + GATE_STEPS * j + u, step)
                     v0 = across(value_rows, base + GATE_STEPS * j + u, step)
                     keyed = taps[0] * k0 + taps[1] * k1 + taps[2] * k2
                     valued = taps[3] * v0 + taps[4] * v1 + taps[5] * v2
-                    h = bits + jnp.int32(-1640531535) * u
-                    h = h ^ lax.shift_right_logical(h, jnp.full_like(h, 16))
-                    h = h * jnp.int32(2146121005)
-                    h = h ^ lax.shift_right_logical(h, jnp.full_like(h, 15))
-                    h = h * jnp.int32(-2073254261)
-                    keep = (h & jnp.int32(-536870912)) != 0
-                    values.append(jnp.where(keep, keyed * valued, 0.0))
+                    at = pl.multiple_of(part * half + (GATE_STEPS * j + u) * SUBS, SUBS)
+                    values.append(keyed * valued * mask_ref[place_of, pl.ds(at, SUBS), :])
                     k1, k2, v1, v2 = k0, k1, v0, v1
                 wides = []
                 for u in range(0, GATE_STEPS, 2):
@@ -115,7 +142,7 @@
                     for g in wides:
                         x = x * a + g
                     after.append(x)
-                return (tuple(after), k1, k2, v1, v2, bits + jnp.int32((-1640531535 * GATE_STEPS + 2**31) % 2**32 - 2**31))
+                return (tuple(after), k1, k2, v1, v2)
 
             zero = jnp.zeros((SUBS, LANES), jnp.float32)
             init = (
@@ -124,24 +151,14 @@
                 across(key_rows, base - GAP - 2, step),
                 across(value_rows, base - GAP - 1, step),
                 across(value_rows, base - GAP - 2, step),
-                bits,
             )
             states = lax.fori_loop(0, step // GATE_STEPS, quad, init)[0]
-            ends = []
             for r in range(ORDER):
-                x = states[r]
-                for d in (1, 2, 4):
-                    x = x + row(jumps[d], r) * jnp.where(sub >= d, pltpu.roll(x, d, 0), 0.0)
-                before = jnp.where(sub >= 1, pltpu.roll(x, 1, 0), 0.0)
-                last = jnp.broadcast_to(x[SUBS - 1 : SUBS, :], (SUBS, LANES))
-                if part == 1:
-                    rate = row(rates, r)
-                    before = before + jnp.exp(-rate * (sub * step).astype(jnp.float32)) * carried[r]
-                    last = last + row(whole, r) * carried[r]
-                start_ref[part, place_of, r] = before
-                ends.append(last)
-            carried = ends
-        end = jnp.concatenate([last[0:1, :] for last in carried], axis=0)
+                start_ref[part, place_of, r] = states[r]
+            weighted = [x * w for x, w in zip(states, weights)]
+            ends.append(jnp.concatenate([totals_of(weighted[:SUBS], sub), totals_of(weighted[SUBS:], sub)], axis=0))
+        middle_ref[:, lanes_of(place_of)] = ends[0]
+        end = ends[1] + jnp.exp(-rates * float(half)) * ends[0]
 
         @pl.when(is_mine)
         def _():
@@ -187,6 +204,20 @@
     return (tuple(after), q1, q2)
 
 
+def states_in(start_ref, which, group, rates, into, step):
+    sub = lax.broadcasted_iota(jnp.int32, (SUBS, LANES), 0)
+    offset = (sub * step).astype(jnp.float32)
+    jumps = {d: jnp.exp(-rates * float(d * step)) for d in (1, 2, 4)}
+    states = []
+    for r in range(ORDER):
+        x = start_ref[which, group, r]
+        for d in (1, 2, 4):
+            x = x + row(jumps[d], r) * jnp.where(sub >= d, pltpu.roll(x, d, 0), 0.0)
+        x = jnp.where(sub >= 1, pltpu.roll(x, 1, 0), 0.0)
+        states.append(x + jnp.exp(-row(rates, r) * offset) * row(into, r))
+    return tuple(states)
+
+
 def gather(mixed_ref, mixed_rows, lanes, step):
     for n in range(SUBS):
         at = n * (step + GAP)
@@ -194,15 +225,16 @@
 
 
 def local_kernel(tokens, half, step, first, last, which, gated_ref, planes_ref, edge_ref, taps_ref, mix_ref,
-                 residue_ref, skip_ref, start_ref, *rest):
+                 residue_ref, skip_ref, start_ref, middle_ref, *rest):
     local_ref, filtered_ref, query_rows, decays, gains, taps = rest[-6:]
 
     @pl.loop(first, last)
     def _(group):
         lanes = lanes_of(group)
-        query_setup(tokens, half, step, which[0], lanes, planes_ref, edge_ref, taps_ref, mix_ref, query_rows, decays, taps)
+        rates = query_setup(tokens, half, step, which[0], lanes, planes_ref, edge_ref, taps_ref, mix_ref, query_rows, decays, taps)
         fill(gains, residue_ref[:, lanes])
         skip = row(skip_ref[:, lanes], 0)
+        into = jnp.where(which[0] == 1, middle_ref[:, lanes], 0.0)
 
         def quad(j, carry):
             def emit(u, query, total):
@@ -212,16 +244,13 @@
 
             return scan_quad(step, j, carry, gated_ref.at[group], which[0] * half, query_rows, decays, gains, taps, skip, emit)
 
-        states = tuple(start_ref[which[0], group, r] for r in range(ORDER))
+        states = states_in(start_ref, which[0], group, rates, into, step)
         q1, q2 = across(query_rows, BASE - GAP - 1, step), across(query_rows, BASE - GAP - 2, step)
         lax.fori_loop(0, step // QUAD, quad, (states, q1, q2))
 
 
 def blend_kernel(tokens, half, step, groups, which, gated_ref, planes_ref, edge_ref, taps_ref, mix_ref, residue_ref,
-                 skip_ref, start_ref, own_ref, got_ref, mixed_ref, query_rows, decays, gains, taps, mixed_rows):
-    sub = lax.broadcasted_iota(jnp.int32, (SUBS, LANES), 0)
-    offset = (which[0] * half + sub * step).astype(jnp.float32)
-
+                 skip_ref, start_ref, middle_ref, own_ref, got_ref, mixed_ref, query_rows, decays, gains, taps, mixed_rows):
     @pl.loop(0, groups)
     def _(group):
         lanes = lanes_of(group)
@@ -229,6 +258,7 @@
         fill(gains, residue_ref[:, lanes])
         skip = row(skip_ref[:, lanes], 0)
         into = state_of(own_ref, got_ref, which[1], group, groups)
+        into = jnp.where(which[0] == 1, jnp.exp(-rates * float(half)) * into + middle_ref[:, lanes], into)
 
         def quad(j, carry):
             def emit(u, query, total):
@@ -236,9 +266,7 @@
 
             return scan_quad(step, j, carry, gated_ref.at[group], which[0] * half, query_rows, decays, gains, taps, skip, emit)
 
-        states = tuple(
-            start_ref[which[0], group, r] + jnp.exp(-row(rates, r) * offset) * row(into, r) for r in range(ORDER)
-        )
+        states = states_in(start_ref, which[0], group, rates, into, step)
         q1, q2 = across(query_rows, BASE - GAP - 1, step), across(query_rows, BASE - GAP - 2, step)
         lax.fori_loop(0, step // QUAD, quad, (states, q1, q2))
         gather(mixed_ref, mixed_rows, lanes, step)
@@ -300,47 +328,64 @@
     return pl.CostEstimate(flops=vectors, bytes_accessed=moved, transcendentals=0)
 
 
-def gate(counter, place, planes, edge, taps, mix, tokens):
+def mask_of(counter, place, rows, channels):
+    half = rows // 2
+    return pl.pallas_call(
+        lambda *refs: mask_kernel(half, half // SUBS, *refs),
+        out_shape=pltpu.VMEM((channels // LANES, rows, LANES), jnp.float32),
+        grid_spec=pltpu.PrefetchScalarGridSpec(
+            num_scalar_prefetch=2, grid=(1,), in_specs=[], out_specs=pl.BlockSpec(memory_space=pltpu.VMEM)
+        ),
+        name="mask",
+        compiler_params=room(16),
+        cost_estimate=cost(2 * 10**9, 2**20),
+    )(counter, place)
+
+
+def gate(place, mask, planes, edge, taps, mix, tokens):
     rows, channels = planes.shape[1:]
     half = rows // 2
     step = half // SUBS
     blocks = channels // WIDTH
-    spread_rows = BASE + 2 * SUBS * (step + GAP)
+    spread_rows = 2 * BASE + 2 * SUBS * (step + GAP)
     first = lambda b, owner: jnp.clip(b - owner * (blocks // 2), 0, blocks // 2 - 1)
     return pl.pallas_call(
         lambda *refs: gate_kernel(tokens, half, step, *refs),
         out_shape=(
             pltpu.VMEM((channels // LANES, rows, LANES), jnp.bfloat16),
             pltpu.VMEM((2, channels // LANES, ORDER, SUBS, LANES), jnp.float32),
+            pltpu.VMEM((ORDER, channels), jnp.float32),
             jax.ShapeDtypeStruct((ORDER, channels // 2), jnp.float32),
             jax.ShapeDtypeStruct((ORDER, channels // 2), jnp.float32),
         ),
         grid_spec=pltpu.PrefetchScalarGridSpec(
-            num_scalar_prefetch=2,
+            num_scalar_prefetch=1,
             grid=(blocks,),
             in_specs=[
-                pl.BlockSpec((None, rows, WIDTH), lambda b, c, s: (1, 0, b)),
-                pl.BlockSpec((None, rows, WIDTH), lambda b, c, s: (2, 0, b)),
                 pl.BlockSpec(memory_space=pltpu.VMEM),
-                pl.BlockSpec((3, SHORT, WIDTH), lambda b, c, s: (0, 0, b)),
-                pl.BlockSpec((ORDER, WIDTH), lambda b, c, s: (0, b)),
+                pl.BlockSpec((None, rows, WIDTH), lambda b, s: (1, 0, b)),
+                pl.BlockSpec((None, rows, WIDTH), lambda b, s: (2, 0, b)),
+                pl.BlockSpec(memory_space=pltpu.VMEM),
+                pl.BlockSpec((3, SHORT, WIDTH), lambda b, s: (0, 0, b)),
+                pl.BlockSpec((ORDER, WIDTH), lambda b, s: (0, b)),
             ],
             out_specs=(
                 pl.BlockSpec(memory_space=pltpu.VMEM),
                 pl.BlockSpec(memory_space=pltpu.VMEM),
-                pl.BlockSpec((ORDER, WIDTH), lambda b, c, s: (0, first(b, s[2]))),
-                pl.BlockSpec((ORDER, WIDTH), lambda b, c, s: (0, first(b, 1 - s[2]))),
+                pl.BlockSpec(memory_space=pltpu.VMEM),
+                pl.BlockSpec((ORDER, WIDTH), lambda b, s: (0, first(b, s[2]))),
+                pl.BlockSpec((ORDER, WIDTH), lambda b, s: (0, first(b, 1 - s[2]))),
             ),
             scratch_shapes=[pltpu.VMEM((spread_rows, LANES), jnp.float32)] * 2 + [table(), table(2 * SHORT)],
         ),
         name="gate",
         compiler_params=room(16),
-        cost_estimate=cost(15 * 10**9, 4 * rows * channels),
-    )(counter, place, planes, planes, edge, taps, mix)
+        cost_estimate=cost(11 * 10**9, 4 * rows * channels),
+    )(place, mask, planes, planes, edge, taps, mix)
 
 
 def scan_scratch(step):
-    return [pltpu.VMEM((BASE + SUBS * (step + GAP), LANES), jnp.float32), table(), table(), table(SHORT)]
+    return [pltpu.VMEM((2 * BASE + SUBS * (step + GAP), LANES), jnp.float32), table(), table(), table(SHORT)]
 
 
 def resident(kernel, which, operands, out_shape, scratch, aliases, time):
@@ -380,7 +425,7 @@
     return resident(
         lambda *refs: carry_kernel(tokens, half, step, groups // 2, mine, *refs), which,
         (*parts, mix, residue, state, *before), pltpu.VMEM((half, groups * LANES), jnp.bfloat16),
-        [table(), pltpu.VMEM((SUBS * (step + GAP), LANES), jnp.float32)], {6: 0} if before else {}, 2.5,
+        [table(), pltpu.VMEM((2 * BASE + SUBS * (step + GAP), LANES), jnp.float32)], {6: 0} if before else {}, 2.5,
     )
 
 
@@ -391,7 +436,7 @@
     return resident(
         lambda *refs: blend_kernel(tokens, half, step, groups, *refs), which, (*operands, own, got),
         jax.ShapeDtypeStruct((half, groups * LANES), jnp.bfloat16),
-        scan_scratch(step) + [pltpu.VMEM((SUBS * (step + GAP), LANES), jnp.float32)], {}, 9,
+        scan_scratch(step) + [pltpu.VMEM((2 * BASE + SUBS * (step + GAP), LANES), jnp.float32)], {}, 9,
     )
 
 
@@ -485,10 +530,11 @@
     place = scalars(index * rows, side * channels, index % 2)
     to_send = scalars(1 - side, index % 2)
     to_keep = scalars(side, index % 2)
-    gated, start, mine, other = gate(
-        far_memory(counter), place, far_memory(planes), edge, far_memory(short_filter), far_memory(decay_mix), tokens
+    mask = mask_of(far_memory(counter), place, rows, channels)
+    gated, start, middle, mine, other = gate(
+        place, mask, far_memory(planes), edge, far_memory(short_filter), far_memory(decay_mix), tokens
     )
-    operands = (gated, planes, edge, short_filter, decay_mix, mode_residue, skip_gain[None], start)
+    operands = (gated, planes, edge, short_filter, decay_mix, mode_residue, skip_gain[None], start, middle)
     parts = [()]
 
     def between(piece):

time: 101 us -> 103 us (1.020)
  local copies, waits for them, and re-layouts: 0.98 us -> 5.27 us
  starting transfers between devices: 24 us -> 20.8 us
  Pallas kernels: 62.4 us -> 63.6 us
    unnamed x20 -> x24, local copies, waits for them, and re-layouts: 0.06 us -> 4.35 us
    ppermute x5, starting transfers between devices: 13.3 us -> 10.4 us  [ring(): return lax.ppermute(value, 'ctx', pairs)]
    pallas_call x1, Pallas kernels: 13.5 us -> 10.7 us  [gate(): pl.pallas_call(lambda *refs: gate_kernel(tokens, half, step, *refs), out_...]
    pallas_call x0 -> x1, Pallas kernels: none -> 2.55 us  [mask_of(): pl.pallas_call(lambda *refs: mask_kernel(half, half // SUBS, *refs), out_...]
    pallas_call x6, Pallas kernels: 22.5 us -> 23.9 us  [resident(): pl.pallas_call(kernel, out_shape=out_shape, grid_spec=pltpu.PrefetchScala...]
  transfers between devices with their start and end apart: 15 -> 15, of which waited for: 6 -> 5; matrix products, arithmetic and copies ran while one was open for 0% -> 0% of each run, Pallas kernels for 44% -> 48%
where the time goes in v4:
time: 103 us; the launch traced here: 102 us
  Pallas kernels  63.6 us (62%)
  starting transfers between devices  20.8 us (20%)
  waiting for transfers between devices  11.9 us (12%)
  local copies, waits for them, and re-layouts  5.27 us (5%)
    pallas_call x6, Pallas kernels, resident(): pl.pallas_call(kernel, out_shape=out_shape, grid_spec=pltpu.PrefetchScala...  23.9 us
    pallas_call x10, Pallas kernels, project(): pl.pallas_call(project_kernel, out_shape=jax.ShapeDtypeStruct((rows, cols...  19.5 us
    pallas_call x1, Pallas kernels, gate(): pl.pallas_call(lambda *refs: gate_kernel(tokens, half, step, *refs), out_...  10.7 us
    ppermute x5, starting transfers between devices, ring(): return lax.ppermute(value, 'ctx', pairs)  10.4 us
    ppermute x9, waiting for transfers between devices, body(): received.append(lax.ppermute(part, 'ch', [(0, 1), (1, 0)]))  10.3 us
    ppermute x9, starting transfers between devices, body(): received.append(lax.ppermute(part, 'ch', [(0, 1), (1, 0)]))  9.15 us
    pallas_call x9, Pallas kernels, combine(): pl.pallas_call(combine_kernel, out_shape=jax.ShapeDtypeStruct(own.shape,...  6.93 us
    unnamed x24, local copies, waits for them, and re-layouts  4.35 us
  transfers between devices with their start and end apart: 15, of which 5 were waited for; matrix products, arithmetic and copies ran while one was open for 0% of the time, Pallas kernels for 48%

profile of v4, /device:TPU:0, one launch (start us, length us, event | category | flops | bytes accessed | tf_op | source)
XLA Modules:
  0.0 102.2 jit_solution(1612701111193897219)
XLA Ops:
  0.0 0.9 slice.4
  0.9 1.3 %collective-permute-start = (bf16[3,2,2048]{2,1,0:T(2,128)(2,1)S(1)}, bf16[3,2,2048]{2,1,0:T(2,128)(2,1)S(1)}, u32[]{:S(2)}, u32[]{:S(2)}) collective-permute-start(bf16[3,2,2048]{2,1,0:T(2,128)(2,1)S(1)} %slice.4), channel_id=1, source_target_pairs={{0,8},{8,16},{16,24},{24,32},{32,40},{40,48},{48,56},{56,64},{64,7... | collective-permute-start | bytes 73736 | tf_op jit(solution)/shard_map/ppermute | solution.py:521
  2.3 2.6 %mask.1.refs_1_ = f32[16,512,128]{2,1,0:T(8,128)S(1)} custom-call(s32[2]{0:T(128)} %refs_0_.1, s32[4]{0:T(128)S(1)} %compare_select_fusion.refs_1_.refs_0_), custom_call_target="tpu_custom_call" | custom-call | flops 2000000000 | bytes 1048576 | tf_op jit(solution)/shard_map/mask/pallas_call | solution.py:333
  4.8 2.0 %copy-done.4 = f32[16,512,128]{2,1,0:T(8,128)} copy-done((f32[16,512,128]{2,1,0:T(8,128)}, f32[16,512,128]{2,1,0:T(8,128)S(1)}, u32[]{:S(2)}) %copy-start.4) | copy-done | bytes 4194328
  6.9 2.3 %copy-done.5 = f32[16,512,128]{2,1,0:T(8,128)S(1)} copy-done((f32[16,512,128]{2,1,0:T(8,128)S(1)}, f32[16,512,128]{2,1,0:T(8,128)}, u32[]{:S(2)}) %copy-start.5) | copy-done | bytes 4194328
  9.2 10.7 %gate.1 = (bf16[16,512,128]{2,1,0:T(8,128)(2,1)S(1)}, f32[2,16,16,8,128]{4,3,2,1,0:T(8,128)S(1)}, f32[16,2048]{1,0:T(8,128)S(1)}, f32[16,1024]{1,0:T(8,128)S(1)}, f32[16,1024]{1,0:T(8,128)S(1)}) custom-call(s32[4]{0:T(128)S(1)} %compare_select_fusion.refs_1_.refs_0_, f32[16,512,128]{2,1,0:T(8,128)S(1)} %copy-done.5, bf16[3,512,2048]{2,1,0:T(8,128)(2,1)} %bitcast.5, ...), custom_call_target="tpu_custom_call" | custom-call | flops 11000000512 | bytes 4194304 | tf_op jit(solution)/shard_map/gate/pallas_call | solution.py:352
  19.9 4.8 %collective-permute-start.1 = (f32[16,1024]{1,0:T(8,128)S(1)}, f32[16,1024]{1,0:T(8,128)S(1)}, u32[]{:S(2)}, u32[]{:S(2)}) collective-permute-start(f32[16,1024]{1,0:T(8,128)S(1)} %get-tuple-element.21), channel_id=1, source_target_pairs={{0,8},{8,0},{16,24},{24,16},{32,40},{40,32},{48,56},{56,48},{64,72... | collective-permute-start | bytes 196616 | tf_op jit(solution)/shard_map/ppermute | solution.py:487
  24.7 0.9 collective-permute-done.1
  26.5 4.6 %shard_map.73 = (f32[16,256,128]{2,1,0:T(8,128)S(1)}, f32[16,256,128]{2,1,0:T(8,128)S(1)}) custom-call(s32[4]{0:T(128)S(1)} %select_select_fusion.refs_0_, bf16[16,512,128]{2,1,0:T(8,128)(2,1)S(1)} %get-tuple-element.17.refs_1_, bf16[3,512,2048]{2,1,0:T(8,128)(2,1)S(1)} %bitcast.9, bf16[3,2,2048]{2,1,0:T(2,128)(2,1)S(1)} %collective-permute-done.refs_4_.refs_3_, ...), custom_call_target="tpu_custom_call" | custom-call | flops 4400000000 | bytes 1048576 | tf_op jit(solution)/shard_map/pallas_call | solution.py:394
  31.7 1.7 %collective-permute-start.3 = (f32[16,1024]{1,0:T(8,128)S(1)}, f32[16,1024]{1,0:T(8,128)S(1)}, u32[]{:S(2)}, u32[]{:S(2)}) collective-permute-start(f32[16,1024]{1,0:T(8,128)S(1)} %add_select_fusion.2), channel_id=1, source_target_pairs={{0,32},{8,40},{16,48},{24,56},{32,0},{40,8},{48,16},{56,24},{64,96... | collective-permute-start | bytes 196616 | tf_op jit(solution)/shard_map/ppermute | solution.py:487
  33.3 2.5 %shard_map.74 = (f32[16,256,128]{2,1,0:T(8,128)S(1)}, f32[16,256,128]{2,1,0:T(8,128)S(1)}) custom-call(s32[4]{0:T(128)S(1)} %select_select_fusion.refs_0_, bf16[16,512,128]{2,1,0:T(8,128)(2,1)S(1)} %get-tuple-element.17.refs_1_, bf16[3,512,2048]{2,1,0:T(8,128)(2,1)S(1)} %bitcast.10, ...), custom_call_target="tpu_custom_call", output_to_operand_aliasing={{0}: (10, {}), {1}: (11, {})} | custom-call | flops 2200000000 | bytes 1048576 | tf_op jit(solution)/shard_map/pallas_call | solution.py:394
  36.1 3.1 %collective-permute-start.4 = (f32[16,1024]{1,0:T(8,128)S(1)}, f32[16,1024]{1,0:T(8,128)S(1)}, u32[]{:S(2)}, u32[]{:S(2)}) collective-permute-start(f32[16,1024]{1,0:T(8,128)S(1)} %add_select_fusion.1), channel_id=1, source_target_pairs={{0,96},{8,104},{16,112},{24,120},{32,64},{40,72},{48,80},{56,88},{... | collective-permute-start | bytes 196616 | tf_op jit(solution)/shard_map/ppermute | solution.py:487
  39.2 2.5 %shard_map.75 = (f32[16,256,128]{2,1,0:T(8,128)S(1)}, f32[16,256,128]{2,1,0:T(8,128)S(1)}) custom-call(s32[4]{0:T(128)S(1)} %select_select_fusion.refs_0_, bf16[16,512,128]{2,1,0:T(8,128)(2,1)S(1)} %get-tuple-element.17.refs_1_, bf16[3,512,2048]{2,1,0:T(8,128)(2,1)S(1)} %bitcast.11, ...), custom_call_target="tpu_custom_call", output_to_operand_aliasing={{0}: (10, {}), {1}: (11, {})} | custom-call | flops 2200000000 | bytes 1048576 | tf_op jit(solution)/shard_map/pallas_call | solution.py:394
  41.9 2.6 %shard_map.76.refs_6_ = bf16[256,2048]{1,0:T(8,128)(2,1)S(1)} custom-call(s32[4]{0:T(128)S(1)} %select_select_fusion.refs_0_, f32[16,256,128]{2,1,0:T(8,128)S(1)} %get-tuple-element.26.refs_1_, f32[16,256,128]{2,1,0:T(8,128)S(1)} %get-tuple-element.27.refs_2_, f32[16,2048]{1,0:T(8,128)S(1)} %copy-done, f32[16,2048]{1,0:T(8,128)S(1)} %copy-done.1, ...), custom_call_target="tpu_custom_call" | custom-call | flops 2500000000 | bytes 1048576 | tf_op jit(solution)/shard_map/pallas_call | solution.py:394
  44.6 2.6 %shard_map.77.mixed_ref = bf16[256,2048]{1,0:T(8,128)(2,1)S(1)} custom-call(s32[4]{0:T(128)S(1)} %select_select_fusion.refs_0_, f32[16,256,128]{2,1,0:T(8,128)S(1)} %get-tuple-element.26.refs_1_, f32[16,256,128]{2,1,0:T(8,128)S(1)} %get-tuple-element.27.refs_2_, f32[16,2048]{1,0:T(8,128)S(1)} %copy-done, ...), custom_call_target="tpu_custom_call", output_to_operand_aliasing={{}: (6, {})} | custom-call | flops 2500000000 | bytes 1048576 | tf_op jit(solution)/shard_map/pallas_call | solution.py:394
  48.2 1.3 %collective-permute-start.6 = (bf16[256,256]{1,0:T(8,128)(2,1)S(1)}, bf16[256,256]{1,0:T(8,128)(2,1)S(1)}, u32[]{:S(2)}, u32[]{:S(2)}) collective-permute-start(bf16[256,256]{1,0:T(8,128)(2,1)S(1)} %shard_map.78), channel_id=1, source_target_pairs={{0,4},{4,0},{1,5},{5,1},{2,6},{6,2},{3,7},{7,3},{8,12},{12,8},{9,1... | collective-permute-start | bytes 393224 | tf_op jit(solution)/shard_map/ppermute | solution.py:551
  49.5 1.3 %shard_map.87 = bf16[256,512]{1,0:T(8,128)(2,1)S(1)} custom-call(bf16[256,2048]{1,0:T(8,128)(2,1)S(1)} %shard_map.77.mixed_ref, bf16[2048,4096]{1,0:T(8,128)(2,1)S(1)} %bitcast.3), custom_call_target="tpu_custom_call" | custom-call | flops 536870912 | bytes 3145728 | tf_op jit(solution)/shard_map/pallas_call | solution.py:446
  50.8 1.3 %shard_map.86 = bf16[256,512]{1,0:T(8,128)(2,1)S(1)} custom-call(bf16[256,2048]{1,0:T(8,128)(2,1)S(1)} %shard_map.77.mixed_ref, bf16[2048,4096]{1,0:T(8,128)(2,1)S(1)} %bitcast.3), custom_call_target="tpu_custom_call" | custom-call | flops 536870912 | bytes 3145728 | tf_op jit(solution)/shard_map/pallas_call | solution.py:446
  52.0 1.3 %shard_map.85 = bf16[256,512]{1,0:T(8,128)(2,1)S(1)} custom-call(bf16[256,2048]{1,0:T(8,128)(2,1)S(1)} %shard_map.77.mixed_ref, bf16[2048,4096]{1,0:T(8,128)(2,1)S(1)} %bitcast.3), custom_call_target="tpu_custom_call" | custom-call | flops 536870912 | bytes 3145728 | tf_op jit(solution)/shard_map/pallas_call | solution.py:446
  53.3 0.9 collective-permute-start.14
  54.2 1.2 %collective-permute-start.11 = (bf16[256,512]{1,0:T(8,128)(2,1)S(1)}, bf16[256,512]{1,0:T(8,128)(2,1)S(1)}, u32[]{:S(2)}, u32[]{:S(2)}) collective-permute-start(bf16[256,512]{1,0:T(8,128)(2,1)S(1)} %shard_map.85), channel_id=1, source_target_pairs={{0,4},{4,0},{1,5},{5,1},{2,6},{6,2},{3,7},{7,3},{8,12},{12,8},{9,1... | collective-permute-start | bytes 786440 | tf_op jit(solution)/shard_map/ppermute | solution.py:551
  56.2 1.2 %collective-permute-start.13 = (bf16[256,512]{1,0:T(8,128)(2,1)S(1)}, bf16[256,512]{1,0:T(8,128)(2,1)S(1)}, u32[]{:S(2)}, u32[]{:S(2)}) collective-permute-start(bf16[256,512]{1,0:T(8,128)(2,1)S(1)} %shard_map.87), channel_id=1, source_target_pairs={{0,4},{4,0},{1,5},{5,1},{2,6},{6,2},{3,7},{7,3},{8,12},{12,8},{9,1... | collective-permute-start | bytes 786440 | tf_op jit(solution)/shard_map/ppermute | solution.py:551
  57.4 9.0 %shard_map.79.mixed_ref = bf16[256,2048]{1,0:T(8,128)(2,1)S(1)} custom-call(s32[4]{0:T(128)S(1)} %select_select_fusion.1.refs_0_, bf16[16,512,128]{2,1,0:T(8,128)(2,1)S(1)} %get-tuple-element.17.refs_1_, bf16[3,512,2048]{2,1,0:T(8,128)(2,1)S(1)} %bitcast.12, bf16[3,2,2048]{2,1,0:T(2,128)(2,1)S(1)} %collective-permute-done.refs_4_.refs_3_, ...), custom_call_target="tpu_custom_call" | custom-call | flops 8999999488 | bytes 1048576 | tf_op jit(solution)/shard_map/pallas_call | solution.py:394
  66.4 1.3 %shard_map.84 = bf16[256,512]{1,0:T(8,128)(2,1)S(1)} custom-call(bf16[256,2048]{1,0:T(8,128)(2,1)S(1)} %shard_map.77.mixed_ref, bf16[2048,4096]{1,0:T(8,128)(2,1)S(1)} %bitcast.3), custom_call_target="tpu_custom_call" | custom-call | flops 536870912 | bytes 3145728 | tf_op jit(solution)/shard_map/pallas_call | solution.py:446
  67.7 1.3 %shard_map.83 = bf16[256,512]{1,0:T(8,128)(2,1)S(1)} custom-call(bf16[256,2048]{1,0:T(8,128)(2,1)S(1)} %shard_map.77.mixed_ref, bf16[2048,4096]{1,0:T(8,128)(2,1)S(1)} %bitcast.3), custom_call_target="tpu_custom_call" | custom-call | flops 536870912 | bytes 3145728 | tf_op jit(solution)/shard_map/pallas_call | solution.py:446
  69.0 1.3 %shard_map.82 = bf16[256,512]{1,0:T(8,128)(2,1)S(1)} custom-call(bf16[256,2048]{1,0:T(8,128)(2,1)S(1)} %shard_map.77.mixed_ref, bf16[2048,4096]{1,0:T(8,128)(2,1)S(1)} %bitcast.3), custom_call_target="tpu_custom_call" | custom-call | flops 536870912 | bytes 3145728 | tf_op jit(solution)/shard_map/pallas_call | solution.py:446
  70.2 1.3 %shard_map.81 = bf16[256,512]{1,0:T(8,128)(2,1)S(1)} custom-call(bf16[256,2048]{1,0:T(8,128)(2,1)S(1)} %shard_map.77.mixed_ref, bf16[2048,4096]{1,0:T(8,128)(2,1)S(1)} %bitcast.3), custom_call_target="tpu_custom_call" | custom-call | flops 536870912 | bytes 3145728 | tf_op jit(solution)/shard_map/pallas_call | solution.py:446
  71.5 0.9 collective-permute-start.7
  72.4 1.2 %collective-permute-start.8 = (bf16[256,512]{1,0:T(8,128)(2,1)S(1)}, bf16[256,512]{1,0:T(8,128)(2,1)S(1)}, u32[]{:S(2)}, u32[]{:S(2)}) collective-permute-start(bf16[256,512]{1,0:T(8,128)(2,1)S(1)} %shard_map.82), channel_id=1, source_target_pairs={{0,4},{4,0},{1,5},{5,1},{2,6},{6,2},{3,7},{7,3},{8,12},{12,8},{9,1... | collective-permute-start | bytes 786440 | tf_op jit(solution)/shard_map/ppermute | solution.py:551
  74.4 2.2 %collective-permute-done.13.got_ref = bf16[256,512]{1,0:T(8,128)(2,1)S(1)} collective-permute-done((bf16[256,512]{1,0:T(8,128)(2,1)S(1)}, bf16[256,512]{1,0:T(8,128)(2,1)S(1)}, u32[]{:S(2)}, u32[]{:S(2)}) %collective-permute-start.13) | collective-permute-done | bytes 262176 | tf_op jit(solution)/shard_map/ppermute | solution.py:551
  77.4 9.8 %shard_map.80.own_ref = f32[256,4096]{1,0:T(8,128)S(1)} custom-call(bf16[256,2048]{1,0:T(8,128)(2,1)S(1)} %shard_map.79.mixed_ref, bf16[2048,4096]{1,0:T(8,128)(2,1)S(1)} %bitcast.3), custom_call_target="tpu_custom_call" | custom-call | flops 4294967296 | bytes 17825792 | tf_op jit(solution)/shard_map/pallas_call | solution.py:446
  90.2 8.1 %collective-permute-done.10.got_ref = bf16[256,512]{1,0:T(8,128)(2,1)S(1)} collective-permute-done((bf16[256,512]{1,0:T(8,128)(2,1)S(1)}, bf16[256,512]{1,0:T(8,128)(2,1)S(1)}, u32[]{:S(2)}, u32[]{:S(2)}) %collective-permute-start.10) | collective-permute-done | bytes 262176 | tf_op jit(solution)/shard_map/ppermute | solution.py:551
  (59 shorter events, 12.1 us)
Async XLA Ops:
  0.9 5.9 %collective-permute-start = (bf16[3,2,2048]{2,1,0:T(2,128)(2,1)S(1)}, bf16[3,2,2048]{2,1,0:T(2,128)(2,1)S(1)}, u32[]{:S(2)}, u32[]{:S(2)}) collective-permute-start(bf16[3,2,2048]{2,1,0:T(2,128)(2,1)S(1)} %slice.4), channel_id=1, source_target_pairs={{0,8},{8,16},{16,24},{24,32},{32,40},{40,48},{48,56},{56,64},{64,7... | collective-permute-start | bytes 73736 | tf_op jit(solution)/shard_map/ppermute | solution.py:521
  4.8 2.0 %copy-start.4 = (f32[16,512,128]{2,1,0:T(8,128)}, f32[16,512,128]{2,1,0:T(8,128)S(1)}, u32[]{:S(2)}) copy-start(f32[16,512,128]{2,1,0:T(8,128)S(1)} %mask.1.refs_1_) | copy-start | bytes 12582916
  6.8 19.6 %slice-start.4 = ((s8[6291456]{0:T(1024)(128)(4,1)}), s8[2097152]{0:T(1024)(128)(4,1)S(1)}, s32[]{:S(2)}) async-start(s8[6291456]{0:T(1024)(128)(4,1)} %bitcast.7), calls=%async_computation.4 | async-start | bytes 4194304
  6.8 18.9 %copy-start = (f32[16,2048]{1,0:T(8,128)S(1)}, f32[16,2048]{1,0:T(8,128)}, u32[]{:S(2)}) copy-start(f32[16,2048]{1,0:T(8,128)} %refs_5_.9) | copy-start | bytes 393220
  6.8 19.6 %slice-start.5 = ((s8[6291456]{0:T(1024)(128)(4,1)}), s8[4194304]{0:T(1024)(128)(4,1)S(1)}, s32[]{:S(2)}) async-start(s8[6291456]{0:T(1024)(128)(4,1)} %bitcast.7), calls=%async_computation.5 | async-start | bytes 8388608
  6.8 19.6 %copy-start.1 = (f32[16,2048]{1,0:T(8,128)S(1)}, f32[16,2048]{1,0:T(8,128)}, u32[]{:S(2)}) copy-start(f32[16,2048]{1,0:T(8,128)} %refs_6_.9) | copy-start | bytes 393220
  6.8 19.6 %copy-start.2 = (f32[3,3,2048]{2,1,0:T(4,128)S(1)}, f32[3,3,2048]{2,1,0:T(4,128)}, u32[]{:S(2)}) copy-start(f32[3,3,2048]{2,1,0:T(4,128)} %refs_4_.11) | copy-start | bytes 221188
  6.8 19.6 %copy-start.3 = (f32[2048]{0:T(1024)S(1)}, f32[2048]{0:T(1024)}, u32[]{:S(2)}) copy-start(f32[2048]{0:T(1024)} %param.11) | copy-start | bytes 24580
  6.9 2.3 %copy-start.5 = (f32[16,512,128]{2,1,0:T(8,128)S(1)}, f32[16,512,128]{2,1,0:T(8,128)}, u32[]{:S(2)}) copy-start(f32[16,512,128]{2,1,0:T(8,128)} %copy-done.4) | copy-start | bytes 12582916
  19.9 5.7 %collective-permute-start.1 = (f32[16,1024]{1,0:T(8,128)S(1)}, f32[16,1024]{1,0:T(8,128)S(1)}, u32[]{:S(2)}, u32[]{:S(2)}) collective-permute-start(f32[16,1024]{1,0:T(8,128)S(1)} %get-tuple-element.21), channel_id=1, source_target_pairs={{0,8},{8,0},{16,24},{24,16},{32,40},{40,32},{48,56},{56,48},{64,72... | collective-permute-start | bytes 196616 | tf_op jit(solution)/shard_map/ppermute | solution.py:487
  25.7 5.9 %collective-permute-start.2 = (f32[16,1024]{1,0:T(8,128)S(1)}, f32[16,1024]{1,0:T(8,128)S(1)}, u32[]{:S(2)}, u32[]{:S(2)}) collective-permute-start(f32[16,1024]{1,0:T(8,128)S(1)} %select_add_fusion), channel_id=1, source_target_pairs={{0,16},{8,24},{16,0},{24,8},{32,48},{40,56},{48,32},{56,40},{64,80... | collective-permute-start | bytes 196616 | tf_op jit(solution)/shard_map/ppermute | solution.py:487
  31.7 4.3 %collective-permute-start.3 = (f32[16,1024]{1,0:T(8,128)S(1)}, f32[16,1024]{1,0:T(8,128)S(1)}, u32[]{:S(2)}, u32[]{:S(2)}) collective-permute-start(f32[16,1024]{1,0:T(8,128)S(1)} %add_select_fusion.2), channel_id=1, source_target_pairs={{0,32},{8,40},{16,48},{24,56},{32,0},{40,8},{48,16},{56,24},{64,96... | collective-permute-start | bytes 196616 | tf_op jit(solution)/shard_map/ppermute | solution.py:487
  36.1 5.7 %collective-permute-start.4 = (f32[16,1024]{1,0:T(8,128)S(1)}, f32[16,1024]{1,0:T(8,128)S(1)}, u32[]{:S(2)}, u32[]{:S(2)}) collective-permute-start(f32[16,1024]{1,0:T(8,128)S(1)} %add_select_fusion.1), channel_id=1, source_target_pairs={{0,96},{8,104},{16,112},{24,120},{32,64},{40,72},{48,80},{56,88},{... | collective-permute-start | bytes 196616 | tf_op jit(solution)/shard_map/ppermute | solution.py:487
  39.2 8.1 %slice-start = ((s8[16777216]{0:T(1024)(128)(4,1)}), s8[4194304]{0:T(1024)(128)(4,1)S(1)}, s32[]{:S(2)}) async-start(s8[16777216]{0:T(1024)(128)(4,1)} %bitcast.2), calls=%async_computation | async-start | bytes 8388608
  39.2 8.1 %slice-start.1 = ((s8[16777216]{0:T(1024)(128)(4,1)}), s8[4194304]{0:T(1024)(128)(4,1)S(1)}, s32[]{:S(2)}) async-start(s8[16777216]{0:T(1024)(128)(4,1)} %bitcast.2), calls=%async_computation.1 | async-start | bytes 8388608
  41.8 2.8 %collective-permute-start.5 = (f32[16,1024]{1,0:T(8,128)S(1)}, f32[16,1024]{1,0:T(8,128)S(1)}, u32[]{:S(2)}, u32[]{:S(2)}) collective-permute-start(f32[16,1024]{1,0:T(8,128)S(1)} %get-tuple-element.29), channel_id=1, source_target_pairs={{0,8},{8,0},{16,24},{24,16},{32,40},{40,32},{48,56},{56,48},{64,72... | collective-permute-start | bytes 196616 | tf_op jit(solution)/shard_map/ppermute | solution.py:487
  41.9 5.3 %slice-start.2 = ((s8[16777216]{0:T(1024)(128)(4,1)}), s8[4194304]{0:T(1024)(128)(4,1)S(1)}, s32[]{:S(2)}) async-start(s8[16777216]{0:T(1024)(128)(4,1)} %bitcast.2), calls=%async_computation.2 | async-start | bytes 8388608
  44.6 2.7 %slice-start.3 = ((s8[16777216]{0:T(1024)(128)(4,1)}), s8[4194304]{0:T(1024)(128)(4,1)S(1)}, s32[]{:S(2)}) async-start(s8[16777216]{0:T(1024)(128)(4,1)} %bitcast.2), calls=%async_computation.3 | async-start | bytes 8388608
  48.2 53.3 %collective-permute-start.6 = (bf16[256,256]{1,0:T(8,128)(2,1)S(1)}, bf16[256,256]{1,0:T(8,128)(2,1)S(1)}, u32[]{:S(2)}, u32[]{:S(2)}) collective-permute-start(bf16[256,256]{1,0:T(8,128)(2,1)S(1)} %shard_map.78), channel_id=1, source_target_pairs={{0,4},{4,0},{1,5},{5,1},{2,6},{6,2},{3,7},{7,3},{8,12},{12,8},{9,1... | collective-permute-start | bytes 393224 | tf_op jit(solution)/shard_map/ppermute | solution.py:551
  53.3 18.2 %collective-permute-start.14 = (bf16[256,256]{1,0:T(8,128)(2,1)S(1)}, bf16[256,256]{1,0:T(8,128)(2,1)S(1)}, u32[]{:S(2)}, u32[]{:S(2)}) collective-permute-start(bf16[256,256]{1,0:T(8,128)(2,1)S(1)} %shard_map.88), channel_id=1, source_target_pairs={{0,4},{4,0},{1,5},{5,1},{2,6},{6,2},{3,7},{7,3},{8,12},{12,8},{9,1... | collective-permute-start | bytes 393224 | tf_op jit(solution)/shard_map/ppermute | solution.py:551
  54.2 18.2 %collective-permute-start.11 = (bf16[256,512]{1,0:T(8,128)(2,1)S(1)}, bf16[256,512]{1,0:T(8,128)(2,1)S(1)}, u32[]{:S(2)}, u32[]{:S(2)}) collective-permute-start(bf16[256,512]{1,0:T(8,128)(2,1)S(1)} %shard_map.85), channel_id=1, source_target_pairs={{0,4},{4,0},{1,5},{5,1},{2,6},{6,2},{3,7},{7,3},{8,12},{12,8},{9,1... | collective-permute-start | bytes 786440 | tf_op jit(solution)/shard_map/ppermute | solution.py:551
  55.4 18.2 %collective-permute-start.12 = (bf16[256,512]{1,0:T(8,128)(2,1)S(1)}, bf16[256,512]{1,0:T(8,128)(2,1)S(1)}, u32[]{:S(2)}, u32[]{:S(2)}) collective-permute-start(bf16[256,512]{1,0:T(8,128)(2,1)S(1)} %shard_map.86), channel_id=1, source_target_pairs={{0,4},{4,0},{1,5},{5,1},{2,6},{6,2},{3,7},{7,3},{8,12},{12,8},{9,1... | collective-permute-start | bytes 786440 | tf_op jit(solution)/shard_map/ppermute | solution.py:551
  56.2 20.4 %collective-permute-start.13 = (bf16[256,512]{1,0:T(8,128)(2,1)S(1)}, bf16[256,512]{1,0:T(8,128)(2,1)S(1)}, u32[]{:S(2)}, u32[]{:S(2)}) collective-permute-start(bf16[256,512]{1,0:T(8,128)(2,1)S(1)} %shard_map.87), channel_id=1, source_target_pairs={{0,4},{4,0},{1,5},{5,1},{2,6},{6,2},{3,7},{7,3},{8,12},{12,8},{9,1... | collective-permute-start | bytes 786440 | tf_op jit(solution)/shard_map/ppermute | solution.py:551
  71.5 29.2 %collective-permute-start.7 = (bf16[256,512]{1,0:T(8,128)(2,1)S(1)}, bf16[256,512]{1,0:T(8,128)(2,1)S(1)}, u32[]{:S(2)}, u32[]{:S(2)}) collective-permute-start(bf16[256,512]{1,0:T(8,128)(2,1)S(1)} %shard_map.81), channel_id=1, source_target_pairs={{0,4},{4,0},{1,5},{5,1},{2,6},{6,2},{3,7},{7,3},{8,12},{12,8},{9,1... | collective-permute-start | bytes 786440 | tf_op jit(solution)/shard_map/ppermute | solution.py:551
  72.4 27.5 %collective-permute-start.8 = (bf16[256,512]{1,0:T(8,128)(2,1)S(1)}, bf16[256,512]{1,0:T(8,128)(2,1)S(1)}, u32[]{:S(2)}, u32[]{:S(2)}) collective-permute-start(bf16[256,512]{1,0:T(8,128)(2,1)S(1)} %shard_map.82), channel_id=1, source_target_pairs={{0,4},{4,0},{1,5},{5,1},{2,6},{6,2},{3,7},{7,3},{8,12},{12,8},{9,1... | collective-permute-start | bytes 786440 | tf_op jit(solution)/shard_map/ppermute | solution.py:551
  73.6 25.5 %collective-permute-start.9 = (bf16[256,512]{1,0:T(8,128)(2,1)S(1)}, bf16[256,512]{1,0:T(8,128)(2,1)S(1)}, u32[]{:S(2)}, u32[]{:S(2)}) collective-permute-start(bf16[256,512]{1,0:T(8,128)(2,1)S(1)} %shard_map.83), channel_id=1, source_target_pairs={{0,4},{4,0},{1,5},{5,1},{2,6},{6,2},{3,7},{7,3},{8,12},{12,8},{9,1... | collective-permute-start | bytes 786440 | tf_op jit(solution)/shard_map/ppermute | solution.py:551
  76.6 21.7 %collective-permute-start.10 = (bf16[256,512]{1,0:T(8,128)(2,1)S(1)}, bf16[256,512]{1,0:T(8,128)(2,1)S(1)}, u32[]{:S(2)}, u32[]{:S(2)}) collective-permute-start(bf16[256,512]{1,0:T(8,128)(2,1)S(1)} %shard_map.84), channel_id=1, source_target_pairs={{0,4},{4,0},{1,5},{5,1},{2,6},{6,2},{3,7},{7,3},{8,12},{12,8},{9,1... | collective-permute-start | bytes 786440 | tf_op jit(solution)/shard_map/ppermute | solution.py:551
